TPU v7x, 128 devices: a whole 4x4x4 slice. The times are simulated.
128 devices in a mesh: tracer: 8 (over x, z_hi), tile: 16 (over y, z_lo, core).
Axes of the slice: x: 4, y: 4, z: 4 (z_hi: 2, z_lo: 2; z = z_hi * 2 + z_lo), core: 2. Of those that a mesh axis runs over, the one named last changes fastest.
Arguments:
- tracers: float32 [192, 8, 256, 128], P('tracer', None, 'tile'), may hold values from 0.1 to 2
- air_mass: float32 [8, 8, 256, 128], P('tracer', None, 'tile'), may hold values from 1 to 2
- flux_x: float32 [8, 8, 256, 128], P('tracer', None, 'tile'), may hold values from -0.2 to 0.2
- flux_y: float32 [8, 8, 256, 128], P('tracer', None, 'tile'), may hold values from -0.2 to 0.2
- flux_z: float32 [8, 8, 256, 128], P('tracer', None, 'tile'), may hold values from -0.05 to 0.05
- reactants: int32 [512, 2], replicated, may hold values from 0 to 191
- products: int32 [512, 192], replicated, may hold values 0 or 1
- rate_coeff: float32 [512], replicated, may hold values from 0.01 to 0.1
- record_of_step: int32 [2], replicated, may hold values from 0 to 7
Outputs:
- tracers_out: float32 [192, 8, 256, 128], P('tracer', None, 'tile')
Inputs may be any that keep to these rules, and one draw needn't show every extreme that they name: A reaction's two reactants may be the same tracer.
All inputs are finite; a program needn't handle non-finite values.
Results may differ from a plain program's by a relative error of at most 0.0014.
Values may be sent and summed in bfloat16 or wider, within the bound.
No kernel may reach another device: no remote copies, remote signals or barrier semaphores. Data moves between devices by JAX's collectives and lax.ppermute only.
A program may use at most 128 MiB of HBM per device.

v0:
```python
import jax
import jax.numpy as jnp
from jax import lax
from jax.sharding import PartitionSpec as P

STEPS = 2


def from_root(array, axis, root):
    mine = lax.axis_index(axis) == root
    return lax.psum(jnp.where(mine, array, jnp.zeros_like(array)), axis)


def with_halo(block, sides, width):
    for axis, dim in sides:
        count = lax.axis_size(axis)
        forward = [(i, i + 1) for i in range(count - 1)]
        backward = [(target, source) for source, target in forward]
        low = lax.ppermute(
            lax.slice_in_dim(block, block.shape[dim] - width, None, axis=dim), axis, forward
        )
        high = lax.ppermute(lax.slice_in_dim(block, 0, width, axis=dim), axis, backward)
        block = jnp.concatenate([low, block, high], axis=dim)
    return block


def take_slice(values, first_cell, how_many, dim_along):
    return lax.slice_in_dim(values, first_cell, first_cell + how_many, axis=dim_along)


def pad_three(values, dim_along):
    widths = [(0, 0)] * values.ndim
    widths[dim_along] = (3, 3)
    return jnp.pad(values, widths)


def face_flux(tracer_pad, air_pad, crossing, dim_along):
    cell_count = tracer_pad.shape[dim_along] - 6
    lower = take_slice(tracer_pad, 1, cell_count + 3, dim_along)
    upper = take_slice(tracer_pad, 2, cell_count + 3, dim_along)
    outer = take_slice(tracer_pad, 0, cell_count + 3, dim_along) + take_slice(
        tracer_pad, 3, cell_count + 3, dim_along
    )
    edges = 7.0 / 12.0 * (lower + upper) - 1.0 / 12.0 * outer
    edges = jnp.clip(edges, jnp.minimum(lower, upper), jnp.maximum(lower, upper))
    left_edge = take_slice(edges, 0, cell_count + 2, dim_along)
    right_edge = take_slice(edges, 1, cell_count + 2, dim_along)
    centre = take_slice(tracer_pad, 2, cell_count + 2, dim_along)
    spread = right_edge - left_edge
    bending = 6.0 * (centre - 0.5 * (left_edge + right_edge))
    upwind_air = jnp.where(
        crossing > 0,
        take_slice(air_pad, 2, cell_count + 1, dim_along),
        take_slice(air_pad, 3, cell_count + 1, dim_along),
    )
    courant = jnp.abs(crossing) / jnp.maximum(upwind_air, 0.5)
    factor = 1.0 - 2.0 * courant / 3.0
    from_left = take_slice(right_edge, 0, cell_count + 1, dim_along) - 0.5 * courant * (
        take_slice(spread, 0, cell_count + 1, dim_along)
        - factor * take_slice(bending, 0, cell_count + 1, dim_along)
    )
    from_right = take_slice(left_edge, 1, cell_count + 1, dim_along) + 0.5 * courant * (
        take_slice(spread, 1, cell_count + 1, dim_along)
        + factor * take_slice(bending, 1, cell_count + 1, dim_along)
    )
    return crossing * jnp.where(crossing > 0, from_left, from_right)


def divergence(flux_faces, dim_along, cell_count):
    return take_slice(flux_faces, 1, cell_count, dim_along) - take_slice(
        flux_faces, 0, cell_count, dim_along
    )


def close_walls(south_flux, bottom_flux):
    row_index = lax.broadcasted_iota(jnp.int32, south_flux.shape, 3)
    level_index = lax.broadcasted_iota(jnp.int32, bottom_flux.shape, 1)
    return (
        jnp.where(row_index == 0, 0.0, south_flux),
        jnp.where(level_index == 0, 0.0, bottom_flux),
    )


def advect(tracer_xpad, air_xpad, east_faces, south_flux, bottom_flux, air_now):
    level_count = air_now.shape[1]
    row_count = air_now.shape[2]
    column_count = air_now.shape[3]
    tracer = take_slice(tracer_xpad, 3, row_count, 2)
    north_faces = jnp.concatenate([south_flux, jnp.zeros_like(take_slice(south_flux, 0, 1, 3))], 3)
    upper_faces = jnp.concatenate(
        [bottom_flux, jnp.zeros_like(take_slice(bottom_flux, 0, 1, 1))], 1
    )
    flux_rows = face_flux(tracer_xpad, air_xpad, east_faces, 2)
    flux_columns = face_flux(pad_three(tracer, 3), pad_three(air_now, 3), north_faces, 3)
    flux_levels = face_flux(pad_three(tracer, 1), pad_three(air_now, 1), upper_faces, 1)
    air_next = (
        air_now
        - divergence(east_faces, 2, row_count)
        - divergence(north_faces, 3, column_count)
        - divergence(upper_faces, 1, level_count)
    )
    tracer_mass = (
        air_now * tracer
        - divergence(flux_rows, 2, row_count)
        - divergence(flux_columns, 3, column_count)
        - divergence(flux_levels, 1, level_count)
    )
    return tracer_mass / air_next


def per_device(
    tracers, air_mass, flux_x, flux_y, flux_z, reactants, products, rate_coeff, record_of_step
):
    tracer_count, level_count, row_count, column_count = tracers.shape
    reactions, species = products.shape
    ident = lax.broadcasted_iota(jnp.int32, (reactions, species), 1)
    first_hot = (reactants[:, 0:1] == ident).astype(jnp.float32)
    second_hot = (reactants[:, 1:2] == ident).astype(jnp.float32)
    selector = jnp.concatenate([first_hot, second_hot], 0).astype(jnp.bfloat16)
    net = (products.astype(jnp.float32) - first_hot - second_hot).astype(jnp.bfloat16)
    tile_place = lax.axis_index("tile")
    mixing = tracers
    for step_index in range(STEPS):
        air_now = from_root(air_mass[0], "tracer", record_of_step[step_index])[None]
        east = from_root(flux_x[0], "tracer", record_of_step[step_index])[None]
        south = from_root(flux_y[0], "tracer", record_of_step[step_index])[None]
        bottom = from_root(flux_z[0], "tracer", record_of_step[step_index])[None]
        stacked = jnp.concatenate([mixing, air_now, east], 0)
        extended = with_halo(stacked, (("tile", 2),), 3)
        tracer_xpad = extended[:tracer_count]
        air_xpad = extended[tracer_count : tracer_count + 1]
        east_next = extended[tracer_count + 1 :, :, row_count + 3 : row_count + 4]
        row_index = lax.broadcasted_iota(jnp.int32, east.shape, 2) + tile_place * row_count
        east = jnp.where(row_index == 0, 0.0, east)
        east_faces = jnp.concatenate([east, east_next], 2)
        south, bottom = close_walls(south, bottom)
        advected = advect(tracer_xpad, air_xpad, east_faces, south, bottom, air_now)
        conc = advected.astype(jnp.bfloat16)
        regroup_block = lax.all_to_all(conc, "tracer", split_axis=1, concat_axis=0, tiled=True)
        block_shape = regroup_block.shape
        flattened = regroup_block.reshape(block_shape[0], -1)
        picked = jnp.dot(selector, flattened, preferred_element_type=jnp.float32)
        reaction_rate = (rate_coeff[:, None] * picked[:reactions] * picked[reactions:]).astype(
            jnp.bfloat16
        )
        change = lax.dot_general(
            net, reaction_rate, (((0,), (0,)), ((), ())), preferred_element_type=jnp.float32
        )
        increment = lax.all_to_all(
            change.astype(jnp.bfloat16).reshape(block_shape),
            "tracer",
            split_axis=0,
            concat_axis=1,
            tiled=True,
        )
        mixing = advected + increment.astype(jnp.float32)
    return mixing


def solution(mesh):
    in_specs = (
        P("tracer", None, "tile", None),
        P("tracer", None, "tile", None),
        P("tracer", None, "tile", None),
        P("tracer", None, "tile", None),
        P("tracer", None, "tile", None),
        P(),
        P(),
        P(),
        P(),
    )
    out_specs = P("tracer", None, "tile", None)
    return jax.shard_map(
        per_device, mesh=mesh, in_specs=in_specs, out_specs=out_specs, check_vma=False
    )
```

profile of v0, /device:TPU:16, one launch (start us, length us, event | category | flops | bytes accessed | tf_op | source)
XLA Modules:
  0.0 230.5 jit_solution(7910685020544428439)
XLA Ops:
  10.8 1.6 select_bitcast_fusion.1
  12.4 2.0 copy.71
  14.4 3.1 %fusion.13 = f32[24,11,16,128]{3,1,2,0:T(8,128)} fusion(f32[24,8,16,128]{3,1,2,0:T(8,128)S(1)} %copy.71), kind=kLoop, calls=%fused_computation.37 | loop fusion | flops 4866048 | bytes 3735552 | tf_op jit(solution)/shard_map/jit(clip)/min | solution.py:45
  17.6 4.1 %fusion.6 = f32[24,8,16,131]{3,1,2,0:T(8,128)} fusion(f32[24,8,16,128]{3,1,2,0:T(8,128)S(1)} %copy.71), kind=kLoop, calls=%fused_computation.30 | loop fusion | flops 3621888 | bytes 3182592 | tf_op jit(solution)/shard_map/jit(clip)/min | solution.py:45
  21.7 6.8 %slice_subtract_fusion.2 = (f32[24,10,16,128]{3,1,2,0:T(8,128)}, f32[24,10,16,128]{3,1,2,0:T(8,128)}) fusion(f32[24,11,16,128]{3,1,2,0:T(8,128)} %fusion.13, f32[24,8,16,128]{3,1,2,0:T(8,128)S(1)} %copy.71), kind=kLoop, calls=%fused_computation.96 | loop fusion | flops 2457600 | bytes 9437184 | tf_op jit(solution)/shard_map/sub | solution.py:49
  28.6 7.2 %slice_subtract_fusion.3 = (f32[24,8,16,130]{3,1,2,0:T(8,128)}, f32[24,8,16,130]{3,1,2,0:T(8,128)}) fusion(f32[24,8,16,131]{3,1,2,0:T(8,128)} %fusion.6, f32[24,8,16,128]{3,1,2,0:T(8,128)S(1)} %copy.71), kind=kLoop, calls=%fused_computation.97 | loop fusion | flops 1996800 | bytes 7962624 | tf_op jit(solution)/shard_map/sub | solution.py:49
  35.8 65.4 %all-reduce.15.cloned.1.call-done = (f32[8,16,128]{2,0,1:T(8,128)}, f32[8,16,128]{2,0,1:T(8,128)}, f32[8,16,128]{2,0,1:T(8,128)}, f32[8,16,128]{2,0,1:T(8,128)},...) async-done(((f32[8,16,128]{2,0,1:T(8,128)}, f32[8,16,128]{2,0,1:T(8,128)}, f32[8,16,128]{2,0,1:T(8,128)}, ...) | async-done | bytes 524304 | tf_op jit(solution)/shard_map/psum | solution.py:11
  106.0 1.9 collective-permute-start
  108.0 2.6 %collective-permute-start.1 = (f32[26,8,3,128]{3,1,2,0:T(8,128)S(1)}, f32[26,8,3,128]{3,1,2,0:T(8,128)S(1)}, u32[]{:S(2)}, u32[]{:S(2)}) collective-permute-start(f32[26,8,3,128]{3,1,2,0:T(8,128)S(1)} %get-tuple-element.47), channel_id=1, source_target_pairs={{0,1},{1,2},{2,3},{3,4},{4,5},{5,6},{6,7},{7,8},{8,9},{9,10},{10,1... | collective-permute-start | bytes 958472 | tf_op jit(solution)/shard_map/ppermute | solution.py:19
  110.6 6.0 %fusion.50 = f32[24,9,16,128]{3,1,2,0:T(8,128)S(1)} fusion(f32[24,10,16,128]{3,1,2,0:T(8,128)} %get-tuple-element.36, f32[24,10,16,128]{3,1,2,0:T(8,128)} %get-tuple-element.35, f32[24,11,16,128]{3,1,2,0:T(8,128)S(1)} %copy-done.1, f32[9,16,128]{2,0,1:T(8,128)S(1)} %subtract_bitcast_fusion.2, f32[9,16,128]{2,0,1:T(8,128)S(1)} %get-tuple-element.27, ...), kind=kLoop, calls=%fused_computation.79 | loop fusion | flops 4423680 | bytes 10856448 | tf_op jit(solution)/shard_map/mul | solution.py:66
  118.0 2.6 %fusion.58 = f32[24,8,16,129]{3,1,2,0:T(8,128)S(1)} fusion(f32[24,8,16,130]{3,1,2,0:T(8,128)S(1)} %copy-done.3, f32[24,8,16,130]{3,1,2,0:T(8,128)S(1)} %copy-done.2, f32[24,8,16,131]{3,1,2,0:T(8,128)S(1)} %copy-done, f32[8,16,129]{2,0,1:T(8,128)S(1)} %subtract_bitcast_fusion.3, f32[8,16,129]{2,0,1:T(8,128)S(1)} %get-tuple-element.25, ...), kind=kLoop, calls=%fused_computation.89 | loop fusion | flops 3962880 | bytes 9725568 | tf_op jit(solution)/shard_map/mul | solution.py:66
  126.0 3.5 %all-to-all-start = ((bf16[24,8,16,128]{3,2,0,1:T(8,128)(2,1)}), bf16[24,8,16,128]{3,2,0,1:T(8,128)(2,1)S(1)}, u32[]{:S(2)}, u32[]{:S(2)}) async-start(bf16[24,8,16,128]{3,2,0,1:T(8,128)(2,1)} %copy.78), calls=%async_computation | async-start | bytes 1572864 | tf_op jit(solution)/shard_map/all_to_all | solution.py:139
  130.4 13.5 %all-to-all-done = bf16[24,8,16,128]{3,2,0,1:T(8,128)(2,1)S(1)} async-done(((bf16[24,8,16,128]{3,2,0,1:T(8,128)(2,1)}), bf16[24,8,16,128]{3,2,0,1:T(8,128)(2,1)S(1)}, u32[]{:S(2)}, u32[]{:S(2)}) %all-to-all-start) | async-done | bytes 786464 | tf_op jit(solution)/shard_map/all_to_all | solution.py:139
  147.2 3.9 %all-to-all-start.1 = ((bf16[192,1,16,128]{3,2,1,0:T(8,128)(2,1)}), bf16[192,1,16,128]{3,2,1,0:T(8,128)(2,1)S(1)}, u32[]{:S(2)}, u32[]{:S(2)}) async-start(bf16[192,1,16,128]{3,2,1,0:T(8,128)(2,1)} %bitcast.29), calls=%async_computation.1 | async-start | bytes 1572864 | tf_op jit(solution)/shard_map/all_to_all | solution.py:149
  151.9 12.4 %all-to-all-done.1 = bf16[192,1,16,128]{3,2,1,0:T(8,128)(2,1)S(1)} async-done(((bf16[192,1,16,128]{3,2,1,0:T(8,128)(2,1)}), bf16[192,1,16,128]{3,2,1,0:T(8,128)(2,1)S(1)}, u32[]{:S(2)}, u32[]{:S(2)}) %all-to-all-start.1) | async-done | bytes 786464 | tf_op jit(solution)/shard_map/all_to_all | solution.py:149
  167.0 2.5 %fusion.20 = f32[24,8,16,131]{3,1,2,0:T(8,128)S(1)} fusion(f32[24,8,16,128]{3,1,2,0:T(8,128)S(1)} %bitcast_add_fusion.1), kind=kLoop, calls=%fused_computation.44 | loop fusion | flops 3621888 | bytes 3182592 | tf_op jit(solution)/shard_map/jit(clip)/min | solution.py:45
  169.5 1.9 collective-permute-start.2
  172.6 1.8 slice_subtract_fusion.1
  174.4 2.7 %collective-permute-start.3 = (f32[26,8,3,128]{3,1,2,0:T(8,128)S(1)}, f32[26,8,3,128]{3,1,2,0:T(8,128)S(1)}, u32[]{:S(2)}, u32[]{:S(2)}) collective-permute-start(f32[26,8,3,128]{3,1,2,0:T(8,128)S(1)} %get-tuple-element.43), channel_id=1, source_target_pairs={{0,1},{1,2},{2,3},{3,4},{4,5},{5,6},{6,7},{7,8},{8,9},{9,10},{10,1... | collective-permute-start | bytes 958472 | tf_op jit(solution)/shard_map/ppermute | solution.py:19
  177.1 1.9 fusion.34
  179.0 2.7 %fusion.42 = f32[24,8,16,129]{3,1,2,0:T(8,128)S(1)} fusion(f32[24,8,16,130]{3,1,2,0:T(8,128)S(1)} %get-tuple-element.30, f32[24,8,16,130]{3,1,2,0:T(8,128)S(1)} %get-tuple-element.29, f32[24,8,16,131]{3,1,2,0:T(8,128)S(1)} %fusion.20, f32[8,16,129]{2,0,1:T(8,128)S(1)} %subtract_bitcast_fusion.1, f32[8,16,129]{2,0,1:T(8,128)S(1)} %copy-done.10, ...), kind=kLoop, calls=%fused_computation.69 | loop fusion | flops 3962880 | bytes 9725568 | tf_op jit(solution)/shard_map/mul | solution.py:66
  181.7 1.9 collective-permute-done.3
  186.5 17.2 %all_to_all.48 = bf16[24,8,16,128]{3,2,0,1:T(8,128)(2,1)S(1)} all-to-all(bf16[24,8,16,128]{3,2,0,1:T(8,128)(2,1)S(1)} %copy.85), channel_id=1, replica_groups=mesh['tracer'=8,'tile'=16] {'tracer'}, dimensions={1} | all-to-all | bytes 1572864 | tf_op jit(solution)/shard_map/all_to_all | solution.py:139
  206.1 15.0 %all_to_all.49 = bf16[192,1,16,128]{3,2,1,0:T(8,128)(2,1)S(1)} all-to-all(bf16[192,1,16,128]{3,2,1,0:T(8,128)(2,1)S(1)} %bitcast.150), channel_id=1, replica_groups=mesh['tracer'=8,'tile'=16] {'tracer'}, dimensions={0} | all-to-all | bytes 1572864 | tf_op jit(solution)/shard_map/all_to_all | solution.py:149
  (98 shorter events, 30.8 us)
Async XLA Ops:
  6.5 94.6 %all-reduce.15.cloned.1.call-start = ((), (), s32[]{:S(2)}) async-start(), calls=%async_computation.4 | async-start | bytes 1048576 | tf_op jit(solution)/shard_map/psum | solution.py:11
  101.2 9.4 %copy-start.1 = (f32[24,11,16,128]{3,1,2,0:T(8,128)S(1)}, f32[24,11,16,128]{3,1,2,0:T(8,128)}, u32[]{:S(2)}) copy-start(f32[24,11,16,128]{3,1,2,0:T(8,128)} %fusion.13) | copy-start | bytes 6488068
  106.0 14.7 %collective-permute-start = (f32[26,8,3,128]{3,1,2,0:T(8,128)S(1)}, f32[26,8,3,128]{3,1,2,0:T(8,128)S(1)}, u32[]{:S(2)}, u32[]{:S(2)}) collective-permute-start(f32[26,8,3,128]{3,1,2,0:T(8,128)S(1)} %get-tuple-element.48), channel_id=1, source_target_pairs={{1,0},{2,1},{3,2},{4,3},{5,4},{6,5},{7,6},{8,7},{9,8},{10,9},{11,1... | collective-permute-start | bytes 958472 | tf_op jit(solution)/shard_map/ppermute | solution.py:22
  108.0 12.8 %collective-permute-start.1 = (f32[26,8,3,128]{3,1,2,0:T(8,128)S(1)}, f32[26,8,3,128]{3,1,2,0:T(8,128)S(1)}, u32[]{:S(2)}, u32[]{:S(2)}) collective-permute-start(f32[26,8,3,128]{3,1,2,0:T(8,128)S(1)} %get-tuple-element.47), channel_id=1, source_target_pairs={{0,1},{1,2},{2,3},{3,4},{4,5},{5,6},{6,7},{7,8},{8,9},{9,10},{10,1... | collective-permute-start | bytes 958472 | tf_op jit(solution)/shard_map/ppermute | solution.py:19
  110.6 6.0 %copy-start = (f32[24,8,16,131]{3,1,2,0:T(8,128)S(1)}, f32[24,8,16,131]{3,1,2,0:T(8,128)}, u32[]{:S(2)}) copy-start(f32[24,8,16,131]{3,1,2,0:T(8,128)} %fusion.6) | copy-start | bytes 4829188
  110.6 6.5 %copy-start.2 = (f32[24,8,16,130]{3,1,2,0:T(8,128)S(1)}, f32[24,8,16,130]{3,1,2,0:T(8,128)}, u32[]{:S(2)}) copy-start(f32[24,8,16,130]{3,1,2,0:T(8,128)} %get-tuple-element.33) | copy-start | bytes 4792324
  110.6 7.4 %copy-start.3 = (f32[24,8,16,130]{3,1,2,0:T(8,128)S(1)}, f32[24,8,16,130]{3,1,2,0:T(8,128)}, u32[]{:S(2)}) copy-start(f32[24,8,16,130]{3,1,2,0:T(8,128)} %get-tuple-element.34) | copy-start | bytes 4792324
  118.0 2.6 %copy-start.7 = (f32[8,16,128]{2,0,1:T(8,128)S(1)}, f32[8,16,128]{2,0,1:T(8,128)}, u32[]{:S(2)}) copy-start(f32[8,16,128]{2,0,1:T(8,128)} %get-tuple-element.12) | copy-start | bytes 196612
  118.0 2.6 %copy-start.8 = (f32[8,16,128]{2,0,1:T(8,128)S(1)}, f32[8,16,128]{2,0,1:T(8,128)}, u32[]{:S(2)}) copy-start(f32[8,16,128]{2,0,1:T(8,128)} %get-tuple-element.8) | copy-start | bytes 196612
  118.0 2.7 %copy-start.6 = (f32[8,16,128]{2,0,1:T(8,128)S(1)}, f32[8,16,128]{2,0,1:T(8,128)}, u32[]{:S(2)}) copy-start(f32[8,16,128]{2,0,1:T(8,128)} %get-tuple-element.5) | copy-start | bytes 196612
  122.3 1.4 copy-start.4
  125.0 4.6 %copy-start.12 = (s32[512,2]{0,1:T(2,128)S(1)}, s32[512,2]{0,1:T(2,128)}, u32[]{:S(2)}) copy-start(s32[512,2]{0,1:T(2,128)} %param.14) | copy-start | bytes 12292
  125.0 4.7 %copy-start.5 = (f32[8,16,128]{2,0,1:T(8,128)S(1)}, f32[8,16,128]{2,0,1:T(8,128)}, u32[]{:S(2)}) copy-start(f32[8,16,128]{2,0,1:T(8,128)} %get-tuple-element.9) | copy-start | bytes 196612
  126.0 17.9 %all-to-all-start = ((bf16[24,8,16,128]{3,2,0,1:T(8,128)(2,1)}), bf16[24,8,16,128]{3,2,0,1:T(8,128)(2,1)S(1)}, u32[]{:S(2)}, u32[]{:S(2)}) async-start(bf16[24,8,16,128]{3,2,0,1:T(8,128)(2,1)} %copy.78), calls=%async_computation | async-start | bytes 1572864 | tf_op jit(solution)/shard_map/all_to_all | solution.py:139
  143.9 1.3 copy-start.13
  143.9 1.3 copy-start.15
  147.2 17.2 %all-to-all-start.1 = ((bf16[192,1,16,128]{3,2,1,0:T(8,128)(2,1)}), bf16[192,1,16,128]{3,2,1,0:T(8,128)(2,1)S(1)}, u32[]{:S(2)}, u32[]{:S(2)}) async-start(bf16[192,1,16,128]{3,2,1,0:T(8,128)(2,1)} %bitcast.29), calls=%async_computation.1 | async-start | bytes 1572864 | tf_op jit(solution)/shard_map/all_to_all | solution.py:149
  169.5 12.2 %collective-permute-start.2 = (f32[26,8,3,128]{3,1,2,0:T(8,128)S(1)}, f32[26,8,3,128]{3,1,2,0:T(8,128)S(1)}, u32[]{:S(2)}, u32[]{:S(2)}) collective-permute-start(f32[26,8,3,128]{3,1,2,0:T(8,128)S(1)} %get-tuple-element.44), channel_id=1, source_target_pairs={{1,0},{2,1},{3,2},{4,3},{5,4},{6,5},{7,6},{8,7},{9,8},{10,9},{11,1... | collective-permute-start | bytes 958472 | tf_op jit(solution)/shard_map/ppermute | solution.py:22
  172.6 4.5 %copy-start.9 = (f32[9,16,128]{2,0,1:T(8,128)S(1)}, f32[9,16,128]{2,0,1:T(8,128)}, u32[]{:S(2)}) copy-start(f32[9,16,128]{2,0,1:T(8,128)} %get-tuple-element.56) | copy-start | bytes 221188
  174.4 9.2 %collective-permute-start.3 = (f32[26,8,3,128]{3,1,2,0:T(8,128)S(1)}, f32[26,8,3,128]{3,1,2,0:T(8,128)S(1)}, u32[]{:S(2)}, u32[]{:S(2)}) collective-permute-start(f32[26,8,3,128]{3,1,2,0:T(8,128)S(1)} %get-tuple-element.43), channel_id=1, source_target_pairs={{0,1},{1,2},{2,3},{3,4},{4,5},{5,6},{6,7},{7,8},{8,9},{9,10},{10,1... | collective-permute-start | bytes 958472 | tf_op jit(solution)/shard_map/ppermute | solution.py:19
  177.1 1.9 copy-start.10
  177.1 1.9 copy-start.11
  203.7 1.3 copy-start.14
Sparse Core Ops, SparseCore 0:
  12.5 88.5 all-reduce.14
where the time goes:
time: 234 us; the launch traced here: 231 us
  waiting for transfers between devices  93.2 us (40%)
  other arithmetic  59.4 us (25%)
  blocking collectives  32.2 us (14%)
  starting transfers between devices  16.6 us (7%)
  between operations  15.3 us (7%)
  local copies, waits for them, and re-layouts  9.39 us (4%)
  matrix products  4.37 us (2%)
    psum x1, waiting for transfers between devices, from_root(): return lax.psum(jnp.where(mine, array, jnp.zeros_like(array)), axis)  65.4 us
    sub x6, other arithmetic, face_flux(): spread = right_edge - left_edge  17.6 us
    all_to_all x1, blocking collectives, per_device(): lax.all_to_all(conc, 'tracer', split_axis=1, concat_axis=0, tiled=True)  17.2 us
    all_to_all x1, blocking collectives, per_device(): lax.all_to_all(change.astype(jnp.bfloat16).reshape(block_shape), 'tracer'...  15 us
    mul x6, other arithmetic, face_flux(): return crossing * jnp.where(crossing > 0, from_left, from_right)  14.3 us
    all_to_all x1, waiting for transfers between devices, per_device(): lax.all_to_all(conc, 'tracer', split_axis=1, concat_axis=0, tiled=True)  13.5 us
    all_to_all x1, waiting for transfers between devices, per_device(): lax.all_to_all(change.astype(jnp.bfloat16).reshape(block_shape), 'tracer'...  12.4 us
    min x6, other arithmetic, face_flux(): jnp.clip(edges, jnp.minimum(lower, upper), jnp.maximum(lower, upper))  12.4 us
  transfers between devices with their start and end apart: 7, of which 4 were waited for; matrix products, arithmetic and copies ran while one was open for 18% of the time, Pallas kernels for 0%

commit v1 on v0

v1 whole, which is shorter than its diff:
```python
import functools

import jax
import jax.numpy as jnp
from jax import lax
from jax.experimental import pallas as pl
from jax.experimental.pallas import tpu as pltpu
from jax.sharding import PartitionSpec as P

STEPS = 2
F32 = jnp.float32
BF16 = jnp.bfloat16
ROWS = 16
GROUPS = 24
XA, XB, XC, YA, YB, YC, WA, WB, WC, ZA, ZB, ZC, MASS, INV = range(14)
VMEM = pl.BlockSpec(memory_space=pltpu.VMEM)
SMEM = pl.BlockSpec(memory_space=pltpu.SMEM)


def roll(x, shift):
    return pltpu.roll(x, shift % 128, axis=1)


def lane_of(shape):
    return lax.broadcasted_iota(jnp.int32, shape, 1)


def slot_of(shape):
    return lane_of(shape) & 15


def exchange_blocks(vectors):
    block = lane_of(vectors[0].shape) >> 4
    out = list(vectors)
    for bit in (1, 2, 4):
        low = (block & bit) == 0
        for i in range(8):
            if i & bit:
                continue
            first, second = out[i], out[i | bit]
            out[i] = jnp.where(low, first, roll(second, 16 * bit))
            out[i | bit] = jnp.where(low, roll(first, -16 * bit), second)
    return out


def pack_kernel(q_ref, mass_ref, fx_ref, fy_ref, fz_ref, out_ref):
    def row(r, carry):
        for tg in range(3):
            levels = [
                q_ref[pl.ds(tg * 1024 + lev * 16 + r, 8, stride=128), :] for lev in range(8)
            ]
            for dest, value in enumerate(exchange_blocks(levels)):
                out_ref[dest, 3 * r + tg] = value
        return carry

    lax.fori_loop(0, ROWS, row, 0)
    for field, ref in enumerate((mass_ref, fx_ref, fy_ref, fz_ref)):
        for half in range(2):
            levels = [ref[0, lev, 8 * half : 8 * half + 8, :] for lev in range(8)]
            for dest, value in enumerate(exchange_blocks(levels)):
                out_ref[dest, 48 + 2 * field + half] = value


def unpack_kernel(in_ref, out_ref):
    def row(r, carry):
        for tg in range(3):
            cols = [in_ref[src, 3 * r + tg] for src in range(8)]
            for lev, value in enumerate(exchange_blocks(cols)):
                out_ref[pl.ds(tg * 1024 + lev * 16 + r, 8, stride=128), :] = value
        return carry

    lax.fori_loop(0, ROWS, row, 0)


def write_edges(state_ref, row_up, row_down, col_right, col_left):
    slot = slot_of((8, 128)) >> 2

    def group(g, carry):
        src = g // 3
        tg = g - 3 * src
        for rr in range(3):
            row_down[src * 9 + 3 * rr + tg] = state_ref[src, 3 * rr + tg]
            row_up[src * 9 + 3 * rr + tg] = state_ref[src, 3 * (13 + rr) + tg]
        for block in range(4):
            rows = [state_ref[src, 3 * (4 * block + i) + tg] for i in range(4)]
            right = roll(rows[0], -12)
            left = rows[0]
            for i in range(1, 4):
                right = jnp.where(slot == i, roll(rows[i], 4 * i - 12) if i < 3 else rows[i], right)
                left = jnp.where(slot == i, roll(rows[i], 4 * i), left)
            col_right[g * 4 + block] = right
            col_left[g * 4 + block] = left
        return carry

    lax.fori_loop(0, GROUPS, group, 0)


def edge_kernel(rec_ref, in_ref, weather_ref, row_up, row_down, col_right, col_left):
    write_edges(in_ref, row_up, row_down, col_right, col_left)
    for s in range(STEPS):
        record = rec_ref[s]
        for k in range(8):
            weather_ref[s, k] = in_ref[record, 48 + k]
        row_up[72 + s] = in_ref[record, 48 + 1]
        row_down[72 + 2 * s] = in_ref[record, 48 + 0]
        row_down[72 + 2 * s + 1] = in_ref[record, 48 + 2]
        for half in range(2):
            col_right[96 + 2 * s + half] = in_ref[record, 48 + half]
            col_left[96 + 4 * s + half] = in_ref[record, 48 + half]
            col_left[96 + 4 * s + 2 + half] = in_ref[record, 48 + 4 + half]


def face_weights(flux, mass_low, mass_up):
    upwind = jnp.where(flux > 0, mass_low, mass_up)
    c = jnp.abs(flux) / jnp.maximum(upwind, 0.5)
    side = flux * c
    return flux * (1.0 - c) * (1.0 - c), side * (c - 1.0), side * (3.0 - 2.0 * c)


def write_weights(s, place_ref, weather_ref, row_lo, row_hi, col_lo, col_hi, ext_ref, put):
    tile, col = place_ref[0], place_ref[1]

    def both(ref, *index):
        return jnp.concatenate(
            [ref[index[:-1] + (index[-1],)], ref[index[:-1] + (index[-1] + 1,)]], 0
        )

    mass = both(weather_ref, s, 0)
    ext_ref[0, 0:8] = row_lo[72 + s]
    ext_ref[0, 8:24] = mass
    ext_ref[0, 24:32] = row_hi[72 + 2 * s]
    row = lax.broadcasted_iota(jnp.int32, (16, 128), 0)
    ext_ref[1, 0:16] = jnp.where((row == 0) & (tile == 0), 0.0, both(weather_ref, s, 2))
    ext_ref[1, 16:24] = row_hi[72 + 2 * s + 1]
    ext_ref[1, 24:32] = jnp.zeros((8, 128), F32)
    east = ext_ref[1, 0:24]
    for k, value in enumerate(face_weights(east, ext_ref[0, 7:31], ext_ref[0, 8:32])):
        put(XA + k, 24, value)
    shape = (16, 128)
    slot, lane = slot_of(shape), lane_of(shape)
    mass_x = jnp.where(slot < 8, roll(both(col_hi, 96 + 4 * s), 16), roll(both(col_lo, 96 + 2 * s), -16))
    south = jnp.where((slot == 0) & (col == 0), 0.0, both(weather_ref, s, 4))
    south_x = roll(both(col_hi, 96 + 4 * s + 2), 16)
    low = roll(jnp.where(slot == 15, mass_x, mass), 1)
    for k, value in enumerate(face_weights(south, low, mass)):
        put(YA + k, 16, value)
    low = roll(jnp.where(slot == 15, mass, mass_x), 1)
    for k, value in enumerate(face_weights(south_x, low, mass_x)):
        put(WA + k, 16, value)
    bottom = jnp.where(lane < 16, 0.0, both(weather_ref, s, 6))
    for k, value in enumerate(face_weights(bottom, roll(mass, 16), mass)):
        put(ZA + k, 16, value)
    new_mass = (
        mass
        - (ext_ref[1, 1:17] - ext_ref[1, 0:16])
        - (roll(jnp.where(slot == 0, south_x, south), -1) - south)
        - (roll(bottom, -16) - bottom)
    )
    put(MASS, 16, mass)
    put(INV, 16, 1.0 / new_mass)


def edge_value(low2, low1, up1, up2):
    value = (7.0 / 12.0) * (low1 + up1) - (1.0 / 12.0) * (low2 + up2)
    return jnp.minimum(
        jnp.maximum(value, jnp.minimum(low1, up1)), jnp.maximum(low1, up1)
    )


def face_flux(weights, edge, below, above, q_low, q_up):
    a, b, c = weights
    forward = c > 0
    return a * edge + b * jnp.where(forward, below, above) + c * jnp.where(forward, q_low, q_up)


def advect(q_ref, row_lo, row_hi, col_lo, col_hi, get, out_ref, conc_ref):
    shape = (8, 128)
    slot, lane = slot_of(shape), lane_of(shape)
    first, last, last_two, left_half = slot == 0, slot == 15, slot >= 14, slot < 8

    def one_group(src, tg):
        def q_row(k):
            if k < 0:
                return row_lo[src * 9 + 3 * (k + 3) + tg]
            if k >= ROWS:
                return row_hi[src * 9 + 3 * (k - ROWS) + tg]
            return q_ref[src, 3 * k + tg]

        g = src * 3 + tg
        q = {k: q_row(k) for k in (-3, -2, -1, 0)}
        edges = {}

        def x_edge(k):
            for need in (k - 2, k - 1, k, k + 1):
                if need not in q:
                    q[need] = q_row(need)
            if k not in edges:
                edges[k] = edge_value(q[k - 2], q[k - 1], q[k], q[k + 1])
            return edges[k]

        def x_flux(r):
            return face_flux(
                [get(XA + i, r) for i in range(3)],
                x_edge(r), x_edge(r - 1), x_edge(r + 1), q[r - 1], q[r],
            )

        results = []
        below = x_flux(0)
        for r in range(ROWS):
            above = x_flux(r + 1)
            here = q[r]
            block, i = r // 4, r % 4
            x = jnp.where(
                left_half,
                roll(col_hi[g * 4 + block], 16 - 4 * i),
                roll(col_lo[g * 4 + block], -4 - 4 * i),
            )
            m1 = roll(jnp.where(last, x, here), 1)
            m2 = roll(jnp.where(last_two, x, here), 2)
            p1 = roll(jnp.where(first, x, here), -1)
            edge = edge_value(m2, m1, here, p1)
            x_m1 = roll(jnp.where(last, here, x), 1)
            x_m2 = roll(jnp.where(last_two, here, x), 2)
            x_p1 = roll(jnp.where(first, here, x), -1)
            edge_x = edge_value(x_m2, x_m1, x, x_p1)
            flux_y = face_flux(
                [get(YA + i, r) for i in range(3)], edge,
                roll(jnp.where(last, edge_x, edge), 1),
                roll(jnp.where(first, edge_x, edge), -1), m1, here,
            )
            flux_w = face_flux(
                [get(WA + i, r) for i in range(3)], edge_x,
                roll(jnp.where(last, edge, edge_x), 1), roll(edge_x, -1), x_m1, x,
            )
            flux_y_up = roll(jnp.where(first, flux_w, flux_y), -1)
            m1 = jnp.where(lane >= 16, roll(here, 16), 0.0)
            m2 = jnp.where(lane >= 32, roll(here, 32), 0.0)
            p1 = jnp.where(lane < 112, roll(here, -16), 0.0)
            edge = edge_value(m2, m1, here, p1)
            top = (7.0 / 12.0) * here - (1.0 / 12.0) * m1
            top = jnp.minimum(jnp.maximum(top, jnp.minimum(here, 0.0)), jnp.maximum(here, 0.0))
            flux_z = face_flux(
                [get(ZA + i, r) for i in range(3)], edge, roll(edge, 16),
                jnp.where(lane >= 112, top, roll(edge, -16)), m1, here,
            )
            moved = (
                get(MASS, r) * here
                - (above - below)
                - (flux_y_up - flux_y)
                - (roll(flux_z, -16) - flux_z)
            ) * get(INV, r)
            out_ref[src, 3 * r + tg] = moved
            results.append(moved)
            below = above
        return results

    def pair(p, carry):
        parts = []
        for k in range(2):
            g = 2 * p + k
            src = g // 3
            parts.append(one_group(src, g - 3 * src))
        start = pl.multiple_of(16 * p, 16)
        for r in range(ROWS):
            conc_ref[pl.ds(start, 16), 128 * r : 128 * r + 128] = jnp.concatenate(
                [parts[0][r], parts[1][r]], 0
            ).astype(BF16)
        return carry

    lax.fori_loop(0, GROUPS // 2, pair, 0)


def react(conc_ref, sel_ref, net_ref, coeff_ref, rate_ref, out_ref):
    def block(n, carry):
        lanes = pl.ds(pl.multiple_of(256 * n, 256), 256)
        conc = conc_ref[:, lanes]
        for k in range(4):
            part = slice(128 * k, 128 * k + 128)
            one = jnp.dot(sel_ref[part, :], conc, preferred_element_type=F32)
            two = jnp.dot(
                sel_ref[512 + 128 * k : 640 + 128 * k, :], conc, preferred_element_type=F32
            )
            rate_ref[part, :] = (coeff_ref[part, :] * one * two).astype(BF16)
        change = jnp.dot(net_ref[...], rate_ref[...], preferred_element_type=F32)
        change = change.astype(BF16).astype(F32)
        for i in range(2):
            r = 2 * n + i
            for g in range(GROUPS):
                part = change[8 * g : 8 * g + 8, 128 * i : 128 * i + 128]
                out_ref[g // 3, 3 * r + g % 3] += part
        return carry

    lax.fori_loop(0, ROWS // 2, block, 0)


def first_kernel(
    place_ref, q_ref, weather_ref, row_lo, row_hi, col_lo, col_hi, sel_ref, net_ref, coeff_ref,
    out_ref, later_ref, row_up, row_down, col_right, col_left, now_ref, ext_ref, conc_ref, rate_ref,
):
    for s, ref in enumerate((now_ref, later_ref)):
        def put(k, rows, value, ref=ref):
            ref[k, 0:rows] = value

        write_weights(s, place_ref, weather_ref, row_lo, row_hi, col_lo, col_hi, ext_ref, put)

    def get(k, r):
        return now_ref[k, pl.ds(r, 8, stride=0), :]

    advect(q_ref, row_lo, row_hi, col_lo, col_hi, get, out_ref, conc_ref)
    react(conc_ref, sel_ref, net_ref, coeff_ref, rate_ref, out_ref)
    write_edges(out_ref, row_up, row_down, col_right, col_left)


def second_kernel(
    now_ref, q_ref, row_lo, row_hi, col_lo, col_hi, sel_ref, net_ref, coeff_ref,
    out_ref, conc_ref, rate_ref,
):
    def get(k, r):
        return now_ref[k, pl.ds(r, 8, stride=0), :]

    advect(q_ref, row_lo, row_hi, col_lo, col_hi, get, out_ref, conc_ref)
    react(conc_ref, sel_ref, net_ref, coeff_ref, rate_ref, out_ref)


def blocks(*lead):
    return jax.ShapeDtypeStruct(lead + (8, 128), F32)


def call(kernel, outs, specs, scratch=(), args=()):
    single = not isinstance(outs, (list, tuple))
    return pl.pallas_call(
        kernel,
        out_shape=outs,
        in_specs=specs,
        out_specs=VMEM if single else [VMEM] * len(outs),
        scratch_shapes=list(scratch),
        compiler_params=pltpu.CompilerParams(vmem_limit_bytes=40 * 2**20),
    )(*args)


def swap(x):
    return lax.all_to_all(x, "tracer", split_axis=0, concat_axis=0, tiled=True)


def halo(row_up, row_down, col_right, col_left):
    def shift(x, axis, step):
        count = lax.axis_size(axis)
        pairs = [(i, i + step) for i in range(count) if 0 <= i + step < count]
        return lax.ppermute(x, axis, pairs)

    return (
        shift(row_up, "tile", 1),
        shift(row_down, "tile", -1),
        shift(col_right, "tracer", 1),
        shift(col_left, "tracer", -1),
    )


def per_device(
    tracers, air_mass, flux_x, flux_y, flux_z, reactants, products, rate_coeff, record_of_step
):
    reactions, species = products.shape
    place = jnp.stack([lax.axis_index("tile"), lax.axis_index("tracer")]).astype(jnp.int32)
    ident = lax.broadcasted_iota(jnp.int32, (reactions, species), 1)
    selector = jnp.concatenate(
        [reactants[:, 0:1] == ident, reactants[:, 1:2] == ident], 0
    ).astype(BF16)
    ident = lax.broadcasted_iota(jnp.int32, (species, reactions), 0)
    net = (
        products.T
        - (reactants.T[0:1] == ident).astype(jnp.int32)
        - (reactants.T[1:2] == ident).astype(jnp.int32)
    ).astype(BF16)
    coeff = jnp.broadcast_to(rate_coeff[:, None], (reactions, 256))

    sent = call(
        pack_kernel, blocks(8, 56), [VMEM] * 5,
        args=(tracers.reshape(-1, 128), air_mass, flux_x, flux_y, flux_z),
    )
    state = swap(sent)
    weather, *edges = call(
        edge_kernel,
        [blocks(STEPS, 8), blocks(74), blocks(76), blocks(100), blocks(104)],
        [SMEM, VMEM],
        args=(record_of_step, state),
    )
    scratch = [pltpu.VMEM((species, 128 * ROWS), BF16), pltpu.VMEM((reactions, 256), BF16)]
    weights = (14, 24, 128)
    state, later, *edges = call(
        first_kernel,
        [
            blocks(8, 48), jax.ShapeDtypeStruct(weights, F32),
            blocks(72), blocks(72), blocks(96), blocks(96),
        ],
        [SMEM] + [VMEM] * 9,
        [pltpu.VMEM(weights, F32), pltpu.VMEM((2, 32, 128), F32)] + scratch,
        (place, state, weather) + halo(*edges) + (selector, net, coeff),
    )
    state = call(
        second_kernel,
        blocks(8, 48),
        [VMEM] * 9,
        scratch,
        (later, state) + halo(*edges) + (selector, net, coeff),
    )
    out = call(
        unpack_kernel, jax.ShapeDtypeStruct((tracers.size // 128, 128), F32), [VMEM],
        args=(swap(state),),
    )
    return out.reshape(tracers.shape)


def solution(mesh):
    fields = P("tracer", None, "tile", None)
    return jax.shard_map(
        per_device,
        mesh=mesh,
        in_specs=(fields,) * 5 + (P(),) * 4,
        out_specs=fields,
        check_vma=False,
    )
```

time: 234 us -> 314 us (1.34)
  Pallas kernels: 0 us -> 188 us
  other arithmetic: 59.4 us -> 1.5 us
  waiting for transfers between devices: 93.2 us -> 53.9 us
  starting transfers between devices: 16.6 us -> 32.7 us
  between operations: 15.3 us -> 0.17 us
  blocking collectives: 32.2 us -> 26.9 us
  matrix products: 4.37 us -> 0 us
    pallas_call x0 -> x5, Pallas kernels: none -> 188 us  [call(): pl.pallas_call(kernel, out_shape=outs, in_specs=specs, out_specs=VMEM if...]
    psum x1 -> x0, waiting for transfers between devices: 65.4 us -> none  [from_root(): return lax.psum(jnp.where(mine, array, jnp.zeros_like(array)), axis)]
    ppermute x4 -> x8, waiting for transfers between devices: 1.86 us -> 26.8 us  [shift(): return lax.ppermute(x, axis, pairs)]
    mul x18 -> x0, other arithmetic: 17.8 us -> none  [the longest x6 14.3 us: face_flux(): return crossing * jnp.where(crossing > 0, from_left, from_right)]
    sub x6 -> x0, other arithmetic: 17.6 us -> none  [face_flux(): spread = right_edge - left_edge]
    ppermute x4 -> x8, starting transfers between devices: 9.09 us -> 24.9 us  [shift(): return lax.ppermute(x, axis, pairs)]
    min x6 -> x0, other arithmetic: 12.4 us -> none  [face_flux(): jnp.clip(edges, jnp.minimum(lower, upper), jnp.maximum(lower, upper))]
    all_to_all x2 -> x1, blocking collectives: 32.2 us -> 26.9 us  [swap(): return lax.all_to_all(x, 'tracer', split_axis=0, concat_axis=0, tiled=True)]
  transfers between devices with their start and end apart: 7 -> 9, of which waited for: 4 -> 7; matrix products, arithmetic and copies ran while one was open for 18% -> 0% of each run, Pallas kernels for 0% -> 0%
where the time goes in v1:
time: 314 us; the launch traced here: 311 us
  Pallas kernels  188 us (60%)
  waiting for transfers between devices  53.9 us (17%)
  starting transfers between devices  32.7 us (10%)
  blocking collectives  26.9 us (9%)
  local copies, waits for them, and re-layouts  7.6 us (2%)
    pallas_call x5, Pallas kernels, call(): pl.pallas_call(kernel, out_shape=outs, in_specs=specs, out_specs=VMEM if...  188 us
    all_to_all x1, waiting for transfers between devices, swap(): return lax.all_to_all(x, 'tracer', split_axis=0, concat_axis=0, tiled=True)  27.1 us
    all_to_all x1, blocking collectives, swap(): return lax.all_to_all(x, 'tracer', split_axis=0, concat_axis=0, tiled=True)  26.9 us
    ppermute x8, waiting for transfers between devices, shift(): return lax.ppermute(x, axis, pairs)  26.8 us
    ppermute x8, starting transfers between devices, shift(): return lax.ppermute(x, axis, pairs)  24.9 us
    all_to_all x1, starting transfers between devices, swap(): return lax.all_to_all(x, 'tracer', split_axis=0, concat_axis=0, tiled=True)  7.74 us
    unnamed x22, local copies, waits for them, and re-layouts  7.46 us
  transfers between devices with their start and end apart: 9, of which 7 were waited for; matrix products, arithmetic and copies ran while one was open for 0% of the time, Pallas kernels for 0%

profile of v1, /device:TPU:16, one launch (start us, length us, event | category | flops | bytes accessed | tf_op | source)
XLA Modules:
  0.0 311.1 jit_solution(13582455475362492396)
XLA Ops:
  0.0 1.4 copy-done.1
  1.4 0.8 copy-done.2
  4.8 4.6 %shard_map.91 = f32[8,56,8,128]{3,2,1,0:T(8,128)S(1)} custom-call(f32[3072,128]{1,0:T(8,128)S(1)} %bitcast.15, f32[1,8,16,128]{3,2,1,0:T(8,128)S(1)} %copy-done.2, f32[1,8,16,128]{3,2,1,0:T(8,128)S(1)} %copy-done.3, f32[1,8,16,128]{3,2,1,0:T(8,128)S(1)} %copy-done.4, f32[1,8,16,128]{3,2,1,0:T(8,128)S(1)} %copy-done.5), custom_call_target="tpu_custom_call" | custom-call | tf_op jit(solution)/shard_map/pallas_call | solution.py:331
  9.4 1.3 copy-done
  10.6 7.7 %all-to-all-start = ((f32[8,56,8,128]{3,2,1,0:T(8,128)}), f32[8,56,8,128]{3,2,1,0:T(8,128)S(1)}, u32[]{:S(2)}, u32[]{:S(2)}) async-start(f32[8,56,8,128]{3,2,1,0:T(8,128)} %copy-done), calls=%async_computation | async-start | bytes 3670016 | tf_op jit(solution)/shard_map/all_to_all | solution.py:342
  18.6 27.1 %all-to-all-done.in_ref.q_ref = f32[8,56,8,128]{3,2,1,0:T(8,128)S(1)} async-done(((f32[8,56,8,128]{3,2,1,0:T(8,128)}), f32[8,56,8,128]{3,2,1,0:T(8,128)S(1)}, u32[]{:S(2)}, u32[]{:S(2)}) %all-to-all-start) | async-done | bytes 1835040 | tf_op jit(solution)/shard_map/all_to_all | solution.py:342
  45.8 3.9 %shard_map.92 = (f32[2,8,8,128]{3,2,1,0:T(8,128)S(1)}, f32[74,8,128]{2,1,0:T(8,128)S(1)}, f32[76,8,128]{2,1,0:T(8,128)S(1)}, f32[100,8,128]{2,1,0:T(8,128)}, f32[104,8,128]{2,1,0:T(8,128)}) custom-call(s32[2]{0:T(128)S(1)} %copy-done.6, f32[8,56,8,128]{3,2,1,0:T(8,128)S(1)} %all-to-all-done.in_ref.q_ref), custom_call_target="tpu_custom_call" | custom-call | tf_op jit(solution)/shard_map/pallas_call | solution.py:331
  51.1 3.6 %collective-permute-start.2 = (f32[100,8,128]{2,1,0:T(8,128)}, f32[100,8,128]{2,1,0:T(8,128)S(1)}, u32[]{:S(2)}, u32[]{:S(2)}) collective-permute-start(f32[100,8,128]{2,1,0:T(8,128)} %get-tuple-element.19), channel_id=1, source_target_pairs={{0,16},{16,32},{32,48},{48,64},{64,80},{80,96},{96,112},{1,17},{17... | collective-permute-start | bytes 1228808 | tf_op jit(solution)/shard_map/ppermute | solution.py:349
  54.7 1.3 collective-permute-start.3
  56.2 1.9 collective-permute-start
  58.1 4.5 %collective-permute-start.1 = (f32[76,8,128]{2,1,0:T(8,128)}, f32[76,8,128]{2,1,0:T(8,128)S(1)}, u32[]{:S(2)}, u32[]{:S(2)}) collective-permute-start(f32[76,8,128]{2,1,0:T(8,128)} %copy-done.7), channel_id=1, source_target_pairs={{1,0},{2,1},{3,2},{4,3},{5,4},{6,5},{7,6},{8,7},{9,8},{10,9},{11,1... | collective-permute-start | bytes 933896 | tf_op jit(solution)/shard_map/ppermute | solution.py:349
  62.7 1.1 fusion.1.net_ref
  63.8 4.9 %collective-permute-done.row_lo = f32[74,8,128]{2,1,0:T(8,128)S(1)} collective-permute-done((f32[74,8,128]{2,1,0:T(8,128)}, f32[74,8,128]{2,1,0:T(8,128)S(1)}, u32[]{:S(2)}, u32[]{:S(2)}) %collective-permute-start) | collective-permute-done | bytes 303136 | tf_op jit(solution)/shard_map/ppermute | solution.py:349
  68.9 8.4 %collective-permute-done.2.col_lo = f32[100,8,128]{2,1,0:T(8,128)S(1)} collective-permute-done((f32[100,8,128]{2,1,0:T(8,128)}, f32[100,8,128]{2,1,0:T(8,128)S(1)}, u32[]{:S(2)}, u32[]{:S(2)}) %collective-permute-start.2) | collective-permute-done | bytes 409632 | tf_op jit(solution)/shard_map/ppermute | solution.py:349
  77.5 88.7 %shard_map.93 = (f32[8,48,8,128]{3,2,1,0:T(8,128)S(1)}, f32[14,24,128]{2,1,0:T(8,128)S(1)}, f32[72,8,128]{2,1,0:T(8,128)S(1)}, f32[72,8,128]{2,1,0:T(8,128)S(1)}...) custom-call(s32[2]{0:T(128)S(1)} %pad_add_fusion.place_ref, f32[8,56,8,128]{3,2,1,0:T(8,128)S(1)} %all-to-all-done.in_ref.q_ref, ...), custom_call_target="tpu_custom_call" | custom-call | tf_op jit(solution)/shard_map/pallas_call | solution.py:331
  166.2 5.8 %collective-permute-start.6 = (f32[96,8,128]{2,1,0:T(8,128)S(1)}, f32[96,8,128]{2,1,0:T(8,128)S(1)}, u32[]{:S(2)}, u32[]{:S(2)}) collective-permute-start(f32[96,8,128]{2,1,0:T(8,128)S(1)} %get-tuple-element.25), channel_id=1, source_target_pairs={{0,16},{16,32},{32,48},{48,64},{64,80},{80,96},{96,112},{1,17},{17... | collective-permute-start | bytes 1179656 | tf_op jit(solution)/shard_map/ppermute | solution.py:349
  171.9 1.3 collective-permute-start.7
  173.2 1.9 collective-permute-start.4
  175.2 4.5 %collective-permute-start.5 = (f32[72,8,128]{2,1,0:T(8,128)S(1)}, f32[72,8,128]{2,1,0:T(8,128)S(1)}, u32[]{:S(2)}, u32[]{:S(2)}) collective-permute-start(f32[72,8,128]{2,1,0:T(8,128)S(1)} %get-tuple-element.24), channel_id=1, source_target_pairs={{1,0},{2,1},{3,2},{4,3},{5,4},{6,5},{7,6},{8,7},{9,8},{10,9},{11,1... | collective-permute-start | bytes 884744 | tf_op jit(solution)/shard_map/ppermute | solution.py:349
  179.7 5.7 %collective-permute-done.4.row_lo = f32[72,8,128]{2,1,0:T(8,128)S(1)} collective-permute-done((f32[72,8,128]{2,1,0:T(8,128)S(1)}, f32[72,8,128]{2,1,0:T(8,128)S(1)}, u32[]{:S(2)}, u32[]{:S(2)}) %collective-permute-start.4) | collective-permute-done | bytes 294944 | tf_op jit(solution)/shard_map/ppermute | solution.py:349
  186.1 6.9 %collective-permute-done.6.col_lo = f32[96,8,128]{2,1,0:T(8,128)S(1)} collective-permute-done((f32[96,8,128]{2,1,0:T(8,128)S(1)}, f32[96,8,128]{2,1,0:T(8,128)S(1)}, u32[]{:S(2)}, u32[]{:S(2)}) %collective-permute-start.6) | collective-permute-done | bytes 393248 | tf_op jit(solution)/shard_map/ppermute | solution.py:349
  193.0 85.6 %shard_map.94 = f32[8,48,8,128]{3,2,1,0:T(8,128)S(1)} custom-call(f32[14,24,128]{2,1,0:T(8,128)S(1)} %get-tuple-element.21.now_ref, f32[8,48,8,128]{3,2,1,0:T(8,128)S(1)} %get-tuple-element.22.q_ref, f32[72,8,128]{2,1,0:T(8,128)S(1)} %collective-permute-done.4.row_lo, f32[72,8,128]{2,1,0:T(8,128)S(1)} %collective-permute-done.5.row_hi, ...), custom_call_target="tpu_custom_call" | custom-call | tf_op jit(solution)/shard_map/pallas_call | solution.py:331
  278.6 26.9 %all_to_all.10.in_ref = f32[8,48,8,128]{3,2,1,0:T(8,128)S(1)} all-to-all(f32[8,48,8,128]{3,2,1,0:T(8,128)S(1)} %shard_map.94), channel_id=1, replica_groups=mesh['tracer'=8,'tile'=16] {'tracer'}, dimensions={0} | all-to-all | bytes 3145728 | tf_op jit(solution)/shard_map/all_to_all | solution.py:342
  305.5 5.6 %shard_map.95 = f32[3072,128]{1,0:T(8,128)} custom-call(f32[8,48,8,128]{3,2,1,0:T(8,128)S(1)} %all_to_all.10.in_ref), custom_call_target="tpu_custom_call" | custom-call | tf_op jit(solution)/shard_map/pallas_call | solution.py:331
  (29 shorter events, 5.4 us)
Async XLA Ops:
  0.0 1.4 copy-start.1
  1.4 0.8 copy-start.2
  2.2 0.8 copy-start.3
  3.1 0.8 copy-start.4
  3.9 0.8 copy-start.5
  9.4 1.3 copy-start
  10.6 7.8 %copy-start.9 = (s32[512,2]{0,1:T(2,128)S(1)}, s32[512,2]{0,1:T(2,128)}, u32[]{:S(2)}) copy-start(s32[512,2]{0,1:T(2,128)} %param.14) | copy-start | bytes 12292
  10.6 35.1 %copy-start.6 = (s32[2]{0:T(128)S(1)}, s32[2]{0:T(128)}, u32[]{:S(2)}) copy-start(s32[2]{0:T(128)} %rec_ref.1) | copy-start | bytes 28
  10.6 35.1 %all-to-all-start = ((f32[8,56,8,128]{3,2,1,0:T(8,128)}), f32[8,56,8,128]{3,2,1,0:T(8,128)S(1)}, u32[]{:S(2)}, u32[]{:S(2)}) async-start(f32[8,56,8,128]{3,2,1,0:T(8,128)} %copy-done), calls=%async_computation | async-start | bytes 3670016 | tf_op jit(solution)/shard_map/all_to_all | solution.py:342
  18.6 58.7 %copy-start.10 = (f32[512]{0:T(512)S(1)}, f32[512]{0:T(512)}, u32[]{:S(2)}) copy-start(f32[512]{0:T(512)} %param.16) | copy-start | bytes 6148
  49.7 0.7 copy-start.7
  50.4 0.7 copy-start.8
  51.1 26.2 %collective-permute-start.2 = (f32[100,8,128]{2,1,0:T(8,128)}, f32[100,8,128]{2,1,0:T(8,128)S(1)}, u32[]{:S(2)}, u32[]{:S(2)}) collective-permute-start(f32[100,8,128]{2,1,0:T(8,128)} %get-tuple-element.19), channel_id=1, source_target_pairs={{0,16},{16,32},{32,48},{48,64},{64,80},{80,96},{96,112},{1,17},{17... | collective-permute-start | bytes 1228808 | tf_op jit(solution)/shard_map/ppermute | solution.py:349
  54.7 22.6 %collective-permute-start.3 = (f32[104,8,128]{2,1,0:T(8,128)}, f32[104,8,128]{2,1,0:T(8,128)S(1)}, u32[]{:S(2)}, u32[]{:S(2)}) collective-permute-start(f32[104,8,128]{2,1,0:T(8,128)} %get-tuple-element.20), channel_id=1, source_target_pairs={{16,0},{32,16},{48,32},{64,48},{80,64},{96,80},{112,96},{17,1},{33... | collective-permute-start | bytes 1277960 | tf_op jit(solution)/shard_map/ppermute | solution.py:349
  56.2 12.5 %collective-permute-start = (f32[74,8,128]{2,1,0:T(8,128)}, f32[74,8,128]{2,1,0:T(8,128)S(1)}, u32[]{:S(2)}, u32[]{:S(2)}) collective-permute-start(f32[74,8,128]{2,1,0:T(8,128)} %copy-done.8), channel_id=1, source_target_pairs={{0,1},{1,2},{2,3},{3,4},{4,5},{5,6},{6,7},{7,8},{8,9},{9,10},{10,1... | collective-permute-start | bytes 909320 | tf_op jit(solution)/shard_map/ppermute | solution.py:349
  58.1 10.8 %collective-permute-start.1 = (f32[76,8,128]{2,1,0:T(8,128)}, f32[76,8,128]{2,1,0:T(8,128)S(1)}, u32[]{:S(2)}, u32[]{:S(2)}) collective-permute-start(f32[76,8,128]{2,1,0:T(8,128)} %copy-done.7), channel_id=1, source_target_pairs={{1,0},{2,1},{3,2},{4,3},{5,4},{6,5},{7,6},{8,7},{9,8},{10,9},{11,1... | collective-permute-start | bytes 933896 | tf_op jit(solution)/shard_map/ppermute | solution.py:349
  166.2 26.8 %collective-permute-start.6 = (f32[96,8,128]{2,1,0:T(8,128)S(1)}, f32[96,8,128]{2,1,0:T(8,128)S(1)}, u32[]{:S(2)}, u32[]{:S(2)}) collective-permute-start(f32[96,8,128]{2,1,0:T(8,128)S(1)} %get-tuple-element.25), channel_id=1, source_target_pairs={{0,16},{16,32},{32,48},{48,64},{64,80},{80,96},{96,112},{1,17},{17... | collective-permute-start | bytes 1179656 | tf_op jit(solution)/shard_map/ppermute | solution.py:349
  171.9 21.1 %collective-permute-start.7 = (f32[96,8,128]{2,1,0:T(8,128)S(1)}, f32[96,8,128]{2,1,0:T(8,128)S(1)}, u32[]{:S(2)}, u32[]{:S(2)}) collective-permute-start(f32[96,8,128]{2,1,0:T(8,128)S(1)} %get-tuple-element.26), channel_id=1, source_target_pairs={{16,0},{32,16},{48,32},{64,48},{80,64},{96,80},{112,96},{17,1},{33... | collective-permute-start | bytes 1179656 | tf_op jit(solution)/shard_map/ppermute | solution.py:349
  173.2 12.2 %collective-permute-start.4 = (f32[72,8,128]{2,1,0:T(8,128)S(1)}, f32[72,8,128]{2,1,0:T(8,128)S(1)}, u32[]{:S(2)}, u32[]{:S(2)}) collective-permute-start(f32[72,8,128]{2,1,0:T(8,128)S(1)} %get-tuple-element.23), channel_id=1, source_target_pairs={{0,1},{1,2},{2,3},{3,4},{4,5},{5,6},{6,7},{7,8},{8,9},{9,10},{10,1... | collective-permute-start | bytes 884744 | tf_op jit(solution)/shard_map/ppermute | solution.py:349
  175.2 11.0 %collective-permute-start.5 = (f32[72,8,128]{2,1,0:T(8,128)S(1)}, f32[72,8,128]{2,1,0:T(8,128)S(1)}, u32[]{:S(2)}, u32[]{:S(2)}) collective-permute-start(f32[72,8,128]{2,1,0:T(8,128)S(1)} %get-tuple-element.24), channel_id=1, source_target_pairs={{1,0},{2,1},{3,2},{4,3},{5,4},{6,5},{7,6},{8,7},{9,8},{10,9},{11,1... | collective-permute-start | bytes 884744 | tf_op jit(solution)/shard_map/ppermute | solution.py:349

commit v2 on v1

--- a/solution.py
+++ b/solution.py
@@ -12,6 +12,8 @@
 BF16 = jnp.bfloat16
 ROWS = 16
 GROUPS = 24
+BLOCK = 8
+ORDER = (0, 2, 4, 6, 7, 5, 3, 1)
 XA, XB, XC, YA, YB, YC, WA, WB, WC, ZA, ZB, ZC, MASS, INV = range(14)
 VMEM = pl.BlockSpec(memory_space=pltpu.VMEM)
 SMEM = pl.BlockSpec(memory_space=pltpu.SMEM)
@@ -45,35 +47,30 @@
 
 def pack_kernel(q_ref, mass_ref, fx_ref, fy_ref, fz_ref, out_ref):
     def row(r, carry):
-        for tg in range(3):
-            levels = [
-                q_ref[pl.ds(tg * 1024 + lev * 16 + r, 8, stride=128), :] for lev in range(8)
-            ]
-            for dest, value in enumerate(exchange_blocks(levels)):
-                out_ref[dest, 3 * r + tg] = value
+        levels = [q_ref[pl.ds(lev * 16 + r, 24, stride=128), :] for lev in range(8)]
+        for place, value in enumerate(exchange_blocks(levels)):
+            out_ref[ORDER[place], pl.ds(3 * r, 3)] = value.reshape(3, 8, 128)
         return carry
 
-    lax.fori_loop(0, ROWS, row, 0)
+    lax.fori_loop(0, ROWS, row, 0, unroll=2)
     for field, ref in enumerate((mass_ref, fx_ref, fy_ref, fz_ref)):
-        for half in range(2):
-            levels = [ref[0, lev, 8 * half : 8 * half + 8, :] for lev in range(8)]
-            for dest, value in enumerate(exchange_blocks(levels)):
-                out_ref[dest, 48 + 2 * field + half] = value
+        levels = [ref[0, lev] for lev in range(8)]
+        for place, value in enumerate(exchange_blocks(levels)):
+            out_ref[ORDER[place], 48 + 2 * field : 50 + 2 * field] = value.reshape(2, 8, 128)
 
 
 def unpack_kernel(in_ref, out_ref):
     def row(r, carry):
-        for tg in range(3):
-            cols = [in_ref[src, 3 * r + tg] for src in range(8)]
-            for lev, value in enumerate(exchange_blocks(cols)):
-                out_ref[pl.ds(tg * 1024 + lev * 16 + r, 8, stride=128), :] = value
+        cols = [in_ref[src, pl.ds(3 * r, 3)].reshape(24, 128) for src in ORDER]
+        for lev, value in enumerate(exchange_blocks(cols)):
+            out_ref[pl.ds(lev * 16 + r, 24, stride=128), :] = value
         return carry
 
-    lax.fori_loop(0, ROWS, row, 0)
+    lax.fori_loop(0, ROWS, row, 0, unroll=2)
 
 
 def write_edges(state_ref, row_up, row_down, col_right, col_left):
-    slot = slot_of((8, 128)) >> 2
+    slot = slot_of((32, 128)) >> 2
 
     def group(g, carry):
         src = g // 3
@@ -81,22 +78,35 @@
         for rr in range(3):
             row_down[src * 9 + 3 * rr + tg] = state_ref[src, 3 * rr + tg]
             row_up[src * 9 + 3 * rr + tg] = state_ref[src, 3 * (13 + rr) + tg]
-        for block in range(4):
-            rows = [state_ref[src, 3 * (4 * block + i) + tg] for i in range(4)]
-            right = roll(rows[0], -12)
-            left = rows[0]
-            for i in range(1, 4):
-                right = jnp.where(slot == i, roll(rows[i], 4 * i - 12) if i < 3 else rows[i], right)
-                left = jnp.where(slot == i, roll(rows[i], 4 * i), left)
-            col_right[g * 4 + block] = right
-            col_left[g * 4 + block] = left
+        rows = [
+            jnp.concatenate([state_ref[src, 3 * (4 * block + i) + tg] for block in range(4)], 0)
+            for i in range(4)
+        ]
+        right, left = rows[3], rows[0]
+        for i in range(3):
+            right = jnp.where(slot == i, roll(rows[i], 4 * i - 12), right)
+            left = jnp.where(slot == i + 1, roll(rows[i + 1], 4 * i + 4), left)
+        col_right[pl.ds(g * 4, 4)] = right.reshape(4, 8, 128)
+        col_left[pl.ds(g * 4, 4)] = left.reshape(4, 8, 128)
         return carry
 
-    lax.fori_loop(0, GROUPS, group, 0)
-
-
-def edge_kernel(rec_ref, in_ref, weather_ref, row_up, row_down, col_right, col_left):
-    write_edges(in_ref, row_up, row_down, col_right, col_left)
+    lax.fori_loop(0, GROUPS, group, 0, unroll=2)
+
+
+def narrow(wide_refs, out_refs):
+    for wide, out in zip(wide_refs, out_refs):
+        out[...] = wide[...].reshape(out.shape).astype(BF16)
+
+
+def widen(in_refs, wide_refs):
+    for ref, wide in zip(in_refs, wide_refs):
+        wide[...] = ref[...].astype(F32).reshape(wide.shape)
+
+
+def edge_kernel(rec_ref, in_ref, weather_ref, *refs):
+    out_refs, edges = refs[:4], refs[4:]
+    row_up, row_down, col_right, col_left = edges
+    write_edges(in_ref, *edges)
     for s in range(STEPS):
         record = rec_ref[s]
         for k in range(8):
@@ -108,6 +118,7 @@
             col_right[96 + 2 * s + half] = in_ref[record, 48 + half]
             col_left[96 + 4 * s + half] = in_ref[record, 48 + half]
             col_left[96 + 4 * s + 2 + half] = in_ref[record, 48 + 4 + half]
+    narrow(edges, out_refs)
 
 
 def face_weights(flux, mass_low, mass_up):
@@ -174,11 +185,7 @@
 
 
 def advect(q_ref, row_lo, row_hi, col_lo, col_hi, get, out_ref, conc_ref):
-    shape = (8, 128)
-    slot, lane = slot_of(shape), lane_of(shape)
-    first, last, last_two, left_half = slot == 0, slot == 15, slot >= 14, slot < 8
-
-    def one_group(src, tg):
+    def x_difference(src, tg):
         def q_row(k):
             if k < 0:
                 return row_lo[src * 9 + 3 * (k + 3) + tg]
@@ -186,7 +193,6 @@
                 return row_hi[src * 9 + 3 * (k - ROWS) + tg]
             return q_ref[src, 3 * k + tg]
 
-        g = src * 3 + tg
         q = {k: q_row(k) for k in (-3, -2, -1, 0)}
         edges = {}
 
@@ -204,67 +210,86 @@
                 x_edge(r), x_edge(r - 1), x_edge(r + 1), q[r - 1], q[r],
             )
 
-        results = []
         below = x_flux(0)
         for r in range(ROWS):
             above = x_flux(r + 1)
-            here = q[r]
-            block, i = r // 4, r % 4
-            x = jnp.where(
-                left_half,
-                roll(col_hi[g * 4 + block], 16 - 4 * i),
-                roll(col_lo[g * 4 + block], -4 - 4 * i),
-            )
-            m1 = roll(jnp.where(last, x, here), 1)
-            m2 = roll(jnp.where(last_two, x, here), 2)
-            p1 = roll(jnp.where(first, x, here), -1)
-            edge = edge_value(m2, m1, here, p1)
-            x_m1 = roll(jnp.where(last, here, x), 1)
-            x_m2 = roll(jnp.where(last_two, here, x), 2)
-            x_p1 = roll(jnp.where(first, here, x), -1)
-            edge_x = edge_value(x_m2, x_m1, x, x_p1)
-            flux_y = face_flux(
-                [get(YA + i, r) for i in range(3)], edge,
-                roll(jnp.where(last, edge_x, edge), 1),
-                roll(jnp.where(first, edge_x, edge), -1), m1, here,
-            )
-            flux_w = face_flux(
-                [get(WA + i, r) for i in range(3)], edge_x,
-                roll(jnp.where(last, edge, edge_x), 1), roll(edge_x, -1), x_m1, x,
-            )
-            flux_y_up = roll(jnp.where(first, flux_w, flux_y), -1)
-            m1 = jnp.where(lane >= 16, roll(here, 16), 0.0)
-            m2 = jnp.where(lane >= 32, roll(here, 32), 0.0)
-            p1 = jnp.where(lane < 112, roll(here, -16), 0.0)
-            edge = edge_value(m2, m1, here, p1)
-            top = (7.0 / 12.0) * here - (1.0 / 12.0) * m1
-            top = jnp.minimum(jnp.maximum(top, jnp.minimum(here, 0.0)), jnp.maximum(here, 0.0))
-            flux_z = face_flux(
-                [get(ZA + i, r) for i in range(3)], edge, roll(edge, 16),
-                jnp.where(lane >= 112, top, roll(edge, -16)), m1, here,
-            )
-            moved = (
-                get(MASS, r) * here
-                - (above - below)
-                - (flux_y_up - flux_y)
-                - (roll(flux_z, -16) - flux_z)
-            ) * get(INV, r)
-            out_ref[src, 3 * r + tg] = moved
-            results.append(moved)
+            out_ref[src, 3 * r + tg] = get(MASS, r) * q[r] - (above - below)
             below = above
-        return results
+
+    def stack(parts):
+        return jnp.concatenate(parts, 0)
+
+    def yz_part(members, rows):
+        where = [(src, tg, r) for src, tg in members for r in rows]
+        wide = (8 * len(where), 128)
+        slot, lane = slot_of(wide), lane_of(wide)
+        first, last, last_two, left_half = slot == 0, slot == 15, slot >= 14, slot < 8
+
+        def weight(k):
+            return stack([get(k, r) for _, _, r in where])
+
+        def weights(k):
+            return [weight(k + i) for i in range(3)]
+
+        here = stack([q_ref[src, 3 * r + tg] for src, tg, r in where])
+        x = jnp.where(
+            left_half,
+            stack([roll(col_hi[(3 * src + tg) * 4 + r // 4], 16 - 4 * (r % 4)) for src, tg, r in where]),
+            stack([roll(col_lo[(3 * src + tg) * 4 + r // 4], -4 - 4 * (r % 4)) for src, tg, r in where]),
+        )
+        m1 = roll(jnp.where(last, x, here), 1)
+        m2 = roll(jnp.where(last_two, x, here), 2)
+        p1 = roll(jnp.where(first, x, here), -1)
+        x_m1 = roll(jnp.where(last, here, x), 1)
+        x_m2 = roll(jnp.where(last_two, here, x), 2)
+        x_p1 = roll(jnp.where(first, here, x), -1)
+        edge = edge_value(m2, m1, here, p1)
+        edge_x = edge_value(x_m2, x_m1, x, x_p1)
+        flux_y = face_flux(
+            weights(YA), edge,
+            roll(jnp.where(last, edge_x, edge), 1),
+            roll(jnp.where(first, edge_x, edge), -1), m1, here,
+        )
+        flux_w = face_flux(
+            weights(WA), edge_x,
+            roll(jnp.where(last, edge, edge_x), 1), roll(edge_x, -1), x_m1, x,
+        )
+        total = roll(jnp.where(first, flux_w, flux_y), -1) - flux_y
+        m1 = jnp.where(lane >= 16, roll(here, 16), 0.0)
+        m2 = jnp.where(lane >= 32, roll(here, 32), 0.0)
+        p1 = jnp.where(lane < 112, roll(here, -16), 0.0)
+        edge = edge_value(m2, m1, here, p1)
+        top = (7.0 / 12.0) * here - (1.0 / 12.0) * m1
+        top = jnp.minimum(jnp.maximum(top, jnp.minimum(here, 0.0)), jnp.maximum(here, 0.0))
+        flux_z = face_flux(
+            weights(ZA), edge, roll(edge, 16),
+            jnp.where(lane >= 112, top, roll(edge, -16)), m1, here,
+        )
+        total = total + (roll(flux_z, -16) - flux_z)
+        partial = stack([out_ref[src, 3 * r + tg] for src, tg, r in where])
+        moved = (partial - total) * weight(INV)
+        result = []
+        for n, (src, tg, r) in enumerate(where):
+            result.append(moved[8 * n : 8 * n + 8])
+            out_ref[src, 3 * r + tg] = result[-1]
+        return result
 
     def pair(p, carry):
-        parts = []
+        members = []
         for k in range(2):
             g = 2 * p + k
             src = g // 3
-            parts.append(one_group(src, g - 3 * src))
+            members.append((src, g - 3 * src))
+        for src, tg in members:
+            x_difference(src, tg)
         start = pl.multiple_of(16 * p, 16)
-        for r in range(ROWS):
-            conc_ref[pl.ds(start, 16), 128 * r : 128 * r + 128] = jnp.concatenate(
-                [parts[0][r], parts[1][r]], 0
-            ).astype(BF16)
+        for block in range(ROWS // BLOCK):
+            rows = range(BLOCK * block, BLOCK * block + BLOCK)
+            parts = yz_part(members, rows)
+            for i, r in enumerate(rows):
+                conc_ref[pl.ds(start, 16), 128 * r : 128 * r + 128] = jnp.concatenate(
+                    [parts[i], parts[BLOCK + i]], 0
+                ).astype(BF16)
         return carry
 
     lax.fori_loop(0, GROUPS // 2, pair, 0)
@@ -294,31 +319,38 @@
 
 
 def first_kernel(
-    place_ref, q_ref, weather_ref, row_lo, row_hi, col_lo, col_hi, sel_ref, net_ref, coeff_ref,
-    out_ref, later_ref, row_up, row_down, col_right, col_left, now_ref, ext_ref, conc_ref, rate_ref,
+    place_ref, q_ref, weather_ref, lo_ref, hi_ref, left_ref, right_ref, sel_ref, net_ref, coeff_ref,
+    out_ref, later_ref, up_out, down_out, right_out, left_out,
+    now_ref, ext_ref, conc_ref, rate_ref, row_lo, row_hi, col_lo, col_hi,
 ):
+    halos = (row_lo, row_hi, col_lo, col_hi)
+    widen((lo_ref, hi_ref, left_ref, right_ref), halos)
     for s, ref in enumerate((now_ref, later_ref)):
         def put(k, rows, value, ref=ref):
             ref[k, 0:rows] = value
 
-        write_weights(s, place_ref, weather_ref, row_lo, row_hi, col_lo, col_hi, ext_ref, put)
+        write_weights(s, place_ref, weather_ref, *halos, ext_ref, put)
 
     def get(k, r):
         return now_ref[k, pl.ds(r, 8, stride=0), :]
 
-    advect(q_ref, row_lo, row_hi, col_lo, col_hi, get, out_ref, conc_ref)
+    advect(q_ref, *halos, get, out_ref, conc_ref)
     react(conc_ref, sel_ref, net_ref, coeff_ref, rate_ref, out_ref)
-    write_edges(out_ref, row_up, row_down, col_right, col_left)
+    edges = (row_lo.at[0:72], row_hi.at[0:72], col_lo.at[0:96], col_hi.at[0:96])
+    write_edges(out_ref, *edges)
+    narrow(edges, (up_out, down_out, right_out, left_out))
 
 
 def second_kernel(
-    now_ref, q_ref, row_lo, row_hi, col_lo, col_hi, sel_ref, net_ref, coeff_ref,
-    out_ref, conc_ref, rate_ref,
+    now_ref, q_ref, lo_ref, hi_ref, left_ref, right_ref, sel_ref, net_ref, coeff_ref,
+    out_ref, conc_ref, rate_ref, *halos,
 ):
+    widen((lo_ref, hi_ref, left_ref, right_ref), halos)
+
     def get(k, r):
         return now_ref[k, pl.ds(r, 8, stride=0), :]
 
-    advect(q_ref, row_lo, row_hi, col_lo, col_hi, get, out_ref, conc_ref)
+    advect(q_ref, *halos, get, out_ref, conc_ref)
     react(conc_ref, sel_ref, net_ref, coeff_ref, rate_ref, out_ref)
 
 
@@ -343,16 +375,17 @@
 
 
 def halo(row_up, row_down, col_right, col_left):
-    def shift(x, axis, step):
-        count = lax.axis_size(axis)
-        pairs = [(i, i + step) for i in range(count) if 0 <= i + step < count]
-        return lax.ppermute(x, axis, pairs)
+    tiles = [(i, i + 1) for i in range(lax.axis_size("tile") - 1)]
+    columns = list(zip(ORDER[:-1], ORDER[1:]))
+
+    def back(pairs):
+        return [(target, source) for source, target in pairs]
 
     return (
-        shift(row_up, "tile", 1),
-        shift(row_down, "tile", -1),
-        shift(col_right, "tracer", 1),
-        shift(col_left, "tracer", -1),
+        lax.ppermute(row_up, "tile", tiles),
+        lax.ppermute(row_down, "tile", back(tiles)),
+        lax.ppermute(col_right, "tracer", columns),
+        lax.ppermute(col_left, "tracer", back(columns)),
     )
 
 
@@ -378,29 +411,34 @@
         args=(tracers.reshape(-1, 128), air_mass, flux_x, flux_y, flux_z),
     )
     state = swap(sent)
+    def narrow_blocks(*counts):
+        return [jax.ShapeDtypeStruct((8 * count, 128), BF16) for count in counts]
+
+    def wide_blocks(*counts):
+        return [pltpu.VMEM((count, 8, 128), F32) for count in counts]
+
+    first, plain = (74, 76, 100, 104), (72, 72, 96, 96)
     weather, *edges = call(
         edge_kernel,
-        [blocks(STEPS, 8), blocks(74), blocks(76), blocks(100), blocks(104)],
+        [blocks(STEPS, 8)] + narrow_blocks(*first),
         [SMEM, VMEM],
-        args=(record_of_step, state),
+        wide_blocks(*first),
+        (record_of_step, state),
     )
     scratch = [pltpu.VMEM((species, 128 * ROWS), BF16), pltpu.VMEM((reactions, 256), BF16)]
     weights = (14, 24, 128)
     state, later, *edges = call(
         first_kernel,
-        [
-            blocks(8, 48), jax.ShapeDtypeStruct(weights, F32),
-            blocks(72), blocks(72), blocks(96), blocks(96),
-        ],
+        [blocks(8, 48), jax.ShapeDtypeStruct(weights, F32)] + narrow_blocks(*plain),
         [SMEM] + [VMEM] * 9,
-        [pltpu.VMEM(weights, F32), pltpu.VMEM((2, 32, 128), F32)] + scratch,
+        [pltpu.VMEM(weights, F32), pltpu.VMEM((2, 32, 128), F32)] + scratch + wide_blocks(*first),
         (place, state, weather) + halo(*edges) + (selector, net, coeff),
     )
     state = call(
         second_kernel,
         blocks(8, 48),
         [VMEM] * 9,
-        scratch,
+        scratch + wide_blocks(*plain),
         (later, state) + halo(*edges) + (selector, net, coeff),
     )
     out = call(

time: 314 us -> 152 us (0.48)
  Pallas kernels: 188 us -> 49.6 us
  waiting for transfers between devices: 53.9 us -> 35.9 us
  starting transfers between devices: 32.7 us -> 27.7 us
  blocking collectives: 26.9 us -> 31.1 us
    pallas_call x5, Pallas kernels: 188 us -> 49.6 us  [call(): pl.pallas_call(kernel, out_shape=outs, in_specs=specs, out_specs=VMEM if...]
    ppermute x8, waiting for transfers between devices: 26.8 us -> 8.88 us  [the longest x2 4.5 us: halo(): lax.ppermute(col_left, 'tracer', back(columns))]
    ppermute x8, starting transfers between devices: 24.9 us -> 20 us  [the longest x2 9.08 us: halo(): lax.ppermute(row_down, 'tile', back(tiles))]
    all_to_all x1, blocking collectives: 26.9 us -> 31.1 us  [swap(): return lax.all_to_all(x, 'tracer', split_axis=0, concat_axis=0, tiled=True)]
    unnamed x22 -> x20, local copies, waits for them, and re-layouts: 7.46 us -> 6.04 us
  transfers between devices with their start and end apart: 9 -> 9, of which waited for: 7 -> 5; matrix products, arithmetic and copies ran while one was open for 0% -> 0% of each run, Pallas kernels for 0% -> 0%
where the time goes in v2:
time: 152 us; the launch traced here: 151 us
  Pallas kernels  49.6 us (33%)
  waiting for transfers between devices  35.9 us (24%)
  blocking collectives  31.1 us (20%)
  starting transfers between devices  27.7 us (18%)
  local copies, waits for them, and re-layouts  6.18 us (4%)
    pallas_call x5, Pallas kernels, call(): pl.pallas_call(kernel, out_shape=outs, in_specs=specs, out_specs=VMEM if...  49.6 us
    all_to_all x1, blocking collectives, swap(): return lax.all_to_all(x, 'tracer', split_axis=0, concat_axis=0, tiled=True)  31.1 us
    all_to_all x1, waiting for transfers between devices, swap(): return lax.all_to_all(x, 'tracer', split_axis=0, concat_axis=0, tiled=True)  27 us
    ppermute x2, starting transfers between devices, halo(): lax.ppermute(row_down, 'tile', back(tiles))  9.08 us
    all_to_all x1, starting transfers between devices, swap(): return lax.all_to_all(x, 'tracer', split_axis=0, concat_axis=0, tiled=True)  7.74 us
    unnamed x20, local copies, waits for them, and re-layouts  6.04 us
    ppermute x2, waiting for transfers between devices, halo(): lax.ppermute(col_left, 'tracer', back(columns))  4.5 us
    ppermute x2, starting transfers between devices, halo(): lax.ppermute(col_right, 'tracer', columns)  4.47 us
  transfers between devices with their start and end apart: 9, of which 5 were waited for; matrix products, arithmetic and copies ran while one was open for 0% of the time, Pallas kernels for 0%

profile of v2, /device:TPU:16, one launch (start us, length us, event | category | flops | bytes accessed | tf_op | source)
XLA Modules:
  0.0 151.1 jit_solution(17550365035206972414)
XLA Ops:
  0.0 1.4 copy-done.1
  1.4 0.8 copy-done.2
  2.3 0.8 copy-done.3
  4.8 3.0 %shard_map.91 = f32[8,56,8,128]{3,2,1,0:T(8,128)S(1)} custom-call(f32[3072,128]{1,0:T(8,128)S(1)} %bitcast.15, f32[1,8,16,128]{3,2,1,0:T(8,128)S(1)} %copy-done.2, f32[1,8,16,128]{3,2,1,0:T(8,128)S(1)} %copy-done.3, f32[1,8,16,128]{3,2,1,0:T(8,128)S(1)} %copy-done.4, f32[1,8,16,128]{3,2,1,0:T(8,128)S(1)} %copy-done.5), custom_call_target="tpu_custom_call" | custom-call | tf_op jit(solution)/shard_map/pallas_call | solution.py:363
  7.8 1.3 copy-done
  9.1 7.7 %all-to-all-start = ((f32[8,56,8,128]{3,2,1,0:T(8,128)}), f32[8,56,8,128]{3,2,1,0:T(8,128)S(1)}, u32[]{:S(2)}, u32[]{:S(2)}) async-start(f32[8,56,8,128]{3,2,1,0:T(8,128)} %copy-done), calls=%async_computation | async-start | bytes 3670016 | tf_op jit(solution)/shard_map/all_to_all | solution.py:374
  17.2 27.0 %all-to-all-done.in_ref.q_ref = f32[8,56,8,128]{3,2,1,0:T(8,128)S(1)} async-done(((f32[8,56,8,128]{3,2,1,0:T(8,128)}), f32[8,56,8,128]{3,2,1,0:T(8,128)S(1)}, u32[]{:S(2)}, u32[]{:S(2)}) %all-to-all-start) | async-done | bytes 1835040 | tf_op jit(solution)/shard_map/all_to_all | solution.py:374
  44.2 2.1 %shard_map.92 = (f32[2,8,8,128]{3,2,1,0:T(8,128)S(1)}, bf16[592,128]{1,0:T(8,128)(2,1)S(1)}, bf16[608,128]{1,0:T(8,128)(2,1)S(1)}, bf16[800,128]{1,0:T(8,128)(2,1)S(1)}, bf16[832,128]{1,0:T(8,128)(2,1)S(1)}) custom-call(s32[2]{0:T(128)S(1)} %copy-done.6, f32[8,56,8,128]{3,2,1,0:T(8,128)S(1)} %all-to-all-done.in_ref.q_ref), custom_call_target="tpu_custom_call" | custom-call | tf_op jit(solution)/shard_map/pallas_call | solution.py:363
  46.4 1.9 %collective-permute-start = (bf16[592,128]{1,0:T(8,128)(2,1)S(1)}, bf16[592,128]{1,0:T(8,128)(2,1)S(1)}, u32[]{:S(2)}, u32[]{:S(2)}) collective-permute-start(bf16[592,128]{1,0:T(8,128)(2,1)S(1)} %get-tuple-element.17), channel_id=1, source_target_pairs={{0,1},{1,2},{2,3},{3,4},{4,5},{5,6},{6,7},{7,8},{8,9},{9,10},{10,1... | collective-permute-start | bytes 454664 | tf_op jit(solution)/shard_map/ppermute | solution.py:385
  48.3 4.5 %collective-permute-start.1 = (bf16[608,128]{1,0:T(8,128)(2,1)S(1)}, bf16[608,128]{1,0:T(8,128)(2,1)S(1)}, u32[]{:S(2)}, u32[]{:S(2)}) collective-permute-start(bf16[608,128]{1,0:T(8,128)(2,1)S(1)} %get-tuple-element.18), channel_id=1, source_target_pairs={{1,0},{2,1},{3,2},{4,3},{5,4},{6,5},{7,6},{8,7},{9,8},{10,9},{11,1... | collective-permute-start | bytes 466952 | tf_op jit(solution)/shard_map/ppermute | solution.py:386
  52.8 1.5 collective-permute-start.2
  54.3 1.3 collective-permute-start.3
  55.9 1.7 %collective-permute-done.2.left_ref = bf16[800,128]{1,0:T(8,128)(2,1)S(1)} collective-permute-done((bf16[800,128]{1,0:T(8,128)(2,1)S(1)}, bf16[800,128]{1,0:T(8,128)(2,1)S(1)}, u32[]{:S(2)}, u32[]{:S(2)}) %collective-permute-start.2) | collective-permute-done | bytes 204832 | tf_op jit(solution)/shard_map/ppermute | solution.py:387
  57.6 4.5 %collective-permute-done.3.right_ref = bf16[832,128]{1,0:T(8,128)(2,1)S(1)} collective-permute-done((bf16[832,128]{1,0:T(8,128)(2,1)S(1)}, bf16[832,128]{1,0:T(8,128)(2,1)S(1)}, u32[]{:S(2)}, u32[]{:S(2)}) %collective-permute-start.3) | collective-permute-done | bytes 213024 | tf_op jit(solution)/shard_map/ppermute | solution.py:388
  62.2 21.2 %shard_map.93 = (f32[8,48,8,128]{3,2,1,0:T(8,128)S(1)}, f32[14,24,128]{2,1,0:T(8,128)S(1)}, bf16[576,128]{1,0:T(8,128)(2,1)S(1)}, bf16[576,128]{1,0:T(8,128)(2,1...) custom-call(s32[2]{0:T(128)S(1)} %pad_add_fusion.place_ref, ...), custom_call_target="tpu_custom_call" | custom-call | tf_op jit(solution)/shard_map/pallas_call | solution.py:363
  83.4 3.0 %collective-permute-start.6 = (bf16[768,128]{1,0:T(8,128)(2,1)S(1)}, bf16[768,128]{1,0:T(8,128)(2,1)S(1)}, u32[]{:S(2)}, u32[]{:S(2)}) collective-permute-start(bf16[768,128]{1,0:T(8,128)(2,1)S(1)} %get-tuple-element.25), channel_id=1, source_target_pairs={{0,32},{32,64},{64,96},{96,112},{112,80},{80,48},{48,16},{1,33},{3... | collective-permute-start | bytes 589832 | tf_op jit(solution)/shard_map/ppermute | solution.py:387
  86.4 1.3 collective-permute-start.7
  87.7 1.9 %collective-permute-start.4 = (bf16[576,128]{1,0:T(8,128)(2,1)S(1)}, bf16[576,128]{1,0:T(8,128)(2,1)S(1)}, u32[]{:S(2)}, u32[]{:S(2)}) collective-permute-start(bf16[576,128]{1,0:T(8,128)(2,1)S(1)} %get-tuple-element.23), channel_id=1, source_target_pairs={{0,1},{1,2},{2,3},{3,4},{4,5},{5,6},{6,7},{7,8},{8,9},{9,10},{10,1... | collective-permute-start | bytes 442376 | tf_op jit(solution)/shard_map/ppermute | solution.py:385
  89.6 4.5 %collective-permute-start.5 = (bf16[576,128]{1,0:T(8,128)(2,1)S(1)}, bf16[576,128]{1,0:T(8,128)(2,1)S(1)}, u32[]{:S(2)}, u32[]{:S(2)}) collective-permute-start(bf16[576,128]{1,0:T(8,128)(2,1)S(1)} %get-tuple-element.24), channel_id=1, source_target_pairs={{1,0},{2,1},{3,2},{4,3},{5,4},{6,5},{7,6},{8,7},{9,8},{10,9},{11,1... | collective-permute-start | bytes 442376 | tf_op jit(solution)/shard_map/ppermute | solution.py:386
  94.2 0.9 collective-permute-done.4.lo_ref
  95.0 1.8 %collective-permute-done.5.hi_ref = bf16[576,128]{1,0:T(8,128)(2,1)S(1)} collective-permute-done((bf16[576,128]{1,0:T(8,128)(2,1)S(1)}, bf16[576,128]{1,0:T(8,128)(2,1)S(1)}, u32[]{:S(2)}, u32[]{:S(2)}) %collective-permute-start.5) | collective-permute-done | bytes 147488 | tf_op jit(solution)/shard_map/ppermute | solution.py:386
  96.8 19.0 %shard_map.94 = f32[8,48,8,128]{3,2,1,0:T(8,128)S(1)} custom-call(f32[14,24,128]{2,1,0:T(8,128)S(1)} %get-tuple-element.21.now_ref, f32[8,48,8,128]{3,2,1,0:T(8,128)S(1)} %get-tuple-element.22.q_ref, bf16[576,128]{1,0:T(8,128)(2,1)S(1)} %collective-permute-done.4.lo_ref, bf16[576,128]{1,0:T(8,128)(2,1)S(1)} %collective-permute-done.5.hi_ref, ...), custom_call_target="tpu_custom_call" | custom-call | tf_op jit(solution)/shard_map/pallas_call | solution.py:363
  115.8 31.1 %all_to_all.10.in_ref = f32[8,48,8,128]{3,2,1,0:T(8,128)S(1)} all-to-all(f32[8,48,8,128]{3,2,1,0:T(8,128)S(1)} %shard_map.94), channel_id=1, replica_groups=mesh['tracer'=8,'tile'=16] {'tracer'}, dimensions={0} | all-to-all | bytes 3145728 | tf_op jit(solution)/shard_map/all_to_all | solution.py:374
  146.9 4.3 %shard_map.95 = f32[3072,128]{1,0:T(8,128)} custom-call(f32[8,48,8,128]{3,2,1,0:T(8,128)S(1)} %all_to_all.10.in_ref), custom_call_target="tpu_custom_call" | custom-call | tf_op jit(solution)/shard_map/pallas_call | solution.py:363
  (27 shorter events, 2.4 us)
Async XLA Ops:
  0.0 1.4 copy-start.1
  1.4 0.8 copy-start.2
  2.2 0.8 copy-start.3
  3.1 0.8 copy-start.4
  3.9 0.8 copy-start.5
  7.8 1.3 copy-start
  9.1 7.8 %copy-start.8 = (s32[512,2]{0,1:T(2,128)S(1)}, s32[512,2]{0,1:T(2,128)}, u32[]{:S(2)}) copy-start(s32[512,2]{0,1:T(2,128)} %param.14) | copy-start | bytes 12292
  9.1 8.0 %copy-start.7 = (s32[512,192]{0,1:T(8,128)S(1)}, s32[512,192]{0,1:T(8,128)}, u32[]{:S(2)}) copy-start(s32[512,192]{0,1:T(8,128)} %param.15) | copy-start | bytes 1179652
  9.1 35.1 %copy-start.6 = (s32[2]{0:T(128)S(1)}, s32[2]{0:T(128)}, u32[]{:S(2)}) copy-start(s32[2]{0:T(128)} %rec_ref.1) | copy-start | bytes 28
  9.1 35.1 %all-to-all-start = ((f32[8,56,8,128]{3,2,1,0:T(8,128)}), f32[8,56,8,128]{3,2,1,0:T(8,128)S(1)}, u32[]{:S(2)}, u32[]{:S(2)}) async-start(f32[8,56,8,128]{3,2,1,0:T(8,128)} %copy-done), calls=%async_computation | async-start | bytes 3670016 | tf_op jit(solution)/shard_map/all_to_all | solution.py:374
  17.1 45.0 %copy-start.9 = (f32[512]{0:T(512)S(1)}, f32[512]{0:T(512)}, u32[]{:S(2)}) copy-start(f32[512]{0:T(512)} %param.16) | copy-start | bytes 6148
  46.4 9.5 %collective-permute-start = (bf16[592,128]{1,0:T(8,128)(2,1)S(1)}, bf16[592,128]{1,0:T(8,128)(2,1)S(1)}, u32[]{:S(2)}, u32[]{:S(2)}) collective-permute-start(bf16[592,128]{1,0:T(8,128)(2,1)S(1)} %get-tuple-element.17), channel_id=1, source_target_pairs={{0,1},{1,2},{2,3},{3,4},{4,5},{5,6},{6,7},{7,8},{8,9},{9,10},{10,1... | collective-permute-start | bytes 454664 | tf_op jit(solution)/shard_map/ppermute | solution.py:385
  48.3 7.6 %collective-permute-start.1 = (bf16[608,128]{1,0:T(8,128)(2,1)S(1)}, bf16[608,128]{1,0:T(8,128)(2,1)S(1)}, u32[]{:S(2)}, u32[]{:S(2)}) collective-permute-start(bf16[608,128]{1,0:T(8,128)(2,1)S(1)} %get-tuple-element.18), channel_id=1, source_target_pairs={{1,0},{2,1},{3,2},{4,3},{5,4},{6,5},{7,6},{8,7},{9,8},{10,9},{11,1... | collective-permute-start | bytes 466952 | tf_op jit(solution)/shard_map/ppermute | solution.py:386
  52.8 4.7 %collective-permute-start.2 = (bf16[800,128]{1,0:T(8,128)(2,1)S(1)}, bf16[800,128]{1,0:T(8,128)(2,1)S(1)}, u32[]{:S(2)}, u32[]{:S(2)}) collective-permute-start(bf16[800,128]{1,0:T(8,128)(2,1)S(1)} %get-tuple-element.19), channel_id=1, source_target_pairs={{0,32},{32,64},{64,96},{96,112},{112,80},{80,48},{48,16},{1,33},{3... | collective-permute-start | bytes 614408 | tf_op jit(solution)/shard_map/ppermute | solution.py:387
  54.3 7.7 %collective-permute-start.3 = (bf16[832,128]{1,0:T(8,128)(2,1)S(1)}, bf16[832,128]{1,0:T(8,128)(2,1)S(1)}, u32[]{:S(2)}, u32[]{:S(2)}) collective-permute-start(bf16[832,128]{1,0:T(8,128)(2,1)S(1)} %get-tuple-element.20), channel_id=1, source_target_pairs={{32,0},{64,32},{96,64},{112,96},{80,112},{48,80},{16,48},{33,1},{6... | collective-permute-start | bytes 638984 | tf_op jit(solution)/shard_map/ppermute | solution.py:388
  83.4 13.4 %collective-permute-start.6 = (bf16[768,128]{1,0:T(8,128)(2,1)S(1)}, bf16[768,128]{1,0:T(8,128)(2,1)S(1)}, u32[]{:S(2)}, u32[]{:S(2)}) collective-permute-start(bf16[768,128]{1,0:T(8,128)(2,1)S(1)} %get-tuple-element.25), channel_id=1, source_target_pairs={{0,32},{32,64},{64,96},{96,112},{112,80},{80,48},{48,16},{1,33},{3... | collective-permute-start | bytes 589832 | tf_op jit(solution)/shard_map/ppermute | solution.py:387
  86.4 10.4 %collective-permute-start.7 = (bf16[768,128]{1,0:T(8,128)(2,1)S(1)}, bf16[768,128]{1,0:T(8,128)(2,1)S(1)}, u32[]{:S(2)}, u32[]{:S(2)}) collective-permute-start(bf16[768,128]{1,0:T(8,128)(2,1)S(1)} %get-tuple-element.26), channel_id=1, source_target_pairs={{32,0},{64,32},{96,64},{112,96},{80,112},{48,80},{16,48},{33,1},{6... | collective-permute-start | bytes 589832 | tf_op jit(solution)/shard_map/ppermute | solution.py:388
  87.7 7.4 %collective-permute-start.4 = (bf16[576,128]{1,0:T(8,128)(2,1)S(1)}, bf16[576,128]{1,0:T(8,128)(2,1)S(1)}, u32[]{:S(2)}, u32[]{:S(2)}) collective-permute-start(bf16[576,128]{1,0:T(8,128)(2,1)S(1)} %get-tuple-element.23), channel_id=1, source_target_pairs={{0,1},{1,2},{2,3},{3,4},{4,5},{5,6},{6,7},{7,8},{8,9},{9,10},{10,1... | collective-permute-start | bytes 442376 | tf_op jit(solution)/shard_map/ppermute | solution.py:385
  89.6 7.2 %collective-permute-start.5 = (bf16[576,128]{1,0:T(8,128)(2,1)S(1)}, bf16[576,128]{1,0:T(8,128)(2,1)S(1)}, u32[]{:S(2)}, u32[]{:S(2)}) collective-permute-start(bf16[576,128]{1,0:T(8,128)(2,1)S(1)} %get-tuple-element.24), channel_id=1, source_target_pairs={{1,0},{2,1},{3,2},{4,3},{5,4},{6,5},{7,6},{8,7},{9,8},{10,9},{11,1... | collective-permute-start | bytes 442376 | tf_op jit(solution)/shard_map/ppermute | solution.py:386

commit v3 on v2

v3 whole, which is shorter than its diff:
```python
import jax
import jax.numpy as jnp
from jax import lax
from jax.experimental import pallas as pl
from jax.experimental.pallas import tpu as pltpu
from jax.sharding import PartitionSpec as P

STEPS = 2
F32 = jnp.float32
BF16 = jnp.bfloat16
ROWS = 16
COLS = 16
LANES = 256
ORDER = (0, 2, 4, 6, 7, 5, 3, 1)
XA, YA, ZA, MASS, INV, WA = 0, 3, 6, 9, 10, 11
VMEM = pl.BlockSpec(memory_space=pltpu.VMEM)
SMEM = pl.BlockSpec(memory_space=pltpu.SMEM)


def roll(x, shift):
    return pltpu.roll(x, shift % 128, axis=1)


def lane_of(shape):
    return lax.broadcasted_iota(jnp.int32, shape, 1)


def exchange_blocks(vectors):
    block = lane_of(vectors[0].shape) >> 4
    out = list(vectors)
    for bit in (1, 2, 4):
        low = (block & bit) == 0
        for i in range(8):
            if i & bit:
                continue
            first, second = out[i], out[i | bit]
            out[i] = jnp.where(low, first, roll(second, 16 * bit))
            out[i | bit] = jnp.where(low, roll(first, -16 * bit), second)
    return out


def pack_kernel(q_ref, mass_ref, fx_ref, fy_ref, fz_ref, out_ref):
    def row(r, carry):
        levels = [q_ref[pl.ds(lev * 16 + r, 24, stride=128), :] for lev in range(8)]
        for place, value in enumerate(exchange_blocks(levels)):
            out_ref[ORDER[place], pl.ds(3 * r, 3)] = value.reshape(3, 8, 128)
        return carry

    lax.fori_loop(0, ROWS, row, 0, unroll=2)
    for field, ref in enumerate((mass_ref, fx_ref, fy_ref, fz_ref)):
        for half in range(2):
            rows = [ref[pl.ds(8 * half + r, 8, stride=16), :] for r in range(8)]
            for place, value in enumerate(exchange_blocks(rows)):
                out_ref[ORDER[place], 48 + 2 * field + half] = value


def unpack_kernel(in_ref, out_ref):
    def row(r, carry):
        cols = [in_ref[src, pl.ds(3 * r, 3)].reshape(24, 128) for src in ORDER]
        for lev, value in enumerate(exchange_blocks(cols)):
            out_ref[pl.ds(lev * 16 + r, 24, stride=128), :] = value
        return carry

    lax.fori_loop(0, ROWS, row, 0, unroll=2)


def cell(c):
    return pl.ds(8 * (c + 3), 8)


def write_edges(state_ref, row_up, row_down, col_right, col_left):
    inner = pl.ds(24, 128)
    for k in range(3):
        row_up[128 * k : 128 * k + 128] = state_ref[16 + k, inner].astype(BF16)
        row_down[128 * k : 128 * k + 128] = state_ref[3 + k, inner].astype(BF16)
    for pair in range(ROWS // 2):
        for out, start in ((col_right, 128), (col_left, 24)):
            both = [state_ref[3 + 2 * pair + i, pl.ds(start, 24)] for i in range(2)]
            out[48 * pair : 48 * pair + 48] = jnp.concatenate(both, 0).astype(BF16)


def read_edges(state_ref, row_lo, row_hi, col_lo, col_hi):
    inner = pl.ds(24, 128)
    for k in range(3):
        state_ref[k, inner] = row_lo[128 * k : 128 * k + 128].astype(F32)
        state_ref[19 + k, inner] = row_hi[128 * k : 128 * k + 128].astype(F32)
    for pair in range(ROWS // 2):
        for ref, start in ((col_lo, 0), (col_hi, 152)):
            both = ref[48 * pair : 48 * pair + 48].astype(F32)
            for i in range(2):
                state_ref[3 + 2 * pair + i, pl.ds(start, 24)] = both[24 * i : 24 * i + 24]


def arrange_kernel(
    rec_ref, in_ref, state_ref, weather_ref, row_up, row_down, col_right, col_left, turn_ref
):
    def row(r, carry):
        parts = [in_ref[src, pl.ds(3 * r, 3)].reshape(24, 128) for src in range(8)]
        parts.append(jnp.zeros((LANES - 192, 128), F32))
        stacked = jnp.concatenate(parts, 0)
        for half in range(2):
            turned = stacked[128 * half : 128 * half + 128].T
            for i in range(16):
                start = 128 * (2 * (r & 1) + half) + 64 * (i % 2) + i // 2
                turn_ref[pl.ds(start, 8, stride=8), :] = turned[8 * i : 8 * i + 8]
            whole = turn_ref[pl.ds(pl.multiple_of(128 * (2 * (r & 1) + half), 128), 128), :]
            state_ref[r + 3, pl.ds(24, 128), 128 * half : 128 * half + 128] = whole
        return carry

    lax.fori_loop(0, ROWS, row, 0, unroll=2)
    write_edges(state_ref, row_up, row_down, col_right, col_left)

    def lanes(*blocks):
        return jnp.concatenate(blocks, 1)

    ups, downs, rights, lefts = [], [], [], []
    zero = jnp.zeros((8, 128), F32)
    for s in range(STEPS):
        record = rec_ref[s]
        got = [in_ref[record, 48 + k] for k in range(8)]
        for k in range(8):
            weather_ref[s, k] = got[k]
        ups.append(lanes(got[1], zero))
        downs.append(lanes(got[0], got[2]))
        rights.append(lanes(got[0], got[1]))
        lefts += [lanes(got[0], got[1]), lanes(got[4], got[5])]
    row_up[384:400] = jnp.concatenate(ups, 0).astype(BF16)
    row_down[384:400] = jnp.concatenate(downs, 0).astype(BF16)
    col_right[384:400] = jnp.concatenate(rights, 0).astype(BF16)
    col_left[384:416] = jnp.concatenate(lefts, 0).astype(BF16)


def face_weights(flux, mass_low, mass_up):
    upwind = jnp.where(flux > 0, mass_low, mass_up)
    c = jnp.abs(flux) / jnp.maximum(upwind, 0.5)
    side = flux * c
    return [flux * (1.0 - c) * (1.0 - c), side * (c - 1.0), side * (3.0 - 2.0 * c)]


def write_weights(s, place_ref, weather_ref, row_lo, row_hi, col_lo, col_hi, out_ref):
    tile, column = place_ref[0], place_ref[1]
    shape = (8, 128)
    lane = lane_of(shape)
    slot, group = lane & 15, lane >> 4
    level = lax.broadcasted_iota(jnp.int32, shape, 0)
    zero = jnp.zeros(shape, F32)

    def edge(ref, start, s):
        both = ref[384 + start : 400 + start].astype(F32)[8 * s : 8 * s + 8]
        return both[:, 0:128], both[:, 128:256]

    mass = [weather_ref[s, 0], weather_ref[s, 1]]
    east = [weather_ref[s, 2], weather_ref[s, 3]]
    south = [weather_ref[s, 4], weather_ref[s, 5]]
    bottom = [weather_ref[s, 6], weather_ref[s, 7]]
    mass_before, _ = edge(row_lo, 0, s)
    mass_after, east_after = edge(row_hi, 0, s)
    mass_left = edge(col_lo, 0, s)
    lefts = col_hi[384:416].astype(F32)[16 * s : 16 * s + 16]
    mass_right = [lefts[0:8, 128 * h : 128 * h + 128] for h in range(2)]
    south_right = [lefts[8:16, 128 * h : 128 * h + 128] for h in range(2)]
    east[0] = jnp.where((group == 0) & (tile == 0), 0.0, east[0])
    mass_rows = [mass_before] + mass + [mass_after]
    east_rows = east + [east_after]
    for h in range(2):
        here = mass[h]
        south_h = jnp.where((slot == 0) & (column == 0), 0.0, south[h])
        bottom_h = jnp.where(level == 0, 0.0, bottom[h])
        before = jnp.where(group == 0, roll(mass_rows[h], 16), roll(here, 16))
        east_up = jnp.where(group == 7, roll(east_rows[h + 1], -16), roll(east[h], -16))
        left = jnp.where(slot == 0, roll(mass_left[h], -15), roll(here, 1))
        south_up = jnp.where(slot == 15, roll(south_right[h], 15), roll(south_h, -1))
        below = jnp.concatenate([here[0:1], here[0:7]], 0)
        bottom_up = jnp.concatenate([bottom_h[1:8], zero[0:1]], 0)
        new_mass = here - (east_up - east[h]) - (south_up - south_h) - (bottom_up - bottom_h)
        fields = (
            face_weights(east[h], before, here)
            + face_weights(south_h, left, here)
            + face_weights(bottom_h, below, here)
            + [here, 1.0 / new_mass]
            + face_weights(south_right[h], roll(here, -15), mass_right[h])
            + [zero, zero]
        )
        for part in range(2):
            for r, value in enumerate(exchange_blocks(fields[8 * part : 8 * part + 8])):
                out_ref[8 * h + r, part] = value
    last = face_weights(east_after, roll(mass[1], 16), mass_after)
    out_ref[16, 0] = exchange_blocks(last + [zero] * 5)[0]


def edge_value(low2, low1, up1, up2):
    value = (7.0 / 12.0) * (low1 + up1) - (1.0 / 12.0) * (low2 + up2)
    return jnp.minimum(
        jnp.maximum(value, jnp.minimum(low1, up1)), jnp.maximum(low1, up1)
    )


def face_flux(weights, edge, below, above, q_low, q_up):
    a, b, c = weights
    forward = c > 0
    return a * edge + b * jnp.where(forward, below, above) + c * jnp.where(forward, q_low, q_up)


def advect(state, weight_ref, x_edges, x_flux, z_q, z_edge, z_flux):
    def pick(ref_value, field, c):
        lane = 16 * (field % 8) + c
        return jnp.broadcast_to(ref_value[:, lane : lane + 1], (8, LANES))

    zero = jnp.zeros((16 * COLS + 16, LANES), F32)
    z_q[...] = zero
    z_edge[...] = zero
    z_flux[...] = zero
    first = weight_ref[0, 0]
    for c in range(COLS):
        q = [state[k, cell(c)] for k in range(6)]
        edges = [edge_value(*q[k : k + 4]) for k in range(3)]
        for k in range(3):
            x_edges[k, c] = edges[k]
        weights = [pick(first, XA + i, c) for i in range(3)]
        x_flux[c] = face_flux(weights, edges[1], edges[0], edges[2], q[2], q[3])

    def row(r, carry):
        main = [weight_ref[r, 0], weight_ref[r, 1]]
        ahead = weight_ref[r + 1, 0]

        def weight(field, c):
            return pick(main[field // 8], field, c)

        def z_rows(c, shift=0):
            return pl.ds(16 * c + 8 + shift, 8)

        loaded, edges = {}, {}

        def q_at(c):
            if c not in loaded:
                loaded[c] = state[r + 3, cell(c)]
            return loaded[c]

        def y_edge(c):
            if c not in edges:
                edges[c] = edge_value(q_at(c - 2), q_at(c - 1), q_at(c), q_at(c + 1))
            return edges[c]

        def y_face(c):
            weights = [weight(YA + i, c) if c < COLS else weight(WA + i, 0) for i in range(3)]
            return face_flux(
                weights, y_edge(c), y_edge(c - 1), y_edge(c + 1), q_at(c - 1), q_at(c)
            )

        flux_y = y_face(0)
        for c in range(COLS):
            here = q_at(c)
            z_q[z_rows(c), :] = here
            flux_y_up = y_face(c + 1)
            q1, q2, q3 = [state[r + 3 + k, cell(c)] for k in (1, 2, 3)]
            new_edge = edge_value(here, q1, q2, q3)
            x_edges[r + 3, c] = new_edge
            flux_x_up = face_flux(
                [pick(ahead, XA + i, c) for i in range(3)],
                x_edges[r + 2, c], x_edges[r + 1, c], new_edge, here, q1,
            )
            flux_x = x_flux[c]
            x_flux[c] = flux_x_up
            m2, m1 = z_q[z_rows(c, -2), :], z_q[z_rows(c, -1), :]
            p1, p2 = z_q[z_rows(c, 1), :], z_q[z_rows(c, 2), :]
            edge = edge_value(m2, m1, here, p1)
            z_edge[z_rows(c), :] = edge
            flux_z = face_flux(
                [weight(ZA + i, c) for i in range(3)],
                edge, z_edge[z_rows(c, -1), :], edge_value(m1, here, p1, p2), m1, here,
            )
            z_flux[z_rows(c), :] = flux_z
            total = (flux_x_up - flux_x) + (flux_y_up - flux_y) + (z_flux[z_rows(c, 1), :] - flux_z)
            state[r + 3, cell(c)] = (weight(MASS, c) * here - total) * weight(INV, c)
            flux_y = flux_y_up
        return carry

    lax.fori_loop(0, ROWS, row, 0)


def react(state, sel_ref, net_ref, coeff_ref, rate_ref):
    def block(n, carry):
        rows = [3 + 4 * n + i for i in range(4)]
        inner = pl.ds(24, 128)
        conc = jnp.concatenate([state[r, inner] for r in rows], 0).astype(BF16)
        for k in range(2):
            part = slice(256 * k, 256 * k + 256)
            one = jnp.dot(conc, sel_ref[:, part], preferred_element_type=F32)
            two = jnp.dot(
                conc, sel_ref[:, 512 + 256 * k : 768 + 256 * k], preferred_element_type=F32
            )
            rate_ref[:, part] = (coeff_ref[:, part] * one * two).astype(BF16)
        change = jnp.dot(rate_ref[...], net_ref[...], preferred_element_type=F32)
        change = change.astype(BF16).astype(F32)
        for i, r in enumerate(rows):
            state[r, inner] += change[128 * i : 128 * i + 128]
        return carry

    lax.fori_loop(0, ROWS // 4, block, 0)


def first_kernel(
    place_ref, weather_ref, row_lo, row_hi, col_lo, col_hi, sel_ref, net_ref, coeff_ref, in_ref,
    state, later_ref, row_up, row_down, col_right, col_left, now_ref, rate_ref, *work
):
    del in_ref
    halos = (row_lo, row_hi, col_lo, col_hi)
    for s, ref in enumerate((now_ref, later_ref)):
        write_weights(s, place_ref, weather_ref, *halos, ref)
    read_edges(state, *halos)
    advect(state, now_ref, *work)
    react(state, sel_ref, net_ref, coeff_ref, rate_ref)
    write_edges(state, row_up, row_down, col_right, col_left)


def second_kernel(
    weight_ref, row_lo, row_hi, col_lo, col_hi, sel_ref, net_ref, coeff_ref, in_ref,
    state, out_ref, turn_ref, rate_ref, *work
):
    del in_ref
    read_edges(state, row_lo, row_hi, col_lo, col_hi)
    advect(state, weight_ref, *work)
    react(state, sel_ref, net_ref, coeff_ref, rate_ref)

    def row(r, carry):
        turned = []
        for half in range(2):
            base = 128 * (2 * (r & 1) + half)
            whole = state[r + 3, pl.ds(24, 128), 128 * half : 128 * half + 128]
            turn_ref[pl.ds(pl.multiple_of(base, 128), 128), :] = whole
            parts = [
                turn_ref[pl.ds(base + 64 * (i % 2) + i // 2, 8, stride=8), :] for i in range(16)
            ]
            turned.append(jnp.concatenate(parts, 0).T)
        turned = jnp.concatenate([turned[0], turned[1][0:64]], 0)
        for dest in range(8):
            out_ref[dest, pl.ds(3 * r, 3)] = turned[24 * dest : 24 * dest + 24].reshape(3, 8, 128)
        return carry

    lax.fori_loop(0, ROWS, row, 0, unroll=2)


def blocks(*lead):
    return jax.ShapeDtypeStruct(lead + (8, 128), F32)


def call(kernel, outs, specs, scratch=(), args=(), aliases=None):
    single = not isinstance(outs, (list, tuple))
    return pl.pallas_call(
        kernel,
        out_shape=outs,
        in_specs=specs,
        out_specs=VMEM if single else [VMEM] * len(outs),
        scratch_shapes=list(scratch),
        input_output_aliases=aliases or {},
        compiler_params=pltpu.CompilerParams(vmem_limit_bytes=40 * 2**20),
    )(*args)


def swap(x):
    return lax.all_to_all(x, "tracer", split_axis=0, concat_axis=0, tiled=True)


def halo(row_up, row_down, col_right, col_left):
    tiles = [(i, i + 1) for i in range(lax.axis_size("tile") - 1)]
    columns = list(zip(ORDER[:-1], ORDER[1:]))

    def back(pairs):
        return [(target, source) for source, target in pairs]

    return (
        lax.ppermute(row_up, "tile", tiles),
        lax.ppermute(row_down, "tile", back(tiles)),
        lax.ppermute(col_right, "tracer", columns),
        lax.ppermute(col_left, "tracer", back(columns)),
    )


def per_device(
    tracers, air_mass, flux_x, flux_y, flux_z, reactants, products, rate_coeff, record_of_step
):
    reactions, species = products.shape
    place = jnp.stack([lax.axis_index("tile"), lax.axis_index("tracer")]).astype(jnp.int32)
    pairs = reactants.T
    ident = lax.broadcasted_iota(jnp.int32, (LANES, reactions), 0)
    hot = [pairs[k : k + 1] == ident for k in range(2)]
    selector = jnp.concatenate(hot, 1).astype(BF16)
    ident = lax.broadcasted_iota(jnp.int32, (reactions, LANES), 1)
    net = jnp.pad(products, ((0, 0), (0, LANES - species)))
    for k in range(2):
        net = net - (reactants[:, k : k + 1] == ident).astype(jnp.int32)
    constants = (selector, net.astype(BF16), rate_coeff[None, :])

    sent = call(
        pack_kernel, blocks(8, 56), [VMEM] * 5,
        args=[x.reshape(-1, 128) for x in (tracers, air_mass, flux_x, flux_y, flux_z)],
    )

    def edge_blocks(*counts):
        return [jax.ShapeDtypeStruct((count, LANES), BF16) for count in counts]

    state_shape = jax.ShapeDtypeStruct((ROWS + 6, 8 * (COLS + 6), LANES), F32)
    turn = pltpu.VMEM((512, 128), F32)
    state, weather, *edges = call(
        arrange_kernel,
        [state_shape, blocks(STEPS, 8)] + edge_blocks(400, 400, 400, 416),
        [SMEM, VMEM],
        [turn],
        (record_of_step, swap(sent)),
    )
    column = pltpu.VMEM((16 * COLS + 16, LANES), F32)
    work = [
        pltpu.VMEM((512, reactions), BF16),
        pltpu.VMEM((19, COLS, 8, LANES), F32),
        pltpu.VMEM((COLS, 8, LANES), F32),
        column, column, column,
    ]
    weights = (ROWS + 1, 2, 8, 128)
    state, later, *edges = call(
        first_kernel,
        [state_shape, jax.ShapeDtypeStruct(weights, F32)] + edge_blocks(384, 384, 384, 384),
        [SMEM] + [VMEM] * 9,
        [pltpu.VMEM(weights, F32)] + work,
        (place, weather) + halo(*edges) + constants + (state,),
        {9: 0},
    )
    _, sent = call(
        second_kernel,
        [state_shape, blocks(8, 48)],
        [VMEM] * 9,
        [turn] + work,
        (later,) + halo(*edges) + constants + (state,),
        {8: 0},
    )
    out = call(
        unpack_kernel, jax.ShapeDtypeStruct((tracers.size // 128, 128), F32), [VMEM],
        args=(swap(sent),),
    )
    return out.reshape(tracers.shape)


def solution(mesh):
    fields = P("tracer", None, "tile", None)
    return jax.shard_map(
        per_device,
        mesh=mesh,
        in_specs=(fields,) * 5 + (P(),) * 4,
        out_specs=fields,
        check_vma=False,
    )
```

time: 152 us -> 138 us (0.908); the launches traced: 151 us -> 135 us
  Pallas kernels: 49.6 us -> 36.6 us
  blocking collectives: 31.1 us -> 26.1 us
  waiting for transfers between devices: 35.9 us -> 39.3 us
    pallas_call x5, Pallas kernels: 49.6 us -> 36.6 us  [call(): pl.pallas_call(kernel, out_shape=outs, in_specs=specs, out_specs=VMEM if...]
    all_to_all x1, blocking collectives: 31.1 us -> 26.1 us  [swap(): return lax.all_to_all(x, 'tracer', split_axis=0, concat_axis=0, tiled=True)]
    ppermute x2, waiting for transfers between devices: 4.5 us -> 8.9 us  [halo(): lax.ppermute(col_left, 'tracer', back(columns))]
    ppermute x2, waiting for transfers between devices: 1.73 us -> 3.33 us  [halo(): lax.ppermute(col_right, 'tracer', columns)]
    ppermute x2, waiting for transfers between devices: 1.77 us -> 0.23 us  [halo(): lax.ppermute(row_down, 'tile', back(tiles))]
    unnamed x20 -> x19, local copies, waits for them, and re-layouts: 6.04 us -> 4.97 us
  transfers between devices with their start and end apart: 9 -> 9, of which waited for: 5 -> 6; matrix products, arithmetic and copies ran while one was open for 0% -> 1% of each run, Pallas kernels for 0% -> 0%
where the time goes in v3:
time: 138 us; the launch traced here: 135 us
  waiting for transfers between devices  39.3 us (28%)
  Pallas kernels  36.6 us (27%)
  starting transfers between devices  27.7 us (20%)
  blocking collectives  26.1 us (19%)
  local copies, waits for them, and re-layouts  4.98 us (4%)
    pallas_call x5, Pallas kernels, call(): pl.pallas_call(kernel, out_shape=outs, in_specs=specs, out_specs=VMEM if...  36.6 us
    all_to_all x1, waiting for transfers between devices, swap(): return lax.all_to_all(x, 'tracer', split_axis=0, concat_axis=0, tiled=True)  26.9 us
    all_to_all x1, blocking collectives, swap(): return lax.all_to_all(x, 'tracer', split_axis=0, concat_axis=0, tiled=True)  26.1 us
    ppermute x2, starting transfers between devices, halo(): lax.ppermute(row_down, 'tile', back(tiles))  9.08 us
    ppermute x2, waiting for transfers between devices, halo(): lax.ppermute(col_left, 'tracer', back(columns))  8.9 us
    all_to_all x1, starting transfers between devices, swap(): return lax.all_to_all(x, 'tracer', split_axis=0, concat_axis=0, tiled=True)  7.74 us
    unnamed x19, local copies, waits for them, and re-layouts  4.97 us
    ppermute x2, starting transfers between devices, halo(): lax.ppermute(col_right, 'tracer', columns)  4.5 us
  transfers between devices with their start and end apart: 9, of which 6 were waited for; matrix products, arithmetic and copies ran while one was open for 1% of the time, Pallas kernels for 0%

profile of v3, /device:TPU:16, one launch (start us, length us, event | category | flops | bytes accessed | tf_op | source)
XLA Modules:
  0.0 135.3 jit_solution(13033855927643752009)
XLA Ops:
  0.0 1.4 %copy-done = f32[24,8,16,128]{3,2,1,0:T(8,128)S(1)} copy-done((f32[24,8,16,128]{3,2,1,0:T(8,128)S(1)}, f32[24,8,16,128]{3,2,1,0:T(8,128)}, u32[]{:S(2)}) %copy-start) | copy-done | bytes 1572888
  1.4 0.8 copy-done.1
  2.3 0.8 copy-done.2
  3.1 0.8 copy-done.3
  4.8 4.3 %shard_map.91 = f32[8,56,8,128]{3,2,1,0:T(8,128)} custom-call(f32[3072,128]{1,0:T(8,128)S(1)} %bitcast.14, f32[128,128]{1,0:T(8,128)S(1)} %bitcast.15, f32[128,128]{1,0:T(8,128)S(1)} %bitcast.16, f32[128,128]{1,0:T(8,128)S(1)} %bitcast.17, f32[128,128]{1,0:T(8,128)S(1)} %bitcast.18), custom_call_target="tpu_custom_call" | custom-call | tf_op jit(solution)/shard_map/pallas_call | solution.py:349
  9.0 7.7 %all-to-all-start = ((f32[8,56,8,128]{3,2,1,0:T(8,128)}), f32[8,56,8,128]{3,2,1,0:T(8,128)S(1)}, u32[]{:S(2)}, u32[]{:S(2)}) async-start(f32[8,56,8,128]{3,2,1,0:T(8,128)} %shard_map.91), calls=%async_computation | async-start | bytes 3670016 | tf_op jit(solution)/shard_map/all_to_all | solution.py:361
  17.3 26.9 %all-to-all-done.in_ref = f32[8,56,8,128]{3,2,1,0:T(8,128)S(1)} async-done(((f32[8,56,8,128]{3,2,1,0:T(8,128)}), f32[8,56,8,128]{3,2,1,0:T(8,128)S(1)}, u32[]{:S(2)}, u32[]{:S(2)}) %all-to-all-start) | async-done | bytes 1835040 | tf_op jit(solution)/shard_map/all_to_all | solution.py:361
  44.2 1.9 %shard_map.92 = (f32[22,176,256]{2,1,0:T(8,128)S(1)}, f32[2,8,8,128]{3,2,1,0:T(8,128)S(1)}, bf16[400,256]{1,0:T(8,128)(2,1)S(1)}, bf16[400,256]{1,0:T(8,128)(2,1...) custom-call(s32[2]{0:T(128)S(1)} %copy-done.6, f32[8,56,8,128]{3,2,1,0:T(8,128)S(1)} %all-to-all-done.in_ref), custom_call_target="tpu_custom_call" | custom-call | tf_op jit(solution)/shard_map/pallas_call | solution.py:349
  46.1 1.9 %collective-permute-start = (bf16[400,256]{1,0:T(8,128)(2,1)S(1)}, bf16[400,256]{1,0:T(8,128)(2,1)S(1)}, u32[]{:S(2)}, u32[]{:S(2)}) collective-permute-start(bf16[400,256]{1,0:T(8,128)(2,1)S(1)} %get-tuple-element.19), channel_id=1, source_target_pairs={{0,1},{1,2},{2,3},{3,4},{4,5},{5,6},{6,7},{7,8},{8,9},{9,10},{10,1... | collective-permute-start | bytes 614408 | tf_op jit(solution)/shard_map/ppermute | solution.py:372
  48.1 4.5 %collective-permute-start.1 = (bf16[400,256]{1,0:T(8,128)(2,1)S(1)}, bf16[400,256]{1,0:T(8,128)(2,1)S(1)}, u32[]{:S(2)}, u32[]{:S(2)}) collective-permute-start(bf16[400,256]{1,0:T(8,128)(2,1)S(1)} %get-tuple-element.20), channel_id=1, source_target_pairs={{1,0},{2,1},{3,2},{4,3},{5,4},{6,5},{7,6},{8,7},{9,8},{10,9},{11,1... | collective-permute-start | bytes 614408 | tf_op jit(solution)/shard_map/ppermute | solution.py:373
  52.6 1.5 %collective-permute-start.2 = (bf16[400,256]{1,0:T(8,128)(2,1)S(1)}, bf16[400,256]{1,0:T(8,128)(2,1)S(1)}, u32[]{:S(2)}, u32[]{:S(2)}) collective-permute-start(bf16[400,256]{1,0:T(8,128)(2,1)S(1)} %get-tuple-element.21), channel_id=1, source_target_pairs={{0,32},{32,64},{64,96},{96,112},{112,80},{80,48},{48,16},{1,33},{3... | collective-permute-start | bytes 614408 | tf_op jit(solution)/shard_map/ppermute | solution.py:374
  54.1 1.3 collective-permute-start.3
  55.9 1.5 %collective-permute-done.2.col_lo = bf16[400,256]{1,0:T(8,128)(2,1)S(1)} collective-permute-done((bf16[400,256]{1,0:T(8,128)(2,1)S(1)}, bf16[400,256]{1,0:T(8,128)(2,1)S(1)}, u32[]{:S(2)}, u32[]{:S(2)}) %collective-permute-start.2) | collective-permute-done | bytes 204832 | tf_op jit(solution)/shard_map/ppermute | solution.py:374
  57.3 4.5 %collective-permute-done.3.col_hi = bf16[416,256]{1,0:T(8,128)(2,1)S(1)} collective-permute-done((bf16[416,256]{1,0:T(8,128)(2,1)S(1)}, bf16[416,256]{1,0:T(8,128)(2,1)S(1)}, u32[]{:S(2)}, u32[]{:S(2)}) %collective-permute-start.3) | collective-permute-done | bytes 213024 | tf_op jit(solution)/shard_map/ppermute | solution.py:375
  61.8 13.0 %shard_map.93 = (f32[22,176,256]{2,1,0:T(8,128)S(1)}, f32[17,2,8,128]{3,2,1,0:T(8,128)S(1)}, bf16[384,256]{1,0:T(8,128)(2,1)S(1)}, bf16[384,256]{1,0:T(8,128)(2,...) custom-call(s32[2]{0:T(128)S(1)} %pad_add_fusion.place_ref, ...), custom_call_target="tpu_custom_call", output_to_operand_aliasing={{0}: (9, {})} | custom-call | tf_op jit(solution)/shard_map/pallas_call | solution.py:349
  74.8 1.9 %collective-permute-start.4 = (bf16[384,256]{1,0:T(8,128)(2,1)S(1)}, bf16[384,256]{1,0:T(8,128)(2,1)S(1)}, u32[]{:S(2)}, u32[]{:S(2)}) collective-permute-start(bf16[384,256]{1,0:T(8,128)(2,1)S(1)} %get-tuple-element.25), channel_id=1, source_target_pairs={{0,1},{1,2},{2,3},{3,4},{4,5},{5,6},{6,7},{7,8},{8,9},{9,10},{10,1... | collective-permute-start | bytes 589832 | tf_op jit(solution)/shard_map/ppermute | solution.py:372
  76.7 4.5 %collective-permute-start.5 = (bf16[384,256]{1,0:T(8,128)(2,1)S(1)}, bf16[384,256]{1,0:T(8,128)(2,1)S(1)}, u32[]{:S(2)}, u32[]{:S(2)}) collective-permute-start(bf16[384,256]{1,0:T(8,128)(2,1)S(1)} %get-tuple-element.26), channel_id=1, source_target_pairs={{1,0},{2,1},{3,2},{4,3},{5,4},{6,5},{7,6},{8,7},{9,8},{10,9},{11,1... | collective-permute-start | bytes 589832 | tf_op jit(solution)/shard_map/ppermute | solution.py:373
  81.3 3.0 %collective-permute-start.6 = (bf16[384,256]{1,0:T(8,128)(2,1)S(1)}, bf16[384,256]{1,0:T(8,128)(2,1)S(1)}, u32[]{:S(2)}, u32[]{:S(2)}) collective-permute-start(bf16[384,256]{1,0:T(8,128)(2,1)S(1)} %get-tuple-element.27), channel_id=1, source_target_pairs={{0,32},{32,64},{64,96},{96,112},{112,80},{80,48},{48,16},{1,33},{3... | collective-permute-start | bytes 589832 | tf_op jit(solution)/shard_map/ppermute | solution.py:374
  84.3 1.3 collective-permute-start.7
  85.6 1.8 %collective-permute-done.6.col_lo = bf16[384,256]{1,0:T(8,128)(2,1)S(1)} collective-permute-done((bf16[384,256]{1,0:T(8,128)(2,1)S(1)}, bf16[384,256]{1,0:T(8,128)(2,1)S(1)}, u32[]{:S(2)}, u32[]{:S(2)}) %collective-permute-start.6) | collective-permute-done | bytes 196640 | tf_op jit(solution)/shard_map/ppermute | solution.py:374
  87.5 4.4 %collective-permute-done.7.col_hi = bf16[384,256]{1,0:T(8,128)(2,1)S(1)} collective-permute-done((bf16[384,256]{1,0:T(8,128)(2,1)S(1)}, bf16[384,256]{1,0:T(8,128)(2,1)S(1)}, u32[]{:S(2)}, u32[]{:S(2)}) %collective-permute-start.7) | collective-permute-done | bytes 196640 | tf_op jit(solution)/shard_map/ppermute | solution.py:375
  91.9 13.1 %shard_map.94 = (f32[22,176,256]{2,1,0:T(8,128)S(1)}, f32[8,48,8,128]{3,2,1,0:T(8,128)S(1)}) custom-call(f32[17,2,8,128]{3,2,1,0:T(8,128)S(1)} %get-tuple-element.24.weight_ref, bf16[384,256]{1,0:T(8,128)(2,1)S(1)} %collective-permute-done.4.row_lo, bf16[384,256]{1,0:T(8,128)(2,1)S(1)} %collective-permute-done.5.row_hi, ...), custom_call_target="tpu_custom_call", output_to_operand_aliasing={{0}: (8, {})} | custom-call | tf_op jit(solution)/shard_map/pallas_call | solution.py:349
  105.0 26.1 %all_to_all.10.in_ref = f32[8,48,8,128]{3,2,1,0:T(8,128)S(1)} all-to-all(f32[8,48,8,128]{3,2,1,0:T(8,128)S(1)} %get-tuple-element.30), channel_id=1, replica_groups=mesh['tracer'=8,'tile'=16] {'tracer'}, dimensions={0} | all-to-all | bytes 3145728 | tf_op jit(solution)/shard_map/all_to_all | solution.py:361
  131.1 4.3 %shard_map.95 = f32[3072,128]{1,0:T(8,128)} custom-call(f32[8,48,8,128]{3,2,1,0:T(8,128)S(1)} %all_to_all.10.in_ref), custom_call_target="tpu_custom_call" | custom-call | tf_op jit(solution)/shard_map/pallas_call | solution.py:349
  (25 shorter events, 1.8 us)
Async XLA Ops:
  0.0 1.4 %copy-start = (f32[24,8,16,128]{3,2,1,0:T(8,128)S(1)}, f32[24,8,16,128]{3,2,1,0:T(8,128)}, u32[]{:S(2)}) copy-start(f32[24,8,16,128]{3,2,1,0:T(8,128)} %param.9) | copy-start | bytes 4718596
  1.4 0.8 copy-start.1
  2.2 0.8 copy-start.2
  3.1 0.8 copy-start.3
  3.9 0.8 copy-start.4
  9.0 7.8 %copy-start.7 = (s32[512,192]{0,1:T(8,128)S(1)}, s32[512,192]{0,1:T(8,128)}, u32[]{:S(2)}) copy-start(s32[512,192]{0,1:T(8,128)} %param.15) | copy-start | bytes 1179652
  9.0 8.1 %copy-start.8 = (s32[512,2]{0,1:T(2,128)S(1)}, s32[512,2]{0,1:T(2,128)}, u32[]{:S(2)}) copy-start(s32[512,2]{0,1:T(2,128)} %param.14) | copy-start | bytes 12292
  9.0 35.1 %all-to-all-start = ((f32[8,56,8,128]{3,2,1,0:T(8,128)}), f32[8,56,8,128]{3,2,1,0:T(8,128)S(1)}, u32[]{:S(2)}, u32[]{:S(2)}) async-start(f32[8,56,8,128]{3,2,1,0:T(8,128)} %shard_map.91), calls=%async_computation | async-start | bytes 3670016 | tf_op jit(solution)/shard_map/all_to_all | solution.py:361
  16.8 27.4 %copy-start.6 = (s32[2]{0:T(128)S(1)}, s32[2]{0:T(128)}, u32[]{:S(2)}) copy-start(s32[2]{0:T(128)} %rec_ref.1) | copy-start | bytes 28
  17.1 44.7 %copy-start.5 = (f32[512]{0:T(512)S(1)}, f32[512]{0:T(512)}, u32[]{:S(2)}) copy-start(f32[512]{0:T(512)} %param.16) | copy-start | bytes 6148
  46.1 9.5 %collective-permute-start = (bf16[400,256]{1,0:T(8,128)(2,1)S(1)}, bf16[400,256]{1,0:T(8,128)(2,1)S(1)}, u32[]{:S(2)}, u32[]{:S(2)}) collective-permute-start(bf16[400,256]{1,0:T(8,128)(2,1)S(1)} %get-tuple-element.19), channel_id=1, source_target_pairs={{0,1},{1,2},{2,3},{3,4},{4,5},{5,6},{6,7},{7,8},{8,9},{9,10},{10,1... | collective-permute-start | bytes 614408 | tf_op jit(solution)/shard_map/ppermute | solution.py:372
  48.1 7.8 %collective-permute-start.1 = (bf16[400,256]{1,0:T(8,128)(2,1)S(1)}, bf16[400,256]{1,0:T(8,128)(2,1)S(1)}, u32[]{:S(2)}, u32[]{:S(2)}) collective-permute-start(bf16[400,256]{1,0:T(8,128)(2,1)S(1)} %get-tuple-element.20), channel_id=1, source_target_pairs={{1,0},{2,1},{3,2},{4,3},{5,4},{6,5},{7,6},{8,7},{9,8},{10,9},{11,1... | collective-permute-start | bytes 614408 | tf_op jit(solution)/shard_map/ppermute | solution.py:373
  52.6 4.7 %collective-permute-start.2 = (bf16[400,256]{1,0:T(8,128)(2,1)S(1)}, bf16[400,256]{1,0:T(8,128)(2,1)S(1)}, u32[]{:S(2)}, u32[]{:S(2)}) collective-permute-start(bf16[400,256]{1,0:T(8,128)(2,1)S(1)} %get-tuple-element.21), channel_id=1, source_target_pairs={{0,32},{32,64},{64,96},{96,112},{112,80},{80,48},{48,16},{1,33},{3... | collective-permute-start | bytes 614408 | tf_op jit(solution)/shard_map/ppermute | solution.py:374
  54.1 7.7 %collective-permute-start.3 = (bf16[416,256]{1,0:T(8,128)(2,1)S(1)}, bf16[416,256]{1,0:T(8,128)(2,1)S(1)}, u32[]{:S(2)}, u32[]{:S(2)}) collective-permute-start(bf16[416,256]{1,0:T(8,128)(2,1)S(1)} %get-tuple-element.22), channel_id=1, source_target_pairs={{32,0},{64,32},{96,64},{112,96},{80,112},{48,80},{16,48},{33,1},{6... | collective-permute-start | bytes 638984 | tf_op jit(solution)/shard_map/ppermute | solution.py:375
  74.8 10.8 %collective-permute-start.4 = (bf16[384,256]{1,0:T(8,128)(2,1)S(1)}, bf16[384,256]{1,0:T(8,128)(2,1)S(1)}, u32[]{:S(2)}, u32[]{:S(2)}) collective-permute-start(bf16[384,256]{1,0:T(8,128)(2,1)S(1)} %get-tuple-element.25), channel_id=1, source_target_pairs={{0,1},{1,2},{2,3},{3,4},{4,5},{5,6},{6,7},{7,8},{8,9},{9,10},{10,1... | collective-permute-start | bytes 589832 | tf_op jit(solution)/shard_map/ppermute | solution.py:372
  76.7 8.9 %collective-permute-start.5 = (bf16[384,256]{1,0:T(8,128)(2,1)S(1)}, bf16[384,256]{1,0:T(8,128)(2,1)S(1)}, u32[]{:S(2)}, u32[]{:S(2)}) collective-permute-start(bf16[384,256]{1,0:T(8,128)(2,1)S(1)} %get-tuple-element.26), channel_id=1, source_target_pairs={{1,0},{2,1},{3,2},{4,3},{5,4},{6,5},{7,6},{8,7},{9,8},{10,9},{11,1... | collective-permute-start | bytes 589832 | tf_op jit(solution)/shard_map/ppermute | solution.py:373
  81.3 6.2 %collective-permute-start.6 = (bf16[384,256]{1,0:T(8,128)(2,1)S(1)}, bf16[384,256]{1,0:T(8,128)(2,1)S(1)}, u32[]{:S(2)}, u32[]{:S(2)}) collective-permute-start(bf16[384,256]{1,0:T(8,128)(2,1)S(1)} %get-tuple-element.27), channel_id=1, source_target_pairs={{0,32},{32,64},{64,96},{96,112},{112,80},{80,48},{48,16},{1,33},{3... | collective-permute-start | bytes 589832 | tf_op jit(solution)/shard_map/ppermute | solution.py:374
  84.3 7.6 %collective-permute-start.7 = (bf16[384,256]{1,0:T(8,128)(2,1)S(1)}, bf16[384,256]{1,0:T(8,128)(2,1)S(1)}, u32[]{:S(2)}, u32[]{:S(2)}) collective-permute-start(bf16[384,256]{1,0:T(8,128)(2,1)S(1)} %get-tuple-element.28), channel_id=1, source_target_pairs={{32,0},{64,32},{96,64},{112,96},{80,112},{48,80},{16,48},{33,1},{6... | collective-permute-start | bytes 589832 | tf_op jit(solution)/shard_map/ppermute | solution.py:375

commit v4 on v3

--- a/solution.py
+++ b/solution.py
@@ -10,11 +10,13 @@
 BF16 = jnp.bfloat16
 ROWS = 16
 COLS = 16
+STACK = 16
 LANES = 256
 ORDER = (0, 2, 4, 6, 7, 5, 3, 1)
 XA, YA, ZA, MASS, INV, WA = 0, 3, 6, 9, 10, 11
 VMEM = pl.BlockSpec(memory_space=pltpu.VMEM)
 SMEM = pl.BlockSpec(memory_space=pltpu.SMEM)
+ANY = pl.BlockSpec(memory_space=pltpu.HBM)
 
 
 def roll(x, shift):
@@ -39,29 +41,85 @@
     return out
 
 
-def pack_kernel(q_ref, mass_ref, fx_ref, fy_ref, fz_ref, out_ref):
-    def row(r, carry):
-        levels = [q_ref[pl.ds(lev * 16 + r, 24, stride=128), :] for lev in range(8)]
-        for place, value in enumerate(exchange_blocks(levels)):
-            out_ref[ORDER[place], pl.ds(3 * r, 3)] = value.reshape(3, 8, 128)
-        return carry
-
-    lax.fori_loop(0, ROWS, row, 0, unroll=2)
-    for field, ref in enumerate((mass_ref, fx_ref, fy_ref, fz_ref)):
-        for half in range(2):
-            rows = [ref[pl.ds(8 * half + r, 8, stride=16), :] for r in range(8)]
-            for place, value in enumerate(exchange_blocks(rows)):
-                out_ref[ORDER[place], 48 + 2 * field + half] = value
-
-
-def unpack_kernel(in_ref, out_ref):
-    def row(r, carry):
-        cols = [in_ref[src, pl.ds(3 * r, 3)].reshape(24, 128) for src in ORDER]
-        for lev, value in enumerate(exchange_blocks(cols)):
-            out_ref[pl.ds(lev * 16 + r, 24, stride=128), :] = value
-        return carry
-
-    lax.fori_loop(0, ROWS, row, 0, unroll=2)
+def pack_kernel(
+    q_hbm, mass_hbm, fx_hbm, fy_hbm, fz_hbm, out_hbm, q_ref, field_ref, out_ref, in_sem, out_sem
+):
+    fields = (mass_hbm, fx_hbm, fy_hbm, fz_hbm)
+    loads = [
+        pltpu.make_async_copy(hbm, field_ref.at[i], in_sem.at[i]) for i, hbm in enumerate(fields)
+    ]
+    for tg in range(3):
+        part = pl.ds(1024 * tg, 1024)
+        loads.append(pltpu.make_async_copy(q_hbm.at[part], q_ref.at[part], in_sem.at[4 + tg]))
+    stores = []
+    for i, (start, count) in enumerate(((48, 8), (0, 16), (16, 16), (32, 16))):
+        part = pl.ds(start, count)
+        stores.append(
+            pltpu.make_async_copy(out_ref.at[:, part], out_hbm.at[:, part], out_sem.at[i])
+        )
+    for load in loads:
+        load.start()
+    for i in range(4):
+        loads[i].wait()
+    rows = [
+        jnp.concatenate(
+            [
+                field_ref[i, pl.ds(8 * half + r, 8, stride=16), :]
+                for i in range(4)
+                for half in range(2)
+            ],
+            0,
+        )
+        for r in range(8)
+    ]
+    for place, value in enumerate(exchange_blocks(rows)):
+        out_ref[ORDER[place], 48:56] = value.reshape(8, 8, 128)
+    stores[0].start()
+    for tg in range(3):
+        loads[4 + tg].wait()
+
+        def rows(k, carry, tg=tg):
+            levels = [
+                jnp.concatenate(
+                    [
+                        q_ref[pl.ds(1024 * tg + lev * 16 + STACK * k + i, 8, stride=128), :]
+                        for i in range(STACK)
+                    ],
+                    0,
+                )
+                for lev in range(8)
+            ]
+            for place, value in enumerate(exchange_blocks(levels)):
+                part = pl.ds(16 * tg + STACK * k, STACK)
+                out_ref[ORDER[place], part] = value.reshape(STACK, 8, 128)
+            return carry
+
+        lax.fori_loop(0, ROWS // STACK, rows, 0)
+        stores[1 + tg].start()
+    for store in stores:
+        store.wait()
+
+
+def unpack_kernel(in_ref, out_hbm, out_ref, out_sem):
+    stores = []
+    for tg in range(3):
+        part = pl.ds(1024 * tg, 1024)
+        stores.append(pltpu.make_async_copy(out_ref.at[part], out_hbm.at[part], out_sem.at[tg]))
+    for tg in range(3):
+
+        def rows(k, carry, tg=tg):
+            part = pl.ds(16 * tg + STACK * k, STACK)
+            cols = [in_ref[src, part].reshape(8 * STACK, 128) for src in ORDER]
+            for lev, value in enumerate(exchange_blocks(cols)):
+                for i in range(STACK):
+                    start = 1024 * tg + lev * 16 + STACK * k + i
+                    out_ref[pl.ds(start, 8, stride=128), :] = value[8 * i : 8 * i + 8]
+            return carry
+
+        lax.fori_loop(0, ROWS // STACK, rows, 0)
+        stores[tg].start()
+    for store in stores:
+        store.wait()
 
 
 def cell(c):
@@ -95,7 +153,7 @@
     rec_ref, in_ref, state_ref, weather_ref, row_up, row_down, col_right, col_left, turn_ref
 ):
     def row(r, carry):
-        parts = [in_ref[src, pl.ds(3 * r, 3)].reshape(24, 128) for src in range(8)]
+        parts = [in_ref[src, 16 * tg + r] for src in range(8) for tg in range(3)]
         parts.append(jnp.zeros((LANES - 192, 128), F32))
         stacked = jnp.concatenate(parts, 0)
         for half in range(2):
@@ -333,8 +391,8 @@
             ]
             turned.append(jnp.concatenate(parts, 0).T)
         turned = jnp.concatenate([turned[0], turned[1][0:64]], 0)
-        for dest in range(8):
-            out_ref[dest, pl.ds(3 * r, 3)] = turned[24 * dest : 24 * dest + 24].reshape(3, 8, 128)
+        for g in range(24):
+            out_ref[g // 3, 16 * (g % 3) + r] = turned[8 * g : 8 * g + 8]
         return carry
 
     lax.fori_loop(0, ROWS, row, 0, unroll=2)
@@ -344,16 +402,16 @@
     return jax.ShapeDtypeStruct(lead + (8, 128), F32)
 
 
-def call(kernel, outs, specs, scratch=(), args=(), aliases=None):
+def call(kernel, outs, specs, scratch=(), args=(), aliases=None, out_spec=VMEM, grant=40 * 2**20):
     single = not isinstance(outs, (list, tuple))
     return pl.pallas_call(
         kernel,
         out_shape=outs,
         in_specs=specs,
-        out_specs=VMEM if single else [VMEM] * len(outs),
+        out_specs=out_spec if single else [VMEM] * len(outs),
         scratch_shapes=list(scratch),
         input_output_aliases=aliases or {},
-        compiler_params=pltpu.CompilerParams(vmem_limit_bytes=40 * 2**20),
+        compiler_params=pltpu.CompilerParams(vmem_limit_bytes=grant),
     )(*args)
 
 
@@ -392,8 +450,19 @@
     constants = (selector, net.astype(BF16), rate_coeff[None, :])
 
     sent = call(
-        pack_kernel, blocks(8, 56), [VMEM] * 5,
-        args=[x.reshape(-1, 128) for x in (tracers, air_mass, flux_x, flux_y, flux_z)],
+        pack_kernel,
+        blocks(8, 56),
+        [ANY] * 5,
+        [
+            pltpu.VMEM((3072, 128), F32),
+            pltpu.VMEM((4, 128, 128), F32),
+            pltpu.VMEM((8, 56, 8, 128), F32),
+            pltpu.SemaphoreType.DMA((7,)),
+            pltpu.SemaphoreType.DMA((4,)),
+        ],
+        [x.reshape(-1, 128) for x in (tracers, air_mass, flux_x, flux_y, flux_z)],
+        out_spec=ANY,
+        grant=63 * 2**20,
     )
 
     def edge_blocks(*counts):
@@ -433,8 +502,12 @@
         {8: 0},
     )
     out = call(
-        unpack_kernel, jax.ShapeDtypeStruct((tracers.size // 128, 128), F32), [VMEM],
-        args=(swap(sent),),
+        unpack_kernel,
+        jax.ShapeDtypeStruct((tracers.size // 128, 128), F32),
+        [VMEM],
+        [pltpu.VMEM((3072, 128), F32), pltpu.SemaphoreType.DMA((3,))],
+        (swap(sent),),
+        out_spec=ANY,
     )
     return out.reshape(tracers.shape)
 

time: 138 us -> 131 us (0.949)
  local copies, waits for them, and re-layouts: 4.98 us -> 0.23 us
  Pallas kernels: 36.6 us -> 34.8 us
    unnamed x19 -> x9, local copies, waits for them, and re-layouts: 4.97 us -> 0.22 us
    pallas_call x5, Pallas kernels: 36.6 us -> 34.8 us  [call(): pl.pallas_call(kernel, out_shape=outs, in_specs=specs, out_specs=out_spec...]
where the time goes in v4:
time: 131 us; the launch traced here: 129 us
  waiting for transfers between devices  39.3 us (30%)
  Pallas kernels  34.8 us (27%)
  starting transfers between devices  27.8 us (21%)
  blocking collectives  26.1 us (20%)
    pallas_call x5, Pallas kernels, call(): pl.pallas_call(kernel, out_shape=outs, in_specs=specs, out_specs=out_spec...  34.8 us
    all_to_all x1, waiting for transfers between devices, swap(): return lax.all_to_all(x, 'tracer', split_axis=0, concat_axis=0, tiled=True)  26.9 us
    all_to_all x1, blocking collectives, swap(): return lax.all_to_all(x, 'tracer', split_axis=0, concat_axis=0, tiled=True)  26.1 us
    ppermute x2, starting transfers between devices, halo(): lax.ppermute(row_down, 'tile', back(tiles))  9.08 us
    ppermute x2, waiting for transfers between devices, halo(): lax.ppermute(col_left, 'tracer', back(columns))  8.9 us
    all_to_all x1, starting transfers between devices, swap(): return lax.all_to_all(x, 'tracer', split_axis=0, concat_axis=0, tiled=True)  7.76 us
    ppermute x2, starting transfers between devices, halo(): lax.ppermute(col_right, 'tracer', columns)  4.5 us
    ppermute x2, starting transfers between devices, halo(): lax.ppermute(row_up, 'tile', tiles)  3.84 us
  transfers between devices with their start and end apart: 9, of which 6 were waited for; matrix products, arithmetic and copies ran while one was open for 1% of the time, Pallas kernels for 0%

profile of v4, /device:TPU:16, one launch (start us, length us, event | category | flops | bytes accessed | tf_op | source)
XLA Modules:
  0.0 128.8 jit_solution(18105661914718246093)
XLA Ops:
  0.0 4.1 %shard_map.91 = f32[8,56,8,128]{3,2,1,0:T(8,128)} custom-call(f32[3072,128]{1,0:T(8,128)} %bitcast.16, f32[128,128]{1,0:T(8,128)} %bitcast.17, f32[128,128]{1,0:T(8,128)} %bitcast.18, f32[128,128]{1,0:T(8,128)} %bitcast.19, f32[128,128]{1,0:T(8,128)} %bitcast.20), custom_call_target="tpu_custom_call" | custom-call | tf_op jit(solution)/shard_map/pallas_call | solution.py:407
  4.1 7.8 %all-to-all-start = ((f32[8,56,8,128]{3,2,1,0:T(8,128)}), f32[8,56,8,128]{3,2,1,0:T(8,128)S(1)}, u32[]{:S(2)}, u32[]{:S(2)}) async-start(f32[8,56,8,128]{3,2,1,0:T(8,128)} %shard_map.91), calls=%async_computation | async-start | bytes 3670016 | tf_op jit(solution)/shard_map/all_to_all | solution.py:419
  11.9 0.2 copy.12
  12.2 0.1 iota_compare_fusion.2
  12.4 26.9 %all-to-all-done.in_ref = f32[8,56,8,128]{3,2,1,0:T(8,128)S(1)} async-done(((f32[8,56,8,128]{3,2,1,0:T(8,128)}), f32[8,56,8,128]{3,2,1,0:T(8,128)S(1)}, u32[]{:S(2)}, u32[]{:S(2)}) %all-to-all-start) | async-done | bytes 1835040 | tf_op jit(solution)/shard_map/all_to_all | solution.py:419
  39.3 1.9 %shard_map.92 = (f32[22,176,256]{2,1,0:T(8,128)S(1)}, f32[2,8,8,128]{3,2,1,0:T(8,128)S(1)}, bf16[400,256]{1,0:T(8,128)(2,1)S(1)}, bf16[400,256]{1,0:T(8,128)(2,1...) custom-call(s32[2]{0:T(128)S(1)} %copy-done.1, f32[8,56,8,128]{3,2,1,0:T(8,128)S(1)} %all-to-all-done.in_ref), custom_call_target="tpu_custom_call" | custom-call | tf_op jit(solution)/shard_map/pallas_call | solution.py:407
  41.2 1.9 %collective-permute-start = (bf16[400,256]{1,0:T(8,128)(2,1)S(1)}, bf16[400,256]{1,0:T(8,128)(2,1)S(1)}, u32[]{:S(2)}, u32[]{:S(2)}) collective-permute-start(bf16[400,256]{1,0:T(8,128)(2,1)S(1)} %get-tuple-element.19), channel_id=1, source_target_pairs={{0,1},{1,2},{2,3},{3,4},{4,5},{5,6},{6,7},{7,8},{8,9},{9,10},{10,1... | collective-permute-start | bytes 614408 | tf_op jit(solution)/shard_map/ppermute | solution.py:430
  43.2 4.5 %collective-permute-start.1 = (bf16[400,256]{1,0:T(8,128)(2,1)S(1)}, bf16[400,256]{1,0:T(8,128)(2,1)S(1)}, u32[]{:S(2)}, u32[]{:S(2)}) collective-permute-start(bf16[400,256]{1,0:T(8,128)(2,1)S(1)} %get-tuple-element.20), channel_id=1, source_target_pairs={{1,0},{2,1},{3,2},{4,3},{5,4},{6,5},{7,6},{8,7},{9,8},{10,9},{11,1... | collective-permute-start | bytes 614408 | tf_op jit(solution)/shard_map/ppermute | solution.py:431
  47.7 1.5 %collective-permute-start.2 = (bf16[400,256]{1,0:T(8,128)(2,1)S(1)}, bf16[400,256]{1,0:T(8,128)(2,1)S(1)}, u32[]{:S(2)}, u32[]{:S(2)}) collective-permute-start(bf16[400,256]{1,0:T(8,128)(2,1)S(1)} %get-tuple-element.21), channel_id=1, source_target_pairs={{0,32},{32,64},{64,96},{96,112},{112,80},{80,48},{48,16},{1,33},{3... | collective-permute-start | bytes 614408 | tf_op jit(solution)/shard_map/ppermute | solution.py:432
  49.2 1.3 %collective-permute-start.3 = (bf16[416,256]{1,0:T(8,128)(2,1)S(1)}, bf16[416,256]{1,0:T(8,128)(2,1)S(1)}, u32[]{:S(2)}, u32[]{:S(2)}) collective-permute-start(bf16[416,256]{1,0:T(8,128)(2,1)S(1)} %get-tuple-element.22), channel_id=1, source_target_pairs={{32,0},{64,32},{96,64},{112,96},{80,112},{48,80},{16,48},{33,1},{6... | collective-permute-start | bytes 638984 | tf_op jit(solution)/shard_map/ppermute | solution.py:433
  50.5 0.2 subtract_convert_fusion.net_ref
  50.7 0.2 collective-permute-done.1.row_hi
  51.0 1.5 %collective-permute-done.2.col_lo = bf16[400,256]{1,0:T(8,128)(2,1)S(1)} collective-permute-done((bf16[400,256]{1,0:T(8,128)(2,1)S(1)}, bf16[400,256]{1,0:T(8,128)(2,1)S(1)}, u32[]{:S(2)}, u32[]{:S(2)}) %collective-permute-start.2) | collective-permute-done | bytes 204832 | tf_op jit(solution)/shard_map/ppermute | solution.py:432
  52.4 4.5 %collective-permute-done.3.col_hi = bf16[416,256]{1,0:T(8,128)(2,1)S(1)} collective-permute-done((bf16[416,256]{1,0:T(8,128)(2,1)S(1)}, bf16[416,256]{1,0:T(8,128)(2,1)S(1)}, u32[]{:S(2)}, u32[]{:S(2)}) %collective-permute-start.3) | collective-permute-done | bytes 213024 | tf_op jit(solution)/shard_map/ppermute | solution.py:433
  56.9 12.9 %shard_map.93 = (f32[22,176,256]{2,1,0:T(8,128)S(1)}, f32[17,2,8,128]{3,2,1,0:T(8,128)S(1)}, bf16[384,256]{1,0:T(8,128)(2,1)S(1)}, bf16[384,256]{1,0:T(8,128)(2,...) custom-call(s32[2]{0:T(128)S(1)} %pad_add_fusion.place_ref, ...), custom_call_target="tpu_custom_call", output_to_operand_aliasing={{0}: (9, {})} | custom-call | tf_op jit(solution)/shard_map/pallas_call | solution.py:407
  69.9 1.9 %collective-permute-start.4 = (bf16[384,256]{1,0:T(8,128)(2,1)S(1)}, bf16[384,256]{1,0:T(8,128)(2,1)S(1)}, u32[]{:S(2)}, u32[]{:S(2)}) collective-permute-start(bf16[384,256]{1,0:T(8,128)(2,1)S(1)} %get-tuple-element.25), channel_id=1, source_target_pairs={{0,1},{1,2},{2,3},{3,4},{4,5},{5,6},{6,7},{7,8},{8,9},{9,10},{10,1... | collective-permute-start | bytes 589832 | tf_op jit(solution)/shard_map/ppermute | solution.py:430
  71.8 4.5 %collective-permute-start.5 = (bf16[384,256]{1,0:T(8,128)(2,1)S(1)}, bf16[384,256]{1,0:T(8,128)(2,1)S(1)}, u32[]{:S(2)}, u32[]{:S(2)}) collective-permute-start(bf16[384,256]{1,0:T(8,128)(2,1)S(1)} %get-tuple-element.26), channel_id=1, source_target_pairs={{1,0},{2,1},{3,2},{4,3},{5,4},{6,5},{7,6},{8,7},{9,8},{10,9},{11,1... | collective-permute-start | bytes 589832 | tf_op jit(solution)/shard_map/ppermute | solution.py:431
  76.4 3.0 %collective-permute-start.6 = (bf16[384,256]{1,0:T(8,128)(2,1)S(1)}, bf16[384,256]{1,0:T(8,128)(2,1)S(1)}, u32[]{:S(2)}, u32[]{:S(2)}) collective-permute-start(bf16[384,256]{1,0:T(8,128)(2,1)S(1)} %get-tuple-element.27), channel_id=1, source_target_pairs={{0,32},{32,64},{64,96},{96,112},{112,80},{80,48},{48,16},{1,33},{3... | collective-permute-start | bytes 589832 | tf_op jit(solution)/shard_map/ppermute | solution.py:432
  79.4 1.3 %collective-permute-start.7 = (bf16[384,256]{1,0:T(8,128)(2,1)S(1)}, bf16[384,256]{1,0:T(8,128)(2,1)S(1)}, u32[]{:S(2)}, u32[]{:S(2)}) collective-permute-start(bf16[384,256]{1,0:T(8,128)(2,1)S(1)} %get-tuple-element.28), channel_id=1, source_target_pairs={{32,0},{64,32},{96,64},{112,96},{80,112},{48,80},{16,48},{33,1},{6... | collective-permute-start | bytes 589832 | tf_op jit(solution)/shard_map/ppermute | solution.py:433
  80.7 1.8 %collective-permute-done.6.col_lo = bf16[384,256]{1,0:T(8,128)(2,1)S(1)} collective-permute-done((bf16[384,256]{1,0:T(8,128)(2,1)S(1)}, bf16[384,256]{1,0:T(8,128)(2,1)S(1)}, u32[]{:S(2)}, u32[]{:S(2)}) %collective-permute-start.6) | collective-permute-done | bytes 196640 | tf_op jit(solution)/shard_map/ppermute | solution.py:432
  82.5 4.4 %collective-permute-done.7.col_hi = bf16[384,256]{1,0:T(8,128)(2,1)S(1)} collective-permute-done((bf16[384,256]{1,0:T(8,128)(2,1)S(1)}, bf16[384,256]{1,0:T(8,128)(2,1)S(1)}, u32[]{:S(2)}, u32[]{:S(2)}) %collective-permute-start.7) | collective-permute-done | bytes 196640 | tf_op jit(solution)/shard_map/ppermute | solution.py:433
  86.9 13.2 %shard_map.94 = (f32[22,176,256]{2,1,0:T(8,128)S(1)}, f32[8,48,8,128]{3,2,1,0:T(8,128)S(1)}) custom-call(f32[17,2,8,128]{3,2,1,0:T(8,128)S(1)} %get-tuple-element.24.weight_ref, bf16[384,256]{1,0:T(8,128)(2,1)S(1)} %collective-permute-done.4.row_lo, bf16[384,256]{1,0:T(8,128)(2,1)S(1)} %collective-permute-done.5.row_hi, ...), custom_call_target="tpu_custom_call", output_to_operand_aliasing={{0}: (8, {})} | custom-call | tf_op jit(solution)/shard_map/pallas_call | solution.py:407
  100.1 26.1 %all_to_all.10.in_ref = f32[8,48,8,128]{3,2,1,0:T(8,128)S(1)} all-to-all(f32[8,48,8,128]{3,2,1,0:T(8,128)S(1)} %get-tuple-element.30), channel_id=1, replica_groups=mesh['tracer'=8,'tile'=16] {'tracer'}, dimensions={0} | all-to-all | bytes 3145728 | tf_op jit(solution)/shard_map/all_to_all | solution.py:419
  126.2 2.7 %shard_map.95 = f32[3072,128]{1,0:T(8,128)} custom-call(f32[8,48,8,128]{3,2,1,0:T(8,128)S(1)} %all_to_all.10.in_ref), custom_call_target="tpu_custom_call" | custom-call | tf_op jit(solution)/shard_map/pallas_call | solution.py:407
  (15 shorter events, 0.2 us)
Async XLA Ops:
  4.1 7.8 %copy-start.2 = (s32[512,192]{0,1:T(8,128)S(1)}, s32[512,192]{0,1:T(8,128)}, u32[]{:S(2)}) copy-start(s32[512,192]{0,1:T(8,128)} %param.15) | copy-start | bytes 1179652
  4.1 8.1 %copy-start.3 = (s32[512,2]{0,1:T(2,128)S(1)}, s32[512,2]{0,1:T(2,128)}, u32[]{:S(2)}) copy-start(s32[512,2]{0,1:T(2,128)} %param.14) | copy-start | bytes 12292
  4.1 35.2 %all-to-all-start = ((f32[8,56,8,128]{3,2,1,0:T(8,128)}), f32[8,56,8,128]{3,2,1,0:T(8,128)S(1)}, u32[]{:S(2)}, u32[]{:S(2)}) async-start(f32[8,56,8,128]{3,2,1,0:T(8,128)} %shard_map.91), calls=%async_computation | async-start | bytes 3670016 | tf_op jit(solution)/shard_map/all_to_all | solution.py:419
  11.9 27.4 %copy-start.1 = (s32[2]{0:T(128)S(1)}, s32[2]{0:T(128)}, u32[]{:S(2)}) copy-start(s32[2]{0:T(128)} %rec_ref.1) | copy-start | bytes 28
  12.2 44.8 %copy-start = (f32[512]{0:T(512)S(1)}, f32[512]{0:T(512)}, u32[]{:S(2)}) copy-start(f32[512]{0:T(512)} %param.16) | copy-start | bytes 6148
  41.2 9.5 %collective-permute-start = (bf16[400,256]{1,0:T(8,128)(2,1)S(1)}, bf16[400,256]{1,0:T(8,128)(2,1)S(1)}, u32[]{:S(2)}, u32[]{:S(2)}) collective-permute-start(bf16[400,256]{1,0:T(8,128)(2,1)S(1)} %get-tuple-element.19), channel_id=1, source_target_pairs={{0,1},{1,2},{2,3},{3,4},{4,5},{5,6},{6,7},{7,8},{8,9},{9,10},{10,1... | collective-permute-start | bytes 614408 | tf_op jit(solution)/shard_map/ppermute | solution.py:430
  43.2 7.8 %collective-permute-start.1 = (bf16[400,256]{1,0:T(8,128)(2,1)S(1)}, bf16[400,256]{1,0:T(8,128)(2,1)S(1)}, u32[]{:S(2)}, u32[]{:S(2)}) collective-permute-start(bf16[400,256]{1,0:T(8,128)(2,1)S(1)} %get-tuple-element.20), channel_id=1, source_target_pairs={{1,0},{2,1},{3,2},{4,3},{5,4},{6,5},{7,6},{8,7},{9,8},{10,9},{11,1... | collective-permute-start | bytes 614408 | tf_op jit(solution)/shard_map/ppermute | solution.py:431
  47.7 4.7 %collective-permute-start.2 = (bf16[400,256]{1,0:T(8,128)(2,1)S(1)}, bf16[400,256]{1,0:T(8,128)(2,1)S(1)}, u32[]{:S(2)}, u32[]{:S(2)}) collective-permute-start(bf16[400,256]{1,0:T(8,128)(2,1)S(1)} %get-tuple-element.21), channel_id=1, source_target_pairs={{0,32},{32,64},{64,96},{96,112},{112,80},{80,48},{48,16},{1,33},{3... | collective-permute-start | bytes 614408 | tf_op jit(solution)/shard_map/ppermute | solution.py:432
  49.2 7.7 %collective-permute-start.3 = (bf16[416,256]{1,0:T(8,128)(2,1)S(1)}, bf16[416,256]{1,0:T(8,128)(2,1)S(1)}, u32[]{:S(2)}, u32[]{:S(2)}) collective-permute-start(bf16[416,256]{1,0:T(8,128)(2,1)S(1)} %get-tuple-element.22), channel_id=1, source_target_pairs={{32,0},{64,32},{96,64},{112,96},{80,112},{48,80},{16,48},{33,1},{6... | collective-permute-start | bytes 638984 | tf_op jit(solution)/shard_map/ppermute | solution.py:433
  69.9 10.8 %collective-permute-start.4 = (bf16[384,256]{1,0:T(8,128)(2,1)S(1)}, bf16[384,256]{1,0:T(8,128)(2,1)S(1)}, u32[]{:S(2)}, u32[]{:S(2)}) collective-permute-start(bf16[384,256]{1,0:T(8,128)(2,1)S(1)} %get-tuple-element.25), channel_id=1, source_target_pairs={{0,1},{1,2},{2,3},{3,4},{4,5},{5,6},{6,7},{7,8},{8,9},{9,10},{10,1... | collective-permute-start | bytes 589832 | tf_op jit(solution)/shard_map/ppermute | solution.py:430
  71.8 8.9 %collective-permute-start.5 = (bf16[384,256]{1,0:T(8,128)(2,1)S(1)}, bf16[384,256]{1,0:T(8,128)(2,1)S(1)}, u32[]{:S(2)}, u32[]{:S(2)}) collective-permute-start(bf16[384,256]{1,0:T(8,128)(2,1)S(1)} %get-tuple-element.26), channel_id=1, source_target_pairs={{1,0},{2,1},{3,2},{4,3},{5,4},{6,5},{7,6},{8,7},{9,8},{10,9},{11,1... | collective-permute-start | bytes 589832 | tf_op jit(solution)/shard_map/ppermute | solution.py:431
  76.4 6.2 %collective-permute-start.6 = (bf16[384,256]{1,0:T(8,128)(2,1)S(1)}, bf16[384,256]{1,0:T(8,128)(2,1)S(1)}, u32[]{:S(2)}, u32[]{:S(2)}) collective-permute-start(bf16[384,256]{1,0:T(8,128)(2,1)S(1)} %get-tuple-element.27), channel_id=1, source_target_pairs={{0,32},{32,64},{64,96},{96,112},{112,80},{80,48},{48,16},{1,33},{3... | collective-permute-start | bytes 589832 | tf_op jit(solution)/shard_map/ppermute | solution.py:432
  79.4 7.6 %collective-permute-start.7 = (bf16[384,256]{1,0:T(8,128)(2,1)S(1)}, bf16[384,256]{1,0:T(8,128)(2,1)S(1)}, u32[]{:S(2)}, u32[]{:S(2)}) collective-permute-start(bf16[384,256]{1,0:T(8,128)(2,1)S(1)} %get-tuple-element.28), channel_id=1, source_target_pairs={{32,0},{64,32},{96,64},{112,96},{80,112},{48,80},{16,48},{33,1},{6... | collective-permute-start | bytes 589832 | tf_op jit(solution)/shard_map/ppermute | solution.py:433

commit v5 on v4

--- a/solution.py
+++ b/solution.py
@@ -264,10 +264,8 @@
         lane = 16 * (field % 8) + c
         return jnp.broadcast_to(ref_value[:, lane : lane + 1], (8, LANES))
 
-    zero = jnp.zeros((16 * COLS + 16, LANES), F32)
-    z_q[...] = zero
-    z_edge[...] = zero
-    z_flux[...] = zero
+    for ref in (z_q, z_edge, z_flux):
+        ref[...] = jnp.zeros_like(ref)
     first = weight_ref[0, 0]
     for c in range(COLS):
         q = [state[k, cell(c)] for k in range(6)]
@@ -284,8 +282,13 @@
         def weight(field, c):
             return pick(main[field // 8], field, c)
 
-        def z_rows(c, shift=0):
-            return pl.ds(16 * c + 8 + shift, 8)
+        def z_put(ref, c, value):
+            for half in range(2):
+                ref[half, pl.ds(16 * c + 8, 8), :] = value[:, 128 * half : 128 * half + 128]
+
+        def z_get(ref, c, shift):
+            rows = pl.ds(16 * c + 8 + shift, 8)
+            return jnp.concatenate([ref[half, rows, :] for half in range(2)], 1)
 
         loaded, edges = {}, {}
 
@@ -308,7 +311,7 @@
         flux_y = y_face(0)
         for c in range(COLS):
             here = q_at(c)
-            z_q[z_rows(c), :] = here
+            z_put(z_q, c, here)
             flux_y_up = y_face(c + 1)
             q1, q2, q3 = [state[r + 3 + k, cell(c)] for k in (1, 2, 3)]
             new_edge = edge_value(here, q1, q2, q3)
@@ -319,16 +322,16 @@
             )
             flux_x = x_flux[c]
             x_flux[c] = flux_x_up
-            m2, m1 = z_q[z_rows(c, -2), :], z_q[z_rows(c, -1), :]
-            p1, p2 = z_q[z_rows(c, 1), :], z_q[z_rows(c, 2), :]
+            m2, m1, p1, p2 = [z_get(z_q, c, shift) for shift in (-2, -1, 1, 2)]
             edge = edge_value(m2, m1, here, p1)
-            z_edge[z_rows(c), :] = edge
+            z_put(z_edge, c, edge)
             flux_z = face_flux(
                 [weight(ZA + i, c) for i in range(3)],
-                edge, z_edge[z_rows(c, -1), :], edge_value(m1, here, p1, p2), m1, here,
+                edge, z_get(z_edge, c, -1), edge_value(m1, here, p1, p2), m1, here,
             )
-            z_flux[z_rows(c), :] = flux_z
-            total = (flux_x_up - flux_x) + (flux_y_up - flux_y) + (z_flux[z_rows(c, 1), :] - flux_z)
+            z_put(z_flux, c, flux_z)
+            flux_z_up = z_get(z_flux, c, 1)
+            total = (flux_x_up - flux_x) + (flux_y_up - flux_y) + (flux_z_up - flux_z)
             state[r + 3, cell(c)] = (weight(MASS, c) * here - total) * weight(INV, c)
             flux_y = flux_y_up
         return carry
@@ -477,7 +480,7 @@
         [turn],
         (record_of_step, swap(sent)),
     )
-    column = pltpu.VMEM((16 * COLS + 16, LANES), F32)
+    column = pltpu.VMEM((2, 16 * COLS + 16, 128), F32)
     work = [
         pltpu.VMEM((512, reactions), BF16),
         pltpu.VMEM((19, COLS, 8, LANES), F32),

time: 131 us -> 127 us (0.969)
  Pallas kernels: 34.8 us -> 30.7 us
    pallas_call x5, Pallas kernels: 34.8 us -> 30.7 us  [call(): pl.pallas_call(kernel, out_shape=outs, in_specs=specs, out_specs=out_spec...]
where the time goes in v5:
time: 127 us; the launch traced here: 125 us
  waiting for transfers between devices  39.3 us (31%)
  Pallas kernels  30.7 us (24%)
  starting transfers between devices  27.8 us (22%)
  blocking collectives  26.1 us (21%)
    pallas_call x5, Pallas kernels, call(): pl.pallas_call(kernel, out_shape=outs, in_specs=specs, out_specs=out_spec...  30.7 us
    all_to_all x1, waiting for transfers between devices, swap(): return lax.all_to_all(x, 'tracer', split_axis=0, concat_axis=0, tiled=True)  26.9 us
    all_to_all x1, blocking collectives, swap(): return lax.all_to_all(x, 'tracer', split_axis=0, concat_axis=0, tiled=True)  26.1 us
    ppermute x2, starting transfers between devices, halo(): lax.ppermute(row_down, 'tile', back(tiles))  9.08 us
    ppermute x2, waiting for transfers between devices, halo(): lax.ppermute(col_left, 'tracer', back(columns))  8.9 us
    all_to_all x1, starting transfers between devices, swap(): return lax.all_to_all(x, 'tracer', split_axis=0, concat_axis=0, tiled=True)  7.76 us
    ppermute x2, starting transfers between devices, halo(): lax.ppermute(col_right, 'tracer', columns)  4.5 us
    ppermute x2, starting transfers between devices, halo(): lax.ppermute(row_up, 'tile', tiles)  3.84 us
  transfers between devices with their start and end apart: 9, of which 6 were waited for; matrix products, arithmetic and copies ran while one was open for 1% of the time, Pallas kernels for 0%

profile of v5, /device:TPU:16, one launch (start us, length us, event | category | flops | bytes accessed | tf_op | source)
XLA Modules:
  0.0 124.7 jit_solution(17099533832047246202)
XLA Ops:
  0.0 4.1 %shard_map.91 = f32[8,56,8,128]{3,2,1,0:T(8,128)} custom-call(f32[3072,128]{1,0:T(8,128)} %bitcast.16, f32[128,128]{1,0:T(8,128)} %bitcast.17, f32[128,128]{1,0:T(8,128)} %bitcast.18, f32[128,128]{1,0:T(8,128)} %bitcast.19, f32[128,128]{1,0:T(8,128)} %bitcast.20), custom_call_target="tpu_custom_call" | custom-call | tf_op jit(solution)/shard_map/pallas_call | solution.py:410
  4.1 7.8 %all-to-all-start = ((f32[8,56,8,128]{3,2,1,0:T(8,128)}), f32[8,56,8,128]{3,2,1,0:T(8,128)S(1)}, u32[]{:S(2)}, u32[]{:S(2)}) async-start(f32[8,56,8,128]{3,2,1,0:T(8,128)} %shard_map.91), calls=%async_computation | async-start | bytes 3670016 | tf_op jit(solution)/shard_map/all_to_all | solution.py:422
  11.9 0.2 copy.12
  12.2 0.1 iota_compare_fusion.2
  12.4 26.9 %all-to-all-done.in_ref = f32[8,56,8,128]{3,2,1,0:T(8,128)S(1)} async-done(((f32[8,56,8,128]{3,2,1,0:T(8,128)}), f32[8,56,8,128]{3,2,1,0:T(8,128)S(1)}, u32[]{:S(2)}, u32[]{:S(2)}) %all-to-all-start) | async-done | bytes 1835040 | tf_op jit(solution)/shard_map/all_to_all | solution.py:422
  39.3 1.9 %shard_map.92 = (f32[22,176,256]{2,1,0:T(8,128)S(1)}, f32[2,8,8,128]{3,2,1,0:T(8,128)S(1)}, bf16[400,256]{1,0:T(8,128)(2,1)S(1)}, bf16[400,256]{1,0:T(8,128)(2,1...) custom-call(s32[2]{0:T(128)S(1)} %copy-done.1, f32[8,56,8,128]{3,2,1,0:T(8,128)S(1)} %all-to-all-done.in_ref), custom_call_target="tpu_custom_call" | custom-call | tf_op jit(solution)/shard_map/pallas_call | solution.py:410
  41.2 1.9 %collective-permute-start = (bf16[400,256]{1,0:T(8,128)(2,1)S(1)}, bf16[400,256]{1,0:T(8,128)(2,1)S(1)}, u32[]{:S(2)}, u32[]{:S(2)}) collective-permute-start(bf16[400,256]{1,0:T(8,128)(2,1)S(1)} %get-tuple-element.19), channel_id=1, source_target_pairs={{0,1},{1,2},{2,3},{3,4},{4,5},{5,6},{6,7},{7,8},{8,9},{9,10},{10,1... | collective-permute-start | bytes 614408 | tf_op jit(solution)/shard_map/ppermute | solution.py:433
  43.2 4.5 %collective-permute-start.1 = (bf16[400,256]{1,0:T(8,128)(2,1)S(1)}, bf16[400,256]{1,0:T(8,128)(2,1)S(1)}, u32[]{:S(2)}, u32[]{:S(2)}) collective-permute-start(bf16[400,256]{1,0:T(8,128)(2,1)S(1)} %get-tuple-element.20), channel_id=1, source_target_pairs={{1,0},{2,1},{3,2},{4,3},{5,4},{6,5},{7,6},{8,7},{9,8},{10,9},{11,1... | collective-permute-start | bytes 614408 | tf_op jit(solution)/shard_map/ppermute | solution.py:434
  47.7 1.5 %collective-permute-start.2 = (bf16[400,256]{1,0:T(8,128)(2,1)S(1)}, bf16[400,256]{1,0:T(8,128)(2,1)S(1)}, u32[]{:S(2)}, u32[]{:S(2)}) collective-permute-start(bf16[400,256]{1,0:T(8,128)(2,1)S(1)} %get-tuple-element.21), channel_id=1, source_target_pairs={{0,32},{32,64},{64,96},{96,112},{112,80},{80,48},{48,16},{1,33},{3... | collective-permute-start | bytes 614408 | tf_op jit(solution)/shard_map/ppermute | solution.py:435
  49.2 1.3 %collective-permute-start.3 = (bf16[416,256]{1,0:T(8,128)(2,1)S(1)}, bf16[416,256]{1,0:T(8,128)(2,1)S(1)}, u32[]{:S(2)}, u32[]{:S(2)}) collective-permute-start(bf16[416,256]{1,0:T(8,128)(2,1)S(1)} %get-tuple-element.22), channel_id=1, source_target_pairs={{32,0},{64,32},{96,64},{112,96},{80,112},{48,80},{16,48},{33,1},{6... | collective-permute-start | bytes 638984 | tf_op jit(solution)/shard_map/ppermute | solution.py:436
  50.5 0.2 subtract_convert_fusion.net_ref
  50.7 0.2 collective-permute-done.1.row_hi
  51.0 1.5 %collective-permute-done.2.col_lo = bf16[400,256]{1,0:T(8,128)(2,1)S(1)} collective-permute-done((bf16[400,256]{1,0:T(8,128)(2,1)S(1)}, bf16[400,256]{1,0:T(8,128)(2,1)S(1)}, u32[]{:S(2)}, u32[]{:S(2)}) %collective-permute-start.2) | collective-permute-done | bytes 204832 | tf_op jit(solution)/shard_map/ppermute | solution.py:435
  52.4 4.5 %collective-permute-done.3.col_hi = bf16[416,256]{1,0:T(8,128)(2,1)S(1)} collective-permute-done((bf16[416,256]{1,0:T(8,128)(2,1)S(1)}, bf16[416,256]{1,0:T(8,128)(2,1)S(1)}, u32[]{:S(2)}, u32[]{:S(2)}) %collective-permute-start.3) | collective-permute-done | bytes 213024 | tf_op jit(solution)/shard_map/ppermute | solution.py:436
  56.9 10.9 %shard_map.93 = (f32[22,176,256]{2,1,0:T(8,128)S(1)}, f32[17,2,8,128]{3,2,1,0:T(8,128)S(1)}, bf16[384,256]{1,0:T(8,128)(2,1)S(1)}, bf16[384,256]{1,0:T(8,128)(2,...) custom-call(s32[2]{0:T(128)S(1)} %pad_add_fusion.place_ref, ...), custom_call_target="tpu_custom_call", output_to_operand_aliasing={{0}: (9, {})} | custom-call | tf_op jit(solution)/shard_map/pallas_call | solution.py:410
  67.9 1.9 %collective-permute-start.4 = (bf16[384,256]{1,0:T(8,128)(2,1)S(1)}, bf16[384,256]{1,0:T(8,128)(2,1)S(1)}, u32[]{:S(2)}, u32[]{:S(2)}) collective-permute-start(bf16[384,256]{1,0:T(8,128)(2,1)S(1)} %get-tuple-element.25), channel_id=1, source_target_pairs={{0,1},{1,2},{2,3},{3,4},{4,5},{5,6},{6,7},{7,8},{8,9},{9,10},{10,1... | collective-permute-start | bytes 589832 | tf_op jit(solution)/shard_map/ppermute | solution.py:433
  69.8 4.5 %collective-permute-start.5 = (bf16[384,256]{1,0:T(8,128)(2,1)S(1)}, bf16[384,256]{1,0:T(8,128)(2,1)S(1)}, u32[]{:S(2)}, u32[]{:S(2)}) collective-permute-start(bf16[384,256]{1,0:T(8,128)(2,1)S(1)} %get-tuple-element.26), channel_id=1, source_target_pairs={{1,0},{2,1},{3,2},{4,3},{5,4},{6,5},{7,6},{8,7},{9,8},{10,9},{11,1... | collective-permute-start | bytes 589832 | tf_op jit(solution)/shard_map/ppermute | solution.py:434
  74.3 3.0 %collective-permute-start.6 = (bf16[384,256]{1,0:T(8,128)(2,1)S(1)}, bf16[384,256]{1,0:T(8,128)(2,1)S(1)}, u32[]{:S(2)}, u32[]{:S(2)}) collective-permute-start(bf16[384,256]{1,0:T(8,128)(2,1)S(1)} %get-tuple-element.27), channel_id=1, source_target_pairs={{0,32},{32,64},{64,96},{96,112},{112,80},{80,48},{48,16},{1,33},{3... | collective-permute-start | bytes 589832 | tf_op jit(solution)/shard_map/ppermute | solution.py:435
  77.4 1.3 %collective-permute-start.7 = (bf16[384,256]{1,0:T(8,128)(2,1)S(1)}, bf16[384,256]{1,0:T(8,128)(2,1)S(1)}, u32[]{:S(2)}, u32[]{:S(2)}) collective-permute-start(bf16[384,256]{1,0:T(8,128)(2,1)S(1)} %get-tuple-element.28), channel_id=1, source_target_pairs={{32,0},{64,32},{96,64},{112,96},{80,112},{48,80},{16,48},{33,1},{6... | collective-permute-start | bytes 589832 | tf_op jit(solution)/shard_map/ppermute | solution.py:436
  78.7 1.8 %collective-permute-done.6.col_lo = bf16[384,256]{1,0:T(8,128)(2,1)S(1)} collective-permute-done((bf16[384,256]{1,0:T(8,128)(2,1)S(1)}, bf16[384,256]{1,0:T(8,128)(2,1)S(1)}, u32[]{:S(2)}, u32[]{:S(2)}) %collective-permute-start.6) | collective-permute-done | bytes 196640 | tf_op jit(solution)/shard_map/ppermute | solution.py:435
  80.5 4.4 %collective-permute-done.7.col_hi = bf16[384,256]{1,0:T(8,128)(2,1)S(1)} collective-permute-done((bf16[384,256]{1,0:T(8,128)(2,1)S(1)}, bf16[384,256]{1,0:T(8,128)(2,1)S(1)}, u32[]{:S(2)}, u32[]{:S(2)}) %collective-permute-start.7) | collective-permute-done | bytes 196640 | tf_op jit(solution)/shard_map/ppermute | solution.py:436
  84.9 11.1 %shard_map.94 = (f32[22,176,256]{2,1,0:T(8,128)S(1)}, f32[8,48,8,128]{3,2,1,0:T(8,128)S(1)}) custom-call(f32[17,2,8,128]{3,2,1,0:T(8,128)S(1)} %get-tuple-element.24.weight_ref, bf16[384,256]{1,0:T(8,128)(2,1)S(1)} %collective-permute-done.4.row_lo, bf16[384,256]{1,0:T(8,128)(2,1)S(1)} %collective-permute-done.5.row_hi, ...), custom_call_target="tpu_custom_call", output_to_operand_aliasing={{0}: (8, {})} | custom-call | tf_op jit(solution)/shard_map/pallas_call | solution.py:410
  96.0 26.1 %all_to_all.10.in_ref = f32[8,48,8,128]{3,2,1,0:T(8,128)S(1)} all-to-all(f32[8,48,8,128]{3,2,1,0:T(8,128)S(1)} %get-tuple-element.30), channel_id=1, replica_groups=mesh['tracer'=8,'tile'=16] {'tracer'}, dimensions={0} | all-to-all | bytes 3145728 | tf_op jit(solution)/shard_map/all_to_all | solution.py:422
  122.0 2.7 %shard_map.95 = f32[3072,128]{1,0:T(8,128)} custom-call(f32[8,48,8,128]{3,2,1,0:T(8,128)S(1)} %all_to_all.10.in_ref), custom_call_target="tpu_custom_call" | custom-call | tf_op jit(solution)/shard_map/pallas_call | solution.py:410
  (15 shorter events, 0.2 us)
Async XLA Ops:
  4.1 7.8 %copy-start.2 = (s32[512,192]{0,1:T(8,128)S(1)}, s32[512,192]{0,1:T(8,128)}, u32[]{:S(2)}) copy-start(s32[512,192]{0,1:T(8,128)} %param.15) | copy-start | bytes 1179652
  4.1 8.1 %copy-start.3 = (s32[512,2]{0,1:T(2,128)S(1)}, s32[512,2]{0,1:T(2,128)}, u32[]{:S(2)}) copy-start(s32[512,2]{0,1:T(2,128)} %param.14) | copy-start | bytes 12292
  4.1 35.2 %all-to-all-start = ((f32[8,56,8,128]{3,2,1,0:T(8,128)}), f32[8,56,8,128]{3,2,1,0:T(8,128)S(1)}, u32[]{:S(2)}, u32[]{:S(2)}) async-start(f32[8,56,8,128]{3,2,1,0:T(8,128)} %shard_map.91), calls=%async_computation | async-start | bytes 3670016 | tf_op jit(solution)/shard_map/all_to_all | solution.py:422
  11.9 27.4 %copy-start.1 = (s32[2]{0:T(128)S(1)}, s32[2]{0:T(128)}, u32[]{:S(2)}) copy-start(s32[2]{0:T(128)} %rec_ref.1) | copy-start | bytes 28
  12.2 44.8 %copy-start = (f32[512]{0:T(512)S(1)}, f32[512]{0:T(512)}, u32[]{:S(2)}) copy-start(f32[512]{0:T(512)} %param.16) | copy-start | bytes 6148
  41.2 9.5 %collective-permute-start = (bf16[400,256]{1,0:T(8,128)(2,1)S(1)}, bf16[400,256]{1,0:T(8,128)(2,1)S(1)}, u32[]{:S(2)}, u32[]{:S(2)}) collective-permute-start(bf16[400,256]{1,0:T(8,128)(2,1)S(1)} %get-tuple-element.19), channel_id=1, source_target_pairs={{0,1},{1,2},{2,3},{3,4},{4,5},{5,6},{6,7},{7,8},{8,9},{9,10},{10,1... | collective-permute-start | bytes 614408 | tf_op jit(solution)/shard_map/ppermute | solution.py:433
  43.2 7.8 %collective-permute-start.1 = (bf16[400,256]{1,0:T(8,128)(2,1)S(1)}, bf16[400,256]{1,0:T(8,128)(2,1)S(1)}, u32[]{:S(2)}, u32[]{:S(2)}) collective-permute-start(bf16[400,256]{1,0:T(8,128)(2,1)S(1)} %get-tuple-element.20), channel_id=1, source_target_pairs={{1,0},{2,1},{3,2},{4,3},{5,4},{6,5},{7,6},{8,7},{9,8},{10,9},{11,1... | collective-permute-start | bytes 614408 | tf_op jit(solution)/shard_map/ppermute | solution.py:434
  47.7 4.7 %collective-permute-start.2 = (bf16[400,256]{1,0:T(8,128)(2,1)S(1)}, bf16[400,256]{1,0:T(8,128)(2,1)S(1)}, u32[]{:S(2)}, u32[]{:S(2)}) collective-permute-start(bf16[400,256]{1,0:T(8,128)(2,1)S(1)} %get-tuple-element.21), channel_id=1, source_target_pairs={{0,32},{32,64},{64,96},{96,112},{112,80},{80,48},{48,16},{1,33},{3... | collective-permute-start | bytes 614408 | tf_op jit(solution)/shard_map/ppermute | solution.py:435
  49.2 7.7 %collective-permute-start.3 = (bf16[416,256]{1,0:T(8,128)(2,1)S(1)}, bf16[416,256]{1,0:T(8,128)(2,1)S(1)}, u32[]{:S(2)}, u32[]{:S(2)}) collective-permute-start(bf16[416,256]{1,0:T(8,128)(2,1)S(1)} %get-tuple-element.22), channel_id=1, source_target_pairs={{32,0},{64,32},{96,64},{112,96},{80,112},{48,80},{16,48},{33,1},{6... | collective-permute-start | bytes 638984 | tf_op jit(solution)/shard_map/ppermute | solution.py:436
  67.9 10.8 %collective-permute-start.4 = (bf16[384,256]{1,0:T(8,128)(2,1)S(1)}, bf16[384,256]{1,0:T(8,128)(2,1)S(1)}, u32[]{:S(2)}, u32[]{:S(2)}) collective-permute-start(bf16[384,256]{1,0:T(8,128)(2,1)S(1)} %get-tuple-element.25), channel_id=1, source_target_pairs={{0,1},{1,2},{2,3},{3,4},{4,5},{5,6},{6,7},{7,8},{8,9},{9,10},{10,1... | collective-permute-start | bytes 589832 | tf_op jit(solution)/shard_map/ppermute | solution.py:433
  69.8 8.9 %collective-permute-start.5 = (bf16[384,256]{1,0:T(8,128)(2,1)S(1)}, bf16[384,256]{1,0:T(8,128)(2,1)S(1)}, u32[]{:S(2)}, u32[]{:S(2)}) collective-permute-start(bf16[384,256]{1,0:T(8,128)(2,1)S(1)} %get-tuple-element.26), channel_id=1, source_target_pairs={{1,0},{2,1},{3,2},{4,3},{5,4},{6,5},{7,6},{8,7},{9,8},{10,9},{11,1... | collective-permute-start | bytes 589832 | tf_op jit(solution)/shard_map/ppermute | solution.py:434
  74.3 6.2 %collective-permute-start.6 = (bf16[384,256]{1,0:T(8,128)(2,1)S(1)}, bf16[384,256]{1,0:T(8,128)(2,1)S(1)}, u32[]{:S(2)}, u32[]{:S(2)}) collective-permute-start(bf16[384,256]{1,0:T(8,128)(2,1)S(1)} %get-tuple-element.27), channel_id=1, source_target_pairs={{0,32},{32,64},{64,96},{96,112},{112,80},{80,48},{48,16},{1,33},{3... | collective-permute-start | bytes 589832 | tf_op jit(solution)/shard_map/ppermute | solution.py:435
  77.4 7.6 %collective-permute-start.7 = (bf16[384,256]{1,0:T(8,128)(2,1)S(1)}, bf16[384,256]{1,0:T(8,128)(2,1)S(1)}, u32[]{:S(2)}, u32[]{:S(2)}) collective-permute-start(bf16[384,256]{1,0:T(8,128)(2,1)S(1)} %get-tuple-element.28), channel_id=1, source_target_pairs={{32,0},{64,32},{96,64},{112,96},{80,112},{48,80},{16,48},{33,1},{6... | collective-permute-start | bytes 589832 | tf_op jit(solution)/shard_map/ppermute | solution.py:436

commit v6 on v5

--- a/solution.py
+++ b/solution.py
@@ -1,3 +1,5 @@
+import functools
+
 import jax
 import jax.numpy as jnp
 from jax import lax
@@ -14,6 +16,7 @@
 LANES = 256
 ORDER = (0, 2, 4, 6, 7, 5, 3, 1)
 XA, YA, ZA, MASS, INV, WA = 0, 3, 6, 9, 10, 11
+COST = pl.CostEstimate(flops=60_000_000, bytes_accessed=8_000_000, transcendentals=0)
 VMEM = pl.BlockSpec(memory_space=pltpu.VMEM)
 SMEM = pl.BlockSpec(memory_space=pltpu.SMEM)
 ANY = pl.BlockSpec(memory_space=pltpu.HBM)
@@ -195,7 +198,7 @@
     return [flux * (1.0 - c) * (1.0 - c), side * (c - 1.0), side * (3.0 - 2.0 * c)]
 
 
-def write_weights(s, place_ref, weather_ref, row_lo, row_hi, col_lo, col_hi, out_ref):
+def write_weights(s, place_ref, weather_ref, halos, out_ref):
     tile, column = place_ref[0], place_ref[1]
     shape = (8, 128)
     lane = lane_of(shape)
@@ -203,20 +206,28 @@
     level = lax.broadcasted_iota(jnp.int32, shape, 0)
     zero = jnp.zeros(shape, F32)
 
-    def edge(ref, start, s):
-        both = ref[384 + start : 400 + start].astype(F32)[8 * s : 8 * s + 8]
-        return both[:, 0:128], both[:, 128:256]
+    def edge(ref, size):
+        both = ref[384 : 384 + 2 * size].astype(F32)[size * s : size * s + size]
+        return [
+            both[8 * k : 8 * k + 8, 128 * h : 128 * h + 128]
+            for k in range(size // 8)
+            for h in range(2)
+        ]
 
     mass = [weather_ref[s, 0], weather_ref[s, 1]]
     east = [weather_ref[s, 2], weather_ref[s, 3]]
     south = [weather_ref[s, 4], weather_ref[s, 5]]
     bottom = [weather_ref[s, 6], weather_ref[s, 7]]
-    mass_before, _ = edge(row_lo, 0, s)
-    mass_after, east_after = edge(row_hi, 0, s)
-    mass_left = edge(col_lo, 0, s)
-    lefts = col_hi[384:416].astype(F32)[16 * s : 16 * s + 16]
-    mass_right = [lefts[0:8, 128 * h : 128 * h + 128] for h in range(2)]
-    south_right = [lefts[8:16, 128 * h : 128 * h + 128] for h in range(2)]
+    if halos is None:
+        mass_before = mass_after = east_after = zero
+        mass_left = mass_right = south_right = [zero, zero]
+    else:
+        row_lo, row_hi, col_lo, col_hi = halos
+        mass_before = edge(row_lo, 8)[0]
+        mass_after, east_after = edge(row_hi, 8)
+        mass_left = edge(col_lo, 8)
+        mass_right = edge(col_hi, 16)
+        mass_right, south_right = mass_right[0:2], mass_right[2:4]
     east[0] = jnp.where((group == 0) & (tile == 0), 0.0, east[0])
     mass_rows = [mass_before] + mass + [mass_after]
     east_rows = east + [east_after]
@@ -259,28 +270,21 @@
     return a * edge + b * jnp.where(forward, below, above) + c * jnp.where(forward, q_low, q_up)
 
 
-def advect(state, weight_ref, x_edges, x_flux, z_q, z_edge, z_flux):
-    def pick(ref_value, field, c):
-        lane = 16 * (field % 8) + c
-        return jnp.broadcast_to(ref_value[:, lane : lane + 1], (8, LANES))
-
+def pick(vector, field, c):
+    lane = 16 * (field % 8) + c
+    return jnp.broadcast_to(vector[:, lane : lane + 1], (8, LANES))
+
+
+def advect_inner(state, weight_ref, partial, x_edges, x_flux, z_q, z_edge, z_flux):
     for ref in (z_q, z_edge, z_flux):
         ref[...] = jnp.zeros_like(ref)
-    first = weight_ref[0, 0]
-    for c in range(COLS):
-        q = [state[k, cell(c)] for k in range(6)]
-        edges = [edge_value(*q[k : k + 4]) for k in range(3)]
-        for k in range(3):
-            x_edges[k, c] = edges[k]
-        weights = [pick(first, XA + i, c) for i in range(3)]
-        x_flux[c] = face_flux(weights, edges[1], edges[0], edges[2], q[2], q[3])
-
-    def row(r, carry):
+
+    def row(with_x, r, carry):
         main = [weight_ref[r, 0], weight_ref[r, 1]]
         ahead = weight_ref[r + 1, 0]
 
-        def weight(field, c):
-            return pick(main[field // 8], field, c)
+        def weights(field, c):
+            return [pick(main[(field + i) // 8], field + i, c) for i in range(3)]
 
         def z_put(ref, c, value):
             for half in range(2):
@@ -303,37 +307,91 @@
             return edges[c]
 
         def y_face(c):
-            weights = [weight(YA + i, c) if c < COLS else weight(WA + i, 0) for i in range(3)]
             return face_flux(
-                weights, y_edge(c), y_edge(c - 1), y_edge(c + 1), q_at(c - 1), q_at(c)
+                weights(YA, c), y_edge(c), y_edge(c - 1), y_edge(c + 1), q_at(c - 1), q_at(c)
             )
 
-        flux_y = y_face(0)
+        flux_y = None
         for c in range(COLS):
             here = q_at(c)
             z_put(z_q, c, here)
-            flux_y_up = y_face(c + 1)
-            q1, q2, q3 = [state[r + 3 + k, cell(c)] for k in (1, 2, 3)]
-            new_edge = edge_value(here, q1, q2, q3)
-            x_edges[r + 3, c] = new_edge
-            flux_x_up = face_flux(
-                [pick(ahead, XA + i, c) for i in range(3)],
-                x_edges[r + 2, c], x_edges[r + 1, c], new_edge, here, q1,
-            )
-            flux_x = x_flux[c]
-            x_flux[c] = flux_x_up
             m2, m1, p1, p2 = [z_get(z_q, c, shift) for shift in (-2, -1, 1, 2)]
             edge = edge_value(m2, m1, here, p1)
             z_put(z_edge, c, edge)
             flux_z = face_flux(
-                [weight(ZA + i, c) for i in range(3)],
-                edge, z_get(z_edge, c, -1), edge_value(m1, here, p1, p2), m1, here,
+                weights(ZA, c), edge, z_get(z_edge, c, -1), edge_value(m1, here, p1, p2), m1, here
             )
             z_put(z_flux, c, flux_z)
-            flux_z_up = z_get(z_flux, c, 1)
-            total = (flux_x_up - flux_x) + (flux_y_up - flux_y) + (flux_z_up - flux_z)
-            state[r + 3, cell(c)] = (weight(MASS, c) * here - total) * weight(INV, c)
-            flux_y = flux_y_up
+            total = z_get(z_flux, c, 1) - flux_z
+            if 3 <= c <= 12:
+                flux_y = y_face(3) if c == 3 else flux_y
+                flux_y_up = y_face(c + 1)
+                total = total + (flux_y_up - flux_y)
+                flux_y = flux_y_up
+            if with_x:
+                q1, q2, q3 = [state[r + 3 + k, cell(c)] for k in (1, 2, 3)]
+                new_edge = edge_value(here, q1, q2, q3)
+                x_edges[r + 3, c] = new_edge
+                flux_x_up = face_flux(
+                    [pick(ahead, XA + i, c) for i in range(3)],
+                    x_edges[r + 2, c], x_edges[r + 1, c], new_edge, here, q1,
+                )
+                total = total + (flux_x_up - x_flux[c])
+                x_flux[c] = flux_x_up
+            partial[r, c] = pick(main[MASS // 8], MASS, c) * here - total
+        return carry
+
+    third = weight_ref[3, 0]
+    for c in range(COLS):
+        q = [state[3 + k, cell(c)] for k in range(6)]
+        edges = [edge_value(*q[k : k + 4]) for k in range(3)]
+        for k in range(3):
+            x_edges[3 + k, c] = edges[k]
+        weights = [pick(third, XA + i, c) for i in range(3)]
+        x_flux[c] = face_flux(weights, edges[1], edges[0], edges[2], q[2], q[3])
+    lax.fori_loop(3, 13, functools.partial(row, True), 0)
+    lax.fori_loop(0, 6, lambda k, carry: row(False, jnp.where(k < 3, k, k + 10), carry), 0)
+
+
+def four_faces(q, weights):
+    edges = [edge_value(*q[k : k + 4]) for k in range(6)]
+    flux = [
+        face_flux(weights[k], edges[k + 1], edges[k], edges[k + 2], q[k + 2], q[k + 3])
+        for k in range(4)
+    ]
+    return [flux[k + 1] - flux[k] for k in range(3)]
+
+
+def advect_outer(state, weight_ref, partial):
+    def x_side(side, carry):
+        base = 13 * side
+        vectors = [weight_ref[base + k, 0] for k in range(4)]
+        for c in range(COLS):
+            q = [state[base + k, cell(c)] for k in range(9)]
+            weights = [[pick(vector, XA + i, c) for i in range(3)] for vector in vectors]
+            for k, value in enumerate(four_faces(q, weights)):
+                partial[base + k, c] -= value
+        return carry
+
+    lax.fori_loop(0, 2, x_side, 0)
+
+    def row(r, carry):
+        main = [weight_ref[r, 0], weight_ref[r, 1]]
+
+        def weights(c):
+            field, place = (YA, c) if c < COLS else (WA, 0)
+            return [pick(main[(field + i) // 8], field + i, place) for i in range(3)]
+
+        found = {}
+        for base in (0, 13):
+            q = [state[r + 3, cell(base - 3 + k)] for k in range(9)]
+            for k, value in enumerate(four_faces(q, [weights(base + j) for j in range(4)])):
+                found[base + k] = value
+        for c in range(COLS):
+            value = partial[r, c]
+            if c in found:
+                value = value - found[c]
+            state[r + 3, cell(c)] = value * pick(main[INV // 8], INV, c)
         return carry
 
     lax.fori_loop(0, ROWS, row, 0)
@@ -360,27 +418,37 @@
     lax.fori_loop(0, ROWS // 4, block, 0)
 
 
+def first_inner_kernel(place_ref, weather_ref, state, partial, weight_ref, *work):
+    write_weights(0, place_ref, weather_ref, None, weight_ref)
+    advect_inner(state, weight_ref, partial, *work)
+
+
+def second_inner_kernel(weight_ref, state, partial, *work):
+    advect_inner(state, weight_ref, partial, *work)
+
+
 def first_kernel(
-    place_ref, weather_ref, row_lo, row_hi, col_lo, col_hi, sel_ref, net_ref, coeff_ref, in_ref,
-    state, later_ref, row_up, row_down, col_right, col_left, now_ref, rate_ref, *work
+    place_ref, weather_ref, row_lo, row_hi, col_lo, col_hi, sel_ref, net_ref, coeff_ref,
+    in_ref, partial_ref,
+    state, partial, later_ref, row_up, row_down, col_right, col_left, now_ref, rate_ref,
 ):
-    del in_ref
+    del in_ref, partial_ref
     halos = (row_lo, row_hi, col_lo, col_hi)
     for s, ref in enumerate((now_ref, later_ref)):
-        write_weights(s, place_ref, weather_ref, *halos, ref)
+        write_weights(s, place_ref, weather_ref, halos, ref)
     read_edges(state, *halos)
-    advect(state, now_ref, *work)
+    advect_outer(state, now_ref, partial)
     react(state, sel_ref, net_ref, coeff_ref, rate_ref)
     write_edges(state, row_up, row_down, col_right, col_left)
 
 
 def second_kernel(
-    weight_ref, row_lo, row_hi, col_lo, col_hi, sel_ref, net_ref, coeff_ref, in_ref,
-    state, out_ref, turn_ref, rate_ref, *work
+    weight_ref, row_lo, row_hi, col_lo, col_hi, sel_ref, net_ref, coeff_ref, in_ref, partial_ref,
+    state, partial, out_ref, turn_ref, rate_ref,
 ):
-    del in_ref
+    del in_ref, partial_ref
     read_edges(state, row_lo, row_hi, col_lo, col_hi)
-    advect(state, weight_ref, *work)
+    advect_outer(state, weight_ref, partial)
     react(state, sel_ref, net_ref, coeff_ref, rate_ref)
 
     def row(r, carry):
@@ -405,7 +473,7 @@
     return jax.ShapeDtypeStruct(lead + (8, 128), F32)
 
 
-def call(kernel, outs, specs, scratch=(), args=(), aliases=None, out_spec=VMEM, grant=40 * 2**20):
+def call(kernel, outs, specs, scratch=(), args=(), aliases=None, out_spec=VMEM, grant=40 * 2**20, cost=None):
     single = not isinstance(outs, (list, tuple))
     return pl.pallas_call(
         kernel,
@@ -414,6 +482,7 @@
         out_specs=out_spec if single else [VMEM] * len(outs),
         scratch_shapes=list(scratch),
         input_output_aliases=aliases or {},
+        cost_estimate=cost,
         compiler_params=pltpu.CompilerParams(vmem_limit_bytes=grant),
     )(*args)
 
@@ -482,27 +551,38 @@
     )
     column = pltpu.VMEM((2, 16 * COLS + 16, 128), F32)
     work = [
-        pltpu.VMEM((512, reactions), BF16),
         pltpu.VMEM((19, COLS, 8, LANES), F32),
         pltpu.VMEM((COLS, 8, LANES), F32),
         column, column, column,
     ]
+    rates = pltpu.VMEM((512, reactions), BF16)
     weights = (ROWS + 1, 2, 8, 128)
-    state, later, *edges = call(
+    partial_shape = jax.ShapeDtypeStruct((ROWS, COLS, 8, LANES), F32)
+    halos = halo(*edges)
+    partial = call(
+        first_inner_kernel, partial_shape, [SMEM] + [VMEM] * 2,
+        [pltpu.VMEM(weights, F32)] + work, (place, weather, state), cost=COST,
+    )
+    state, _, later, *edges = call(
         first_kernel,
-        [state_shape, jax.ShapeDtypeStruct(weights, F32)] + edge_blocks(384, 384, 384, 384),
-        [SMEM] + [VMEM] * 9,
-        [pltpu.VMEM(weights, F32)] + work,
-        (place, weather) + halo(*edges) + constants + (state,),
-        {9: 0},
-    )
-    _, sent = call(
+        [state_shape, partial_shape, jax.ShapeDtypeStruct(weights, F32)]
+        + edge_blocks(384, 384, 384, 384),
+        [SMEM] + [VMEM] * 10,
+        [pltpu.VMEM(weights, F32), rates],
+        (place, weather) + halos + constants + (state, partial),
+        {9: 0, 10: 1},
+    )
+    halos = halo(*edges)
+    partial = call(
+        second_inner_kernel, partial_shape, [VMEM] * 2, work, (later, state), cost=COST
+    )
+    _, _, sent = call(
         second_kernel,
-        [state_shape, blocks(8, 48)],
-        [VMEM] * 9,
-        [turn] + work,
-        (later,) + halo(*edges) + constants + (state,),
-        {8: 0},
+        [state_shape, partial_shape, blocks(8, 48)],
+        [VMEM] * 10,
+        [turn, rates],
+        (later,) + halos + constants + (state, partial),
+        {8: 0, 9: 1},
     )
     out = call(
         unpack_kernel,

time: 127 us -> 121 us (0.953); the launches traced: 125 us -> 121 us
  waiting for transfers between devices: 39.3 us -> 27.8 us
  Pallas kernels: 30.7 us -> 34.3 us
  blocking collectives: 26.1 us -> 28.2 us
  starting transfers between devices: 27.8 us -> 29.3 us
    ppermute x2, waiting for transfers between devices: 8.9 us -> 0.96 us  [halo(): lax.ppermute(col_left, 'tracer', back(columns))]
    pallas_call x5 -> x7, Pallas kernels: 30.7 us -> 34.3 us  [call(): pl.pallas_call(kernel, out_shape=outs, in_specs=specs, out_specs=out_spec...]
    ppermute x2, waiting for transfers between devices: 3.33 us -> 0.01 us  [halo(): lax.ppermute(col_right, 'tracer', columns)]
    all_to_all x1, blocking collectives: 26.1 us -> 28.2 us  [swap(): return lax.all_to_all(x, 'tracer', split_axis=0, concat_axis=0, tiled=True)]
    ppermute x2, starting transfers between devices: 4.5 us -> 6.05 us  [halo(): lax.ppermute(col_right, 'tracer', columns)]
  transfers between devices with their start and end apart: 9 -> 9, of which waited for: 6 -> 2; matrix products, arithmetic and copies ran while one was open for 1% -> 1% of each run, Pallas kernels for 0% -> 10%
where the time goes in v6:
time: 121 us
  Pallas kernels  34.3 us (28%)
  starting transfers between devices  29.3 us (24%)
  blocking collectives  28.2 us (23%)
  waiting for transfers between devices  27.8 us (23%)
    pallas_call x7, Pallas kernels, call(): pl.pallas_call(kernel, out_shape=outs, in_specs=specs, out_specs=out_spec...  34.3 us
    all_to_all x1, blocking collectives, swap(): return lax.all_to_all(x, 'tracer', split_axis=0, concat_axis=0, tiled=True)  28.2 us
    all_to_all x1, waiting for transfers between devices, swap(): return lax.all_to_all(x, 'tracer', split_axis=0, concat_axis=0, tiled=True)  26.9 us
    ppermute x2, starting transfers between devices, halo(): lax.ppermute(row_down, 'tile', back(tiles))  9.08 us
    all_to_all x1, starting transfers between devices, swap(): return lax.all_to_all(x, 'tracer', split_axis=0, concat_axis=0, tiled=True)  7.76 us
    ppermute x2, starting transfers between devices, halo(): lax.ppermute(col_right, 'tracer', columns)  6.05 us
    ppermute x2, starting transfers between devices, halo(): lax.ppermute(row_up, 'tile', tiles)  3.84 us
    ppermute x2, starting transfers between devices, halo(): lax.ppermute(col_left, 'tracer', back(columns))  2.58 us
  transfers between devices with their start and end apart: 9, of which 2 were waited for; matrix products, arithmetic and copies ran while one was open for 1% of the time, Pallas kernels for 10%

profile of v6, /device:TPU:16, one launch (start us, length us, event | category | flops | bytes accessed | tf_op | source)
XLA Modules:
  0.0 120.6 jit_solution(15853591408790517818)
XLA Ops:
  0.0 4.1 %shard_map.91 = f32[8,56,8,128]{3,2,1,0:T(8,128)} custom-call(f32[3072,128]{1,0:T(8,128)} %bitcast.16, f32[128,128]{1,0:T(8,128)} %bitcast.17, f32[128,128]{1,0:T(8,128)} %bitcast.18, f32[128,128]{1,0:T(8,128)} %bitcast.19, f32[128,128]{1,0:T(8,128)} %bitcast.20), custom_call_target="tpu_custom_call" | custom-call | tf_op jit(solution)/shard_map/pallas_call | solution.py:478
  4.1 7.8 %all-to-all-start = ((f32[8,56,8,128]{3,2,1,0:T(8,128)}), f32[8,56,8,128]{3,2,1,0:T(8,128)S(1)}, u32[]{:S(2)}, u32[]{:S(2)}) async-start(f32[8,56,8,128]{3,2,1,0:T(8,128)} %shard_map.91), calls=%async_computation | async-start | bytes 3670016 | tf_op jit(solution)/shard_map/all_to_all | solution.py:491
  11.9 0.2 copy.14
  12.1 0.1 pad_add_fusion.place_ref
  12.2 0.1 iota_compare_fusion.2
  12.3 0.1 add_convert_fusion.sel_ref
  12.4 26.9 %all-to-all-done.in_ref = f32[8,56,8,128]{3,2,1,0:T(8,128)S(1)} async-done(((f32[8,56,8,128]{3,2,1,0:T(8,128)}), f32[8,56,8,128]{3,2,1,0:T(8,128)S(1)}, u32[]{:S(2)}, u32[]{:S(2)}) %all-to-all-start) | async-done | bytes 1835040 | tf_op jit(solution)/shard_map/all_to_all | solution.py:491
  39.3 1.9 %shard_map.92 = (f32[22,176,256]{2,1,0:T(8,128)S(1)}, f32[2,8,8,128]{3,2,1,0:T(8,128)S(1)}, bf16[400,256]{1,0:T(8,128)(2,1)S(1)}, bf16[400,256]{1,0:T(8,128)(2,1...) custom-call(s32[2]{0:T(128)S(1)} %copy-done.1, f32[8,56,8,128]{3,2,1,0:T(8,128)S(1)} %all-to-all-done.in_ref), custom_call_target="tpu_custom_call" | custom-call | tf_op jit(solution)/shard_map/pallas_call | solution.py:478
  41.2 1.9 %collective-permute-start = (bf16[400,256]{1,0:T(8,128)(2,1)S(1)}, bf16[400,256]{1,0:T(8,128)(2,1)S(1)}, u32[]{:S(2)}, u32[]{:S(2)}) collective-permute-start(bf16[400,256]{1,0:T(8,128)(2,1)S(1)} %get-tuple-element.19), channel_id=1, source_target_pairs={{0,1},{1,2},{2,3},{3,4},{4,5},{5,6},{6,7},{7,8},{8,9},{9,10},{10,1... | collective-permute-start | bytes 614408 | tf_op jit(solution)/shard_map/ppermute | solution.py:502
  43.2 4.5 %collective-permute-start.1 = (bf16[400,256]{1,0:T(8,128)(2,1)S(1)}, bf16[400,256]{1,0:T(8,128)(2,1)S(1)}, u32[]{:S(2)}, u32[]{:S(2)}) collective-permute-start(bf16[400,256]{1,0:T(8,128)(2,1)S(1)} %get-tuple-element.20), channel_id=1, source_target_pairs={{1,0},{2,1},{3,2},{4,3},{5,4},{6,5},{7,6},{8,7},{9,8},{10,9},{11,1... | collective-permute-start | bytes 614408 | tf_op jit(solution)/shard_map/ppermute | solution.py:503
  47.7 1.5 %collective-permute-start.2 = (bf16[400,256]{1,0:T(8,128)(2,1)S(1)}, bf16[400,256]{1,0:T(8,128)(2,1)S(1)}, u32[]{:S(2)}, u32[]{:S(2)}) collective-permute-start(bf16[400,256]{1,0:T(8,128)(2,1)S(1)} %get-tuple-element.21), channel_id=1, source_target_pairs={{0,32},{32,64},{64,96},{96,112},{112,80},{80,48},{48,16},{1,33},{3... | collective-permute-start | bytes 614408 | tf_op jit(solution)/shard_map/ppermute | solution.py:504
  49.2 1.3 %collective-permute-start.3 = (bf16[416,256]{1,0:T(8,128)(2,1)S(1)}, bf16[416,256]{1,0:T(8,128)(2,1)S(1)}, u32[]{:S(2)}, u32[]{:S(2)}) collective-permute-start(bf16[416,256]{1,0:T(8,128)(2,1)S(1)} %get-tuple-element.22), channel_id=1, source_target_pairs={{32,0},{64,32},{96,64},{112,96},{80,112},{48,80},{16,48},{33,1},{6... | collective-permute-start | bytes 638984 | tf_op jit(solution)/shard_map/ppermute | solution.py:505
  50.5 0.2 subtract_convert_fusion.net_ref
  50.7 6.3 %shard_map.93.partial_ref = f32[16,16,8,256]{3,2,1,0:T(8,128)S(1)} custom-call(s32[2]{0:T(128)S(1)} %pad_add_fusion.place_ref, f32[2,8,8,128]{3,2,1,0:T(8,128)S(1)} %get-tuple-element.18.weather_ref, f32[22,176,256]{2,1,0:T(8,128)S(1)} %get-tuple-element.23.state.in_ref), custom_call_target="tpu_custom_call" | custom-call | flops 60000000 | bytes 8000000 | tf_op jit(solution)/shard_map/pallas_call | solution.py:478
  57.1 6.9 %shard_map.94 = (f32[22,176,256]{2,1,0:T(8,128)S(1)}, f32[16,16,8,256]{3,2,1,0:T(8,128)S(1)}, f32[17,2,8,128]{3,2,1,0:T(8,128)S(1)}, bf16[384,256]{1,0:T(8,128)(...) custom-call(s32[2]{0:T(128)S(1)} %pad_add_fusion.place_ref, ...), custom_call_target="tpu_custom_call", output_to_operand_aliasing={{0}: (9, {}), {1}: (10, {})} | custom-call | tf_op jit(solution)/shard_map/pallas_call | solution.py:478
  63.9 1.9 %collective-permute-start.4 = (bf16[384,256]{1,0:T(8,128)(2,1)S(1)}, bf16[384,256]{1,0:T(8,128)(2,1)S(1)}, u32[]{:S(2)}, u32[]{:S(2)}) collective-permute-start(bf16[384,256]{1,0:T(8,128)(2,1)S(1)} %get-tuple-element.25), channel_id=1, source_target_pairs={{0,1},{1,2},{2,3},{3,4},{4,5},{5,6},{6,7},{7,8},{8,9},{9,10},{10,1... | collective-permute-start | bytes 589832 | tf_op jit(solution)/shard_map/ppermute | solution.py:502
  65.9 4.5 %collective-permute-start.5 = (bf16[384,256]{1,0:T(8,128)(2,1)S(1)}, bf16[384,256]{1,0:T(8,128)(2,1)S(1)}, u32[]{:S(2)}, u32[]{:S(2)}) collective-permute-start(bf16[384,256]{1,0:T(8,128)(2,1)S(1)} %get-tuple-element.26), channel_id=1, source_target_pairs={{1,0},{2,1},{3,2},{4,3},{5,4},{6,5},{7,6},{8,7},{9,8},{10,9},{11,1... | collective-permute-start | bytes 589832 | tf_op jit(solution)/shard_map/ppermute | solution.py:503
  70.4 4.6 %collective-permute-start.6 = (bf16[384,256]{1,0:T(8,128)(2,1)S(1)}, bf16[384,256]{1,0:T(8,128)(2,1)S(1)}, u32[]{:S(2)}, u32[]{:S(2)}) collective-permute-start(bf16[384,256]{1,0:T(8,128)(2,1)S(1)} %get-tuple-element.27), channel_id=1, source_target_pairs={{0,32},{32,64},{64,96},{96,112},{112,80},{80,48},{48,16},{1,33},{3... | collective-permute-start | bytes 589832 | tf_op jit(solution)/shard_map/ppermute | solution.py:504
  75.0 1.3 %collective-permute-start.7 = (bf16[384,256]{1,0:T(8,128)(2,1)S(1)}, bf16[384,256]{1,0:T(8,128)(2,1)S(1)}, u32[]{:S(2)}, u32[]{:S(2)}) collective-permute-start(bf16[384,256]{1,0:T(8,128)(2,1)S(1)} %get-tuple-element.28), channel_id=1, source_target_pairs={{32,0},{64,32},{96,64},{112,96},{80,112},{48,80},{16,48},{33,1},{6... | collective-permute-start | bytes 589832 | tf_op jit(solution)/shard_map/ppermute | solution.py:505
  76.3 5.3 %shard_map.95.partial_ref = f32[16,16,8,256]{3,2,1,0:T(8,128)S(1)} custom-call(f32[17,2,8,128]{3,2,1,0:T(8,128)S(1)} %get-tuple-element.24.weight_ref, f32[22,176,256]{2,1,0:T(8,128)S(1)} %get-tuple-element.29.state.in_ref), custom_call_target="tpu_custom_call" | custom-call | flops 60000000 | bytes 8000000 | tf_op jit(solution)/shard_map/pallas_call | solution.py:478
  81.6 1.0 collective-permute-done.7.col_hi
  82.5 7.2 %shard_map.96 = (f32[22,176,256]{2,1,0:T(8,128)S(1)}, f32[16,16,8,256]{3,2,1,0:T(8,128)S(1)}, f32[8,48,8,128]{3,2,1,0:T(8,128)S(1)}) custom-call(f32[17,2,8,128]{3,2,1,0:T(8,128)S(1)} %get-tuple-element.24.weight_ref, bf16[384,256]{1,0:T(8,128)(2,1)S(1)} %collective-permute-done.4.row_lo, ...), custom_call_target="tpu_custom_call", output_to_operand_aliasing={{0}: (8, {}), {1}: (9, {})} | custom-call | tf_op jit(solution)/shard_map/pallas_call | solution.py:478
  89.7 28.2 %all_to_all.10.in_ref = f32[8,48,8,128]{3,2,1,0:T(8,128)S(1)} all-to-all(f32[8,48,8,128]{3,2,1,0:T(8,128)S(1)} %get-tuple-element.30), channel_id=1, replica_groups=mesh['tracer'=8,'tile'=16] {'tracer'}, dimensions={0} | all-to-all | bytes 3145728 | tf_op jit(solution)/shard_map/all_to_all | solution.py:491
  117.9 2.7 %shard_map.97 = f32[3072,128]{1,0:T(8,128)} custom-call(f32[8,48,8,128]{3,2,1,0:T(8,128)S(1)} %all_to_all.10.in_ref), custom_call_target="tpu_custom_call" | custom-call | tf_op jit(solution)/shard_map/pallas_call | solution.py:478
  (17 shorter events, 0.1 us)
Async XLA Ops:
  4.1 7.8 %copy-start.2 = (s32[512,192]{0,1:T(8,128)S(1)}, s32[512,192]{0,1:T(8,128)}, u32[]{:S(2)}) copy-start(s32[512,192]{0,1:T(8,128)} %param.15) | copy-start | bytes 1179652
  4.1 8.1 %copy-start.3 = (s32[512,2]{0,1:T(2,128)S(1)}, s32[512,2]{0,1:T(2,128)}, u32[]{:S(2)}) copy-start(s32[512,2]{0,1:T(2,128)} %param.14) | copy-start | bytes 12292
  4.1 35.2 %copy-start.1 = (s32[2]{0:T(128)S(1)}, s32[2]{0:T(128)}, u32[]{:S(2)}) copy-start(s32[2]{0:T(128)} %rec_ref.1) | copy-start | bytes 28
  4.1 35.2 %all-to-all-start = ((f32[8,56,8,128]{3,2,1,0:T(8,128)}), f32[8,56,8,128]{3,2,1,0:T(8,128)S(1)}, u32[]{:S(2)}, u32[]{:S(2)}) async-start(f32[8,56,8,128]{3,2,1,0:T(8,128)} %shard_map.91), calls=%async_computation | async-start | bytes 3670016 | tf_op jit(solution)/shard_map/all_to_all | solution.py:491
  41.2 15.8 %collective-permute-start = (bf16[400,256]{1,0:T(8,128)(2,1)S(1)}, bf16[400,256]{1,0:T(8,128)(2,1)S(1)}, u32[]{:S(2)}, u32[]{:S(2)}) collective-permute-start(bf16[400,256]{1,0:T(8,128)(2,1)S(1)} %get-tuple-element.19), channel_id=1, source_target_pairs={{0,1},{1,2},{2,3},{3,4},{4,5},{5,6},{6,7},{7,8},{8,9},{9,10},{10,1... | collective-permute-start | bytes 614408 | tf_op jit(solution)/shard_map/ppermute | solution.py:502
  43.2 13.9 %collective-permute-start.1 = (bf16[400,256]{1,0:T(8,128)(2,1)S(1)}, bf16[400,256]{1,0:T(8,128)(2,1)S(1)}, u32[]{:S(2)}, u32[]{:S(2)}) collective-permute-start(bf16[400,256]{1,0:T(8,128)(2,1)S(1)} %get-tuple-element.20), channel_id=1, source_target_pairs={{1,0},{2,1},{3,2},{4,3},{5,4},{6,5},{7,6},{8,7},{9,8},{10,9},{11,1... | collective-permute-start | bytes 614408 | tf_op jit(solution)/shard_map/ppermute | solution.py:503
  47.7 9.3 %collective-permute-start.2 = (bf16[400,256]{1,0:T(8,128)(2,1)S(1)}, bf16[400,256]{1,0:T(8,128)(2,1)S(1)}, u32[]{:S(2)}, u32[]{:S(2)}) collective-permute-start(bf16[400,256]{1,0:T(8,128)(2,1)S(1)} %get-tuple-element.21), channel_id=1, source_target_pairs={{0,32},{32,64},{64,96},{96,112},{112,80},{80,48},{48,16},{1,33},{3... | collective-permute-start | bytes 614408 | tf_op jit(solution)/shard_map/ppermute | solution.py:504
  49.2 7.8 %collective-permute-start.3 = (bf16[416,256]{1,0:T(8,128)(2,1)S(1)}, bf16[416,256]{1,0:T(8,128)(2,1)S(1)}, u32[]{:S(2)}, u32[]{:S(2)}) collective-permute-start(bf16[416,256]{1,0:T(8,128)(2,1)S(1)} %get-tuple-element.22), channel_id=1, source_target_pairs={{32,0},{64,32},{96,64},{112,96},{80,112},{48,80},{16,48},{33,1},{6... | collective-permute-start | bytes 638984 | tf_op jit(solution)/shard_map/ppermute | solution.py:505
  50.7 6.3 %copy-start = (f32[512]{0:T(512)S(1)}, f32[512]{0:T(512)}, u32[]{:S(2)}) copy-start(f32[512]{0:T(512)} %param.16) | copy-start | bytes 6148
  63.9 17.6 %collective-permute-start.4 = (bf16[384,256]{1,0:T(8,128)(2,1)S(1)}, bf16[384,256]{1,0:T(8,128)(2,1)S(1)}, u32[]{:S(2)}, u32[]{:S(2)}) collective-permute-start(bf16[384,256]{1,0:T(8,128)(2,1)S(1)} %get-tuple-element.25), channel_id=1, source_target_pairs={{0,1},{1,2},{2,3},{3,4},{4,5},{5,6},{6,7},{7,8},{8,9},{9,10},{10,1... | collective-permute-start | bytes 589832 | tf_op jit(solution)/shard_map/ppermute | solution.py:502
  65.9 15.7 %collective-permute-start.5 = (bf16[384,256]{1,0:T(8,128)(2,1)S(1)}, bf16[384,256]{1,0:T(8,128)(2,1)S(1)}, u32[]{:S(2)}, u32[]{:S(2)}) collective-permute-start(bf16[384,256]{1,0:T(8,128)(2,1)S(1)} %get-tuple-element.26), channel_id=1, source_target_pairs={{1,0},{2,1},{3,2},{4,3},{5,4},{6,5},{7,6},{8,7},{9,8},{10,9},{11,1... | collective-permute-start | bytes 589832 | tf_op jit(solution)/shard_map/ppermute | solution.py:503
  70.4 11.2 %collective-permute-start.6 = (bf16[384,256]{1,0:T(8,128)(2,1)S(1)}, bf16[384,256]{1,0:T(8,128)(2,1)S(1)}, u32[]{:S(2)}, u32[]{:S(2)}) collective-permute-start(bf16[384,256]{1,0:T(8,128)(2,1)S(1)} %get-tuple-element.27), channel_id=1, source_target_pairs={{0,32},{32,64},{64,96},{96,112},{112,80},{80,48},{48,16},{1,33},{3... | collective-permute-start | bytes 589832 | tf_op jit(solution)/shard_map/ppermute | solution.py:504
  75.0 7.6 %collective-permute-start.7 = (bf16[384,256]{1,0:T(8,128)(2,1)S(1)}, bf16[384,256]{1,0:T(8,128)(2,1)S(1)}, u32[]{:S(2)}, u32[]{:S(2)}) collective-permute-start(bf16[384,256]{1,0:T(8,128)(2,1)S(1)} %get-tuple-element.28), channel_id=1, source_target_pairs={{32,0},{64,32},{96,64},{112,96},{80,112},{48,80},{16,48},{33,1},{6... | collective-permute-start | bytes 589832 | tf_op jit(solution)/shard_map/ppermute | solution.py:505

commit v7 on v6

--- a/solution.py
+++ b/solution.py
@@ -153,7 +153,8 @@
 
 
 def arrange_kernel(
-    rec_ref, in_ref, state_ref, weather_ref, row_up, row_down, col_right, col_left, turn_ref
+    rec_ref, place_ref, in_ref,
+    state_ref, weather_ref, weight_ref, row_up, row_down, col_right, col_left, turn_ref,
 ):
     def row(r, carry):
         parts = [in_ref[src, 16 * tg + r] for src in range(8) for tg in range(3)]
@@ -168,7 +169,7 @@
             state_ref[r + 3, pl.ds(24, 128), 128 * half : 128 * half + 128] = whole
         return carry
 
-    lax.fori_loop(0, ROWS, row, 0, unroll=2)
+    lax.fori_loop(0, ROWS, row, 0, unroll=8)
     write_edges(state_ref, row_up, row_down, col_right, col_left)
 
     def lanes(*blocks):
@@ -189,6 +190,7 @@
     row_down[384:400] = jnp.concatenate(downs, 0).astype(BF16)
     col_right[384:400] = jnp.concatenate(rights, 0).astype(BF16)
     col_left[384:416] = jnp.concatenate(lefts, 0).astype(BF16)
+    write_weights(0, place_ref, weather_ref, None, weight_ref)
 
 
 def face_weights(flux, mass_low, mass_up):
@@ -286,9 +288,9 @@
         def weights(field, c):
             return [pick(main[(field + i) // 8], field + i, c) for i in range(3)]
 
-        def z_put(ref, c, value):
+        def z_put(ref, c, value, shift=0):
             for half in range(2):
-                ref[half, pl.ds(16 * c + 8, 8), :] = value[:, 128 * half : 128 * half + 128]
+                ref[half, pl.ds(16 * c + 8 + shift, 8), :] = value[:, 128 * half : 128 * half + 128]
 
         def z_get(ref, c, shift):
             rows = pl.ds(16 * c + 8 + shift, 8)
@@ -311,15 +313,20 @@
                 weights(YA, c), y_edge(c), y_edge(c - 1), y_edge(c + 1), q_at(c - 1), q_at(c)
             )
 
+        for c in range(COLS):
+            z_put(z_q, c, q_at(c))
+        for half in range(2):
+            low = [z_q[half, pl.ds(8 + k, COLS, stride=16), :] for k in range(2)]
+            none = jnp.zeros_like(low[0])
+            z_edge[half, pl.ds(8, COLS, stride=16), :] = edge_value(none, none, *low)
         flux_y = None
         for c in range(COLS):
             here = q_at(c)
-            z_put(z_q, c, here)
-            m2, m1, p1, p2 = [z_get(z_q, c, shift) for shift in (-2, -1, 1, 2)]
-            edge = edge_value(m2, m1, here, p1)
-            z_put(z_edge, c, edge)
+            m1, p1, p2 = [z_get(z_q, c, shift) for shift in (-1, 1, 2)]
+            edge_up = edge_value(m1, here, p1, p2)
+            z_put(z_edge, c, edge_up, 1)
             flux_z = face_flux(
-                weights(ZA, c), edge, z_get(z_edge, c, -1), edge_value(m1, here, p1, p2), m1, here
+                weights(ZA, c), z_get(z_edge, c, 0), z_get(z_edge, c, -1), edge_up, m1, here
             )
             z_put(z_flux, c, flux_z)
             total = z_get(z_flux, c, 1) - flux_z
@@ -399,7 +406,7 @@
 
 def react(state, sel_ref, net_ref, coeff_ref, rate_ref):
     def block(n, carry):
-        rows = [3 + 4 * n + i for i in range(4)]
+        rows = [3 + 16 * n + i for i in range(16)]
         inner = pl.ds(24, 128)
         conc = jnp.concatenate([state[r, inner] for r in rows], 0).astype(BF16)
         for k in range(2):
@@ -415,15 +422,10 @@
             state[r, inner] += change[128 * i : 128 * i + 128]
         return carry
 
-    lax.fori_loop(0, ROWS // 4, block, 0)
-
-
-def first_inner_kernel(place_ref, weather_ref, state, partial, weight_ref, *work):
-    write_weights(0, place_ref, weather_ref, None, weight_ref)
-    advect_inner(state, weight_ref, partial, *work)
-
-
-def second_inner_kernel(weight_ref, state, partial, *work):
+    lax.fori_loop(0, ROWS // 16, block, 0)
+
+
+def inner_kernel(weight_ref, state, partial, *work):
     advect_inner(state, weight_ref, partial, *work)
 
 
@@ -466,7 +468,7 @@
             out_ref[g // 3, 16 * (g % 3) + r] = turned[8 * g : 8 * g + 8]
         return carry
 
-    lax.fori_loop(0, ROWS, row, 0, unroll=2)
+    lax.fori_loop(0, ROWS, row, 0, unroll=8)
 
 
 def blocks(*lead):
@@ -542,12 +544,14 @@
 
     state_shape = jax.ShapeDtypeStruct((ROWS + 6, 8 * (COLS + 6), LANES), F32)
     turn = pltpu.VMEM((512, 128), F32)
-    state, weather, *edges = call(
+    weights = (ROWS + 1, 2, 8, 128)
+    weights_shape = jax.ShapeDtypeStruct(weights, F32)
+    state, weather, early, *edges = call(
         arrange_kernel,
-        [state_shape, blocks(STEPS, 8)] + edge_blocks(400, 400, 400, 416),
-        [SMEM, VMEM],
+        [state_shape, blocks(STEPS, 8), weights_shape] + edge_blocks(400, 400, 400, 416),
+        [SMEM, SMEM, VMEM],
         [turn],
-        (record_of_step, swap(sent)),
+        (record_of_step, place, swap(sent)),
     )
     column = pltpu.VMEM((2, 16 * COLS + 16, 128), F32)
     work = [
@@ -555,17 +559,15 @@
         pltpu.VMEM((COLS, 8, LANES), F32),
         column, column, column,
     ]
-    rates = pltpu.VMEM((512, reactions), BF16)
-    weights = (ROWS + 1, 2, 8, 128)
+    rates = pltpu.VMEM((2048, reactions), BF16)
     partial_shape = jax.ShapeDtypeStruct((ROWS, COLS, 8, LANES), F32)
     halos = halo(*edges)
     partial = call(
-        first_inner_kernel, partial_shape, [SMEM] + [VMEM] * 2,
-        [pltpu.VMEM(weights, F32)] + work, (place, weather, state), cost=COST,
+        inner_kernel, partial_shape, [VMEM] * 2, work, (early, state), cost=COST
     )
     state, _, later, *edges = call(
         first_kernel,
-        [state_shape, partial_shape, jax.ShapeDtypeStruct(weights, F32)]
+        [state_shape, partial_shape, weights_shape]
         + edge_blocks(384, 384, 384, 384),
         [SMEM] + [VMEM] * 10,
         [pltpu.VMEM(weights, F32), rates],
@@ -574,7 +576,7 @@
     )
     halos = halo(*edges)
     partial = call(
-        second_inner_kernel, partial_shape, [VMEM] * 2, work, (later, state), cost=COST
+        inner_kernel, partial_shape, [VMEM] * 2, work, (later, state), cost=COST
     )
     _, _, sent = call(
         second_kernel,

time: 121 us -> 118 us (0.975)
  Pallas kernels: 34.3 us -> 30.9 us
    pallas_call x7, Pallas kernels: 34.3 us -> 30.9 us  [call(): pl.pallas_call(kernel, out_shape=outs, in_specs=specs, out_specs=out_spec...]
  transfers between devices with their start and end apart: 9 -> 9, of which waited for: 2 -> 3; matrix products, arithmetic and copies ran while one was open for 1% -> 1% of each run, Pallas kernels for 10% -> 9%
where the time goes in v7:
time: 118 us; the launch traced here: 117 us
  Pallas kernels  30.9 us (26%)
  waiting for transfers between devices  28.9 us (24%)
  starting transfers between devices  28.4 us (24%)
  blocking collectives  28.1 us (24%)
    pallas_call x7, Pallas kernels, call(): pl.pallas_call(kernel, out_shape=outs, in_specs=specs, out_specs=out_spec...  30.9 us
    all_to_all x1, blocking collectives, swap(): return lax.all_to_all(x, 'tracer', split_axis=0, concat_axis=0, tiled=True)  28.1 us
    all_to_all x1, waiting for transfers between devices, swap(): return lax.all_to_all(x, 'tracer', split_axis=0, concat_axis=0, tiled=True)  26.9 us
    ppermute x2, starting transfers between devices, halo(): lax.ppermute(row_down, 'tile', back(tiles))  9.08 us
    all_to_all x1, starting transfers between devices, swap(): return lax.all_to_all(x, 'tracer', split_axis=0, concat_axis=0, tiled=True)  7.76 us
    ppermute x2, starting transfers between devices, halo(): lax.ppermute(col_right, 'tracer', columns)  5.11 us
    ppermute x2, starting transfers between devices, halo(): lax.ppermute(row_up, 'tile', tiles)  3.84 us
    ppermute x2, starting transfers between devices, halo(): lax.ppermute(col_left, 'tracer', back(columns))  2.58 us
  transfers between devices with their start and end apart: 9, of which 3 were waited for; matrix products, arithmetic and copies ran while one was open for 1% of the time, Pallas kernels for 9%

profile of v7, /device:TPU:16, one launch (start us, length us, event | category | flops | bytes accessed | tf_op | source)
XLA Modules:
  0.0 117.2 jit_solution(12671256168228440583)
XLA Ops:
  0.0 4.1 %shard_map.91 = f32[8,56,8,128]{3,2,1,0:T(8,128)} custom-call(f32[3072,128]{1,0:T(8,128)} %bitcast.16, f32[128,128]{1,0:T(8,128)} %bitcast.17, f32[128,128]{1,0:T(8,128)} %bitcast.18, f32[128,128]{1,0:T(8,128)} %bitcast.19, f32[128,128]{1,0:T(8,128)} %bitcast.20), custom_call_target="tpu_custom_call" | custom-call | tf_op jit(solution)/shard_map/pallas_call | solution.py:480
  4.1 7.8 %all-to-all-start = ((f32[8,56,8,128]{3,2,1,0:T(8,128)}), f32[8,56,8,128]{3,2,1,0:T(8,128)S(1)}, u32[]{:S(2)}, u32[]{:S(2)}) async-start(f32[8,56,8,128]{3,2,1,0:T(8,128)} %shard_map.91), calls=%async_computation | async-start | bytes 3670016 | tf_op jit(solution)/shard_map/all_to_all | solution.py:493
  11.9 0.2 copy.14
  12.1 0.1 pad_add_fusion.place_ref
  12.2 0.1 iota_compare_fusion.2
  12.4 26.9 %all-to-all-done.in_ref = f32[8,56,8,128]{3,2,1,0:T(8,128)S(1)} async-done(((f32[8,56,8,128]{3,2,1,0:T(8,128)}), f32[8,56,8,128]{3,2,1,0:T(8,128)S(1)}, u32[]{:S(2)}, u32[]{:S(2)}) %all-to-all-start) | async-done | bytes 1835040 | tf_op jit(solution)/shard_map/all_to_all | solution.py:493
  39.3 1.8 %shard_map.92 = (f32[22,176,256]{2,1,0:T(8,128)S(1)}, f32[2,8,8,128]{3,2,1,0:T(8,128)S(1)}, f32[17,2,8,128]{3,2,1,0:T(8,128)S(1)}, bf16[400,256]{1,0:T(8,128)(2,...) custom-call(s32[2]{0:T(128)S(1)} %copy-done.1, ...), custom_call_target="tpu_custom_call" | custom-call | tf_op jit(solution)/shard_map/pallas_call | solution.py:480
  41.1 1.9 %collective-permute-start = (bf16[400,256]{1,0:T(8,128)(2,1)S(1)}, bf16[400,256]{1,0:T(8,128)(2,1)S(1)}, u32[]{:S(2)}, u32[]{:S(2)}) collective-permute-start(bf16[400,256]{1,0:T(8,128)(2,1)S(1)} %get-tuple-element.20), channel_id=1, source_target_pairs={{0,1},{1,2},{2,3},{3,4},{4,5},{5,6},{6,7},{7,8},{8,9},{9,10},{10,1... | collective-permute-start | bytes 614408 | tf_op jit(solution)/shard_map/ppermute | solution.py:504
  43.0 4.5 %collective-permute-start.1 = (bf16[400,256]{1,0:T(8,128)(2,1)S(1)}, bf16[400,256]{1,0:T(8,128)(2,1)S(1)}, u32[]{:S(2)}, u32[]{:S(2)}) collective-permute-start(bf16[400,256]{1,0:T(8,128)(2,1)S(1)} %get-tuple-element.21), channel_id=1, source_target_pairs={{1,0},{2,1},{3,2},{4,3},{5,4},{6,5},{7,6},{8,7},{9,8},{10,9},{11,1... | collective-permute-start | bytes 614408 | tf_op jit(solution)/shard_map/ppermute | solution.py:505
  47.6 1.5 %collective-permute-start.2 = (bf16[400,256]{1,0:T(8,128)(2,1)S(1)}, bf16[400,256]{1,0:T(8,128)(2,1)S(1)}, u32[]{:S(2)}, u32[]{:S(2)}) collective-permute-start(bf16[400,256]{1,0:T(8,128)(2,1)S(1)} %get-tuple-element.22), channel_id=1, source_target_pairs={{0,32},{32,64},{64,96},{96,112},{112,80},{80,48},{48,16},{1,33},{3... | collective-permute-start | bytes 614408 | tf_op jit(solution)/shard_map/ppermute | solution.py:506
  49.1 1.3 %collective-permute-start.3 = (bf16[416,256]{1,0:T(8,128)(2,1)S(1)}, bf16[416,256]{1,0:T(8,128)(2,1)S(1)}, u32[]{:S(2)}, u32[]{:S(2)}) collective-permute-start(bf16[416,256]{1,0:T(8,128)(2,1)S(1)} %get-tuple-element.23), channel_id=1, source_target_pairs={{32,0},{64,32},{96,64},{112,96},{80,112},{48,80},{16,48},{33,1},{6... | collective-permute-start | bytes 638984 | tf_op jit(solution)/shard_map/ppermute | solution.py:507
  50.4 0.2 subtract_convert_fusion.net_ref
  50.6 5.2 %shard_map.93.partial_ref = f32[16,16,8,256]{3,2,1,0:T(8,128)S(1)} custom-call(f32[17,2,8,128]{3,2,1,0:T(8,128)S(1)} %get-tuple-element.25.weight_ref, f32[22,176,256]{2,1,0:T(8,128)S(1)} %get-tuple-element.24.state.in_ref), custom_call_target="tpu_custom_call" | custom-call | flops 60000000 | bytes 8000000 | tf_op jit(solution)/shard_map/pallas_call | solution.py:480
  55.9 1.0 collective-permute-done.3.col_hi
  56.8 5.9 %shard_map.94 = (f32[22,176,256]{2,1,0:T(8,128)S(1)}, f32[16,16,8,256]{3,2,1,0:T(8,128)S(1)}, f32[17,2,8,128]{3,2,1,0:T(8,128)S(1)}, bf16[384,256]{1,0:T(8,128)(...) custom-call(s32[2]{0:T(128)S(1)} %pad_add_fusion.place_ref, ...), custom_call_target="tpu_custom_call", output_to_operand_aliasing={{0}: (9, {}), {1}: (10, {})} | custom-call | tf_op jit(solution)/shard_map/pallas_call | solution.py:480
  62.8 1.9 %collective-permute-start.4 = (bf16[384,256]{1,0:T(8,128)(2,1)S(1)}, bf16[384,256]{1,0:T(8,128)(2,1)S(1)}, u32[]{:S(2)}, u32[]{:S(2)}) collective-permute-start(bf16[384,256]{1,0:T(8,128)(2,1)S(1)} %get-tuple-element.27), channel_id=1, source_target_pairs={{0,1},{1,2},{2,3},{3,4},{4,5},{5,6},{6,7},{7,8},{8,9},{9,10},{10,1... | collective-permute-start | bytes 589832 | tf_op jit(solution)/shard_map/ppermute | solution.py:504
  64.7 4.5 %collective-permute-start.5 = (bf16[384,256]{1,0:T(8,128)(2,1)S(1)}, bf16[384,256]{1,0:T(8,128)(2,1)S(1)}, u32[]{:S(2)}, u32[]{:S(2)}) collective-permute-start(bf16[384,256]{1,0:T(8,128)(2,1)S(1)} %get-tuple-element.28), channel_id=1, source_target_pairs={{1,0},{2,1},{3,2},{4,3},{5,4},{6,5},{7,6},{8,7},{9,8},{10,9},{11,1... | collective-permute-start | bytes 589832 | tf_op jit(solution)/shard_map/ppermute | solution.py:505
  69.2 3.6 %collective-permute-start.6 = (bf16[384,256]{1,0:T(8,128)(2,1)S(1)}, bf16[384,256]{1,0:T(8,128)(2,1)S(1)}, u32[]{:S(2)}, u32[]{:S(2)}) collective-permute-start(bf16[384,256]{1,0:T(8,128)(2,1)S(1)} %get-tuple-element.29), channel_id=1, source_target_pairs={{0,32},{32,64},{64,96},{96,112},{112,80},{80,48},{48,16},{1,33},{3... | collective-permute-start | bytes 589832 | tf_op jit(solution)/shard_map/ppermute | solution.py:506
  72.9 1.3 %collective-permute-start.7 = (bf16[384,256]{1,0:T(8,128)(2,1)S(1)}, bf16[384,256]{1,0:T(8,128)(2,1)S(1)}, u32[]{:S(2)}, u32[]{:S(2)}) collective-permute-start(bf16[384,256]{1,0:T(8,128)(2,1)S(1)} %get-tuple-element.30), channel_id=1, source_target_pairs={{32,0},{64,32},{96,64},{112,96},{80,112},{48,80},{16,48},{33,1},{6... | collective-permute-start | bytes 589832 | tf_op jit(solution)/shard_map/ppermute | solution.py:507
  74.2 5.2 %shard_map.95.partial_ref = f32[16,16,8,256]{3,2,1,0:T(8,128)S(1)} custom-call(f32[17,2,8,128]{3,2,1,0:T(8,128)S(1)} %get-tuple-element.26.weight_ref, f32[22,176,256]{2,1,0:T(8,128)S(1)} %get-tuple-element.31.state.in_ref), custom_call_target="tpu_custom_call" | custom-call | flops 60000000 | bytes 8000000 | tf_op jit(solution)/shard_map/pallas_call | solution.py:480
  79.4 1.0 collective-permute-done.7.col_hi
  80.4 6.0 %shard_map.96 = (f32[22,176,256]{2,1,0:T(8,128)S(1)}, f32[16,16,8,256]{3,2,1,0:T(8,128)S(1)}, f32[8,48,8,128]{3,2,1,0:T(8,128)S(1)}) custom-call(f32[17,2,8,128]{3,2,1,0:T(8,128)S(1)} %get-tuple-element.26.weight_ref, bf16[384,256]{1,0:T(8,128)(2,1)S(1)} %collective-permute-done.4.row_lo, ...), custom_call_target="tpu_custom_call", output_to_operand_aliasing={{0}: (8, {}), {1}: (9, {})} | custom-call | tf_op jit(solution)/shard_map/pallas_call | solution.py:480
  86.4 28.1 %all_to_all.10.in_ref = f32[8,48,8,128]{3,2,1,0:T(8,128)S(1)} all-to-all(f32[8,48,8,128]{3,2,1,0:T(8,128)S(1)} %get-tuple-element.32), channel_id=1, replica_groups=mesh['tracer'=8,'tile'=16] {'tracer'}, dimensions={0} | all-to-all | bytes 3145728 | tf_op jit(solution)/shard_map/all_to_all | solution.py:493
  114.6 2.7 %shard_map.97 = f32[3072,128]{1,0:T(8,128)} custom-call(f32[8,48,8,128]{3,2,1,0:T(8,128)S(1)} %all_to_all.10.in_ref), custom_call_target="tpu_custom_call" | custom-call | tf_op jit(solution)/shard_map/pallas_call | solution.py:480
  (17 shorter events, 0.1 us)
Async XLA Ops:
  4.1 7.8 %copy-start.2 = (s32[512,192]{0,1:T(8,128)S(1)}, s32[512,192]{0,1:T(8,128)}, u32[]{:S(2)}) copy-start(s32[512,192]{0,1:T(8,128)} %param.15) | copy-start | bytes 1179652
  4.1 8.1 %copy-start.3 = (s32[512,2]{0,1:T(2,128)S(1)}, s32[512,2]{0,1:T(2,128)}, u32[]{:S(2)}) copy-start(s32[512,2]{0,1:T(2,128)} %param.14) | copy-start | bytes 12292
  4.1 35.2 %copy-start.1 = (s32[2]{0:T(128)S(1)}, s32[2]{0:T(128)}, u32[]{:S(2)}) copy-start(s32[2]{0:T(128)} %rec_ref.1) | copy-start | bytes 28
  4.1 35.2 %all-to-all-start = ((f32[8,56,8,128]{3,2,1,0:T(8,128)}), f32[8,56,8,128]{3,2,1,0:T(8,128)S(1)}, u32[]{:S(2)}, u32[]{:S(2)}) async-start(f32[8,56,8,128]{3,2,1,0:T(8,128)} %shard_map.91), calls=%async_computation | async-start | bytes 3670016 | tf_op jit(solution)/shard_map/all_to_all | solution.py:493
  41.1 14.7 %collective-permute-start = (bf16[400,256]{1,0:T(8,128)(2,1)S(1)}, bf16[400,256]{1,0:T(8,128)(2,1)S(1)}, u32[]{:S(2)}, u32[]{:S(2)}) collective-permute-start(bf16[400,256]{1,0:T(8,128)(2,1)S(1)} %get-tuple-element.20), channel_id=1, source_target_pairs={{0,1},{1,2},{2,3},{3,4},{4,5},{5,6},{6,7},{7,8},{8,9},{9,10},{10,1... | collective-permute-start | bytes 614408 | tf_op jit(solution)/shard_map/ppermute | solution.py:504
  43.0 12.8 %collective-permute-start.1 = (bf16[400,256]{1,0:T(8,128)(2,1)S(1)}, bf16[400,256]{1,0:T(8,128)(2,1)S(1)}, u32[]{:S(2)}, u32[]{:S(2)}) collective-permute-start(bf16[400,256]{1,0:T(8,128)(2,1)S(1)} %get-tuple-element.21), channel_id=1, source_target_pairs={{1,0},{2,1},{3,2},{4,3},{5,4},{6,5},{7,6},{8,7},{9,8},{10,9},{11,1... | collective-permute-start | bytes 614408 | tf_op jit(solution)/shard_map/ppermute | solution.py:505
  47.6 8.3 %collective-permute-start.2 = (bf16[400,256]{1,0:T(8,128)(2,1)S(1)}, bf16[400,256]{1,0:T(8,128)(2,1)S(1)}, u32[]{:S(2)}, u32[]{:S(2)}) collective-permute-start(bf16[400,256]{1,0:T(8,128)(2,1)S(1)} %get-tuple-element.22), channel_id=1, source_target_pairs={{0,32},{32,64},{64,96},{96,112},{112,80},{80,48},{48,16},{1,33},{3... | collective-permute-start | bytes 614408 | tf_op jit(solution)/shard_map/ppermute | solution.py:506
  49.1 7.7 %collective-permute-start.3 = (bf16[416,256]{1,0:T(8,128)(2,1)S(1)}, bf16[416,256]{1,0:T(8,128)(2,1)S(1)}, u32[]{:S(2)}, u32[]{:S(2)}) collective-permute-start(bf16[416,256]{1,0:T(8,128)(2,1)S(1)} %get-tuple-element.23), channel_id=1, source_target_pairs={{32,0},{64,32},{96,64},{112,96},{80,112},{48,80},{16,48},{33,1},{6... | collective-permute-start | bytes 638984 | tf_op jit(solution)/shard_map/ppermute | solution.py:507
  50.6 6.2 %copy-start = (f32[512]{0:T(512)S(1)}, f32[512]{0:T(512)}, u32[]{:S(2)}) copy-start(f32[512]{0:T(512)} %param.16) | copy-start | bytes 6148
  62.8 16.6 %collective-permute-start.4 = (bf16[384,256]{1,0:T(8,128)(2,1)S(1)}, bf16[384,256]{1,0:T(8,128)(2,1)S(1)}, u32[]{:S(2)}, u32[]{:S(2)}) collective-permute-start(bf16[384,256]{1,0:T(8,128)(2,1)S(1)} %get-tuple-element.27), channel_id=1, source_target_pairs={{0,1},{1,2},{2,3},{3,4},{4,5},{5,6},{6,7},{7,8},{8,9},{9,10},{10,1... | collective-permute-start | bytes 589832 | tf_op jit(solution)/shard_map/ppermute | solution.py:504
  64.7 14.7 %collective-permute-start.5 = (bf16[384,256]{1,0:T(8,128)(2,1)S(1)}, bf16[384,256]{1,0:T(8,128)(2,1)S(1)}, u32[]{:S(2)}, u32[]{:S(2)}) collective-permute-start(bf16[384,256]{1,0:T(8,128)(2,1)S(1)} %get-tuple-element.28), channel_id=1, source_target_pairs={{1,0},{2,1},{3,2},{4,3},{5,4},{6,5},{7,6},{8,7},{9,8},{10,9},{11,1... | collective-permute-start | bytes 589832 | tf_op jit(solution)/shard_map/ppermute | solution.py:505
  69.2 10.2 %collective-permute-start.6 = (bf16[384,256]{1,0:T(8,128)(2,1)S(1)}, bf16[384,256]{1,0:T(8,128)(2,1)S(1)}, u32[]{:S(2)}, u32[]{:S(2)}) collective-permute-start(bf16[384,256]{1,0:T(8,128)(2,1)S(1)} %get-tuple-element.29), channel_id=1, source_target_pairs={{0,32},{32,64},{64,96},{96,112},{112,80},{80,48},{48,16},{1,33},{3... | collective-permute-start | bytes 589832 | tf_op jit(solution)/shard_map/ppermute | solution.py:506
  72.9 7.6 %collective-permute-start.7 = (bf16[384,256]{1,0:T(8,128)(2,1)S(1)}, bf16[384,256]{1,0:T(8,128)(2,1)S(1)}, u32[]{:S(2)}, u32[]{:S(2)}) collective-permute-start(bf16[384,256]{1,0:T(8,128)(2,1)S(1)} %get-tuple-element.30), channel_id=1, source_target_pairs={{32,0},{64,32},{96,64},{112,96},{80,112},{48,80},{16,48},{33,1},{6... | collective-permute-start | bytes 589832 | tf_op jit(solution)/shard_map/ppermute | solution.py:507

commit v8 on v7

--- a/solution.py
+++ b/solution.py
@@ -356,8 +356,8 @@
             x_edges[3 + k, c] = edges[k]
         weights = [pick(third, XA + i, c) for i in range(3)]
         x_flux[c] = face_flux(weights, edges[1], edges[0], edges[2], q[2], q[3])
-    lax.fori_loop(3, 13, functools.partial(row, True), 0)
-    lax.fori_loop(0, 6, lambda k, carry: row(False, jnp.where(k < 3, k, k + 10), carry), 0)
+    lax.fori_loop(3, 13, functools.partial(row, True), 0, unroll=2)
+    lax.fori_loop(0, 6, lambda k, carry: row(False, jnp.where(k < 3, k, k + 10), carry), 0, unroll=2)
 
 
 def four_faces(q, weights):
@@ -401,7 +401,7 @@
             state[r + 3, cell(c)] = value * pick(main[INV // 8], INV, c)
         return carry
 
-    lax.fori_loop(0, ROWS, row, 0)
+    lax.fori_loop(0, ROWS, row, 0, unroll=16)
 
 
 def react(state, sel_ref, net_ref, coeff_ref, rate_ref):

time: 118 us -> 115 us (0.975)
  Pallas kernels: 30.9 us -> 28 us
    pallas_call x7, Pallas kernels: 30.9 us -> 28 us  [call(): pl.pallas_call(kernel, out_shape=outs, in_specs=specs, out_specs=out_spec...]
where the time goes in v8:
time: 115 us
  waiting for transfers between devices  28.9 us (25%)
  starting transfers between devices  28.4 us (25%)
  blocking collectives  28.2 us (25%)
  Pallas kernels  28 us (24%)
    all_to_all x1, blocking collectives, swap(): return lax.all_to_all(x, 'tracer', split_axis=0, concat_axis=0, tiled=True)  28.2 us
    pallas_call x7, Pallas kernels, call(): pl.pallas_call(kernel, out_shape=outs, in_specs=specs, out_specs=out_spec...  28 us
    all_to_all x1, waiting for transfers between devices, swap(): return lax.all_to_all(x, 'tracer', split_axis=0, concat_axis=0, tiled=True)  26.9 us
    ppermute x2, starting transfers between devices, halo(): lax.ppermute(row_down, 'tile', back(tiles))  9.08 us
    all_to_all x1, starting transfers between devices, swap(): return lax.all_to_all(x, 'tracer', split_axis=0, concat_axis=0, tiled=True)  7.76 us
    ppermute x2, starting transfers between devices, halo(): lax.ppermute(col_right, 'tracer', columns)  5 us
    ppermute x2, starting transfers between devices, halo(): lax.ppermute(row_up, 'tile', tiles)  3.84 us
    ppermute x2, starting transfers between devices, halo(): lax.ppermute(col_left, 'tracer', back(columns))  2.76 us
  transfers between devices with their start and end apart: 9, of which 3 were waited for; matrix products, arithmetic and copies ran while one was open for 1% of the time, Pallas kernels for 9%

profile of v8, /device:TPU:16, one launch (start us, length us, event | category | flops | bytes accessed | tf_op | source)
XLA Modules:
  0.0 114.6 jit_solution(12506511752683791426)
XLA Ops:
  0.0 4.1 %shard_map.91 = f32[8,56,8,128]{3,2,1,0:T(8,128)} custom-call(f32[3072,128]{1,0:T(8,128)} %bitcast.16, f32[128,128]{1,0:T(8,128)} %bitcast.17, f32[128,128]{1,0:T(8,128)} %bitcast.18, f32[128,128]{1,0:T(8,128)} %bitcast.19, f32[128,128]{1,0:T(8,128)} %bitcast.20), custom_call_target="tpu_custom_call" | custom-call | tf_op jit(solution)/shard_map/pallas_call | solution.py:480
  4.1 7.8 %all-to-all-start = ((f32[8,56,8,128]{3,2,1,0:T(8,128)}), f32[8,56,8,128]{3,2,1,0:T(8,128)S(1)}, u32[]{:S(2)}, u32[]{:S(2)}) async-start(f32[8,56,8,128]{3,2,1,0:T(8,128)} %shard_map.91), calls=%async_computation | async-start | bytes 3670016 | tf_op jit(solution)/shard_map/all_to_all | solution.py:493
  11.9 0.2 copy.14
  12.1 0.1 pad_add_fusion.place_ref
  12.2 0.1 iota_compare_fusion.2
  12.4 26.9 %all-to-all-done.in_ref = f32[8,56,8,128]{3,2,1,0:T(8,128)S(1)} async-done(((f32[8,56,8,128]{3,2,1,0:T(8,128)}), f32[8,56,8,128]{3,2,1,0:T(8,128)S(1)}, u32[]{:S(2)}, u32[]{:S(2)}) %all-to-all-start) | async-done | bytes 1835040 | tf_op jit(solution)/shard_map/all_to_all | solution.py:493
  39.3 1.8 %shard_map.92 = (f32[22,176,256]{2,1,0:T(8,128)S(1)}, f32[2,8,8,128]{3,2,1,0:T(8,128)S(1)}, f32[17,2,8,128]{3,2,1,0:T(8,128)S(1)}, bf16[400,256]{1,0:T(8,128)(2,...) custom-call(s32[2]{0:T(128)S(1)} %copy-done.1, ...), custom_call_target="tpu_custom_call" | custom-call | tf_op jit(solution)/shard_map/pallas_call | solution.py:480
  41.1 1.9 %collective-permute-start = (bf16[400,256]{1,0:T(8,128)(2,1)S(1)}, bf16[400,256]{1,0:T(8,128)(2,1)S(1)}, u32[]{:S(2)}, u32[]{:S(2)}) collective-permute-start(bf16[400,256]{1,0:T(8,128)(2,1)S(1)} %get-tuple-element.20), channel_id=1, source_target_pairs={{0,1},{1,2},{2,3},{3,4},{4,5},{5,6},{6,7},{7,8},{8,9},{9,10},{10,1... | collective-permute-start | bytes 614408 | tf_op jit(solution)/shard_map/ppermute | solution.py:504
  43.0 4.5 %collective-permute-start.1 = (bf16[400,256]{1,0:T(8,128)(2,1)S(1)}, bf16[400,256]{1,0:T(8,128)(2,1)S(1)}, u32[]{:S(2)}, u32[]{:S(2)}) collective-permute-start(bf16[400,256]{1,0:T(8,128)(2,1)S(1)} %get-tuple-element.21), channel_id=1, source_target_pairs={{1,0},{2,1},{3,2},{4,3},{5,4},{6,5},{7,6},{8,7},{9,8},{10,9},{11,1... | collective-permute-start | bytes 614408 | tf_op jit(solution)/shard_map/ppermute | solution.py:505
  47.6 1.5 %collective-permute-start.2 = (bf16[400,256]{1,0:T(8,128)(2,1)S(1)}, bf16[400,256]{1,0:T(8,128)(2,1)S(1)}, u32[]{:S(2)}, u32[]{:S(2)}) collective-permute-start(bf16[400,256]{1,0:T(8,128)(2,1)S(1)} %get-tuple-element.22), channel_id=1, source_target_pairs={{0,32},{32,64},{64,96},{96,112},{112,80},{80,48},{48,16},{1,33},{3... | collective-permute-start | bytes 614408 | tf_op jit(solution)/shard_map/ppermute | solution.py:506
  49.1 1.3 %collective-permute-start.3 = (bf16[416,256]{1,0:T(8,128)(2,1)S(1)}, bf16[416,256]{1,0:T(8,128)(2,1)S(1)}, u32[]{:S(2)}, u32[]{:S(2)}) collective-permute-start(bf16[416,256]{1,0:T(8,128)(2,1)S(1)} %get-tuple-element.23), channel_id=1, source_target_pairs={{32,0},{64,32},{96,64},{112,96},{80,112},{48,80},{16,48},{33,1},{6... | collective-permute-start | bytes 638984 | tf_op jit(solution)/shard_map/ppermute | solution.py:507
  50.4 0.2 subtract_convert_fusion.net_ref
  50.6 5.1 %shard_map.93.partial_ref = f32[16,16,8,256]{3,2,1,0:T(8,128)S(1)} custom-call(f32[17,2,8,128]{3,2,1,0:T(8,128)S(1)} %get-tuple-element.25.weight_ref, f32[22,176,256]{2,1,0:T(8,128)S(1)} %get-tuple-element.24.state.in_ref), custom_call_target="tpu_custom_call" | custom-call | flops 60000000 | bytes 8000000 | tf_op jit(solution)/shard_map/pallas_call | solution.py:480
  55.7 1.1 collective-permute-done.3.col_hi
  56.8 4.6 %shard_map.94 = (f32[22,176,256]{2,1,0:T(8,128)S(1)}, f32[16,16,8,256]{3,2,1,0:T(8,128)S(1)}, f32[17,2,8,128]{3,2,1,0:T(8,128)S(1)}, bf16[384,256]{1,0:T(8,128)(...) custom-call(s32[2]{0:T(128)S(1)} %pad_add_fusion.place_ref, ...), custom_call_target="tpu_custom_call", output_to_operand_aliasing={{0}: (9, {}), {1}: (10, {})} | custom-call | tf_op jit(solution)/shard_map/pallas_call | solution.py:480
  61.4 1.9 %collective-permute-start.4 = (bf16[384,256]{1,0:T(8,128)(2,1)S(1)}, bf16[384,256]{1,0:T(8,128)(2,1)S(1)}, u32[]{:S(2)}, u32[]{:S(2)}) collective-permute-start(bf16[384,256]{1,0:T(8,128)(2,1)S(1)} %get-tuple-element.27), channel_id=1, source_target_pairs={{0,1},{1,2},{2,3},{3,4},{4,5},{5,6},{6,7},{7,8},{8,9},{9,10},{10,1... | collective-permute-start | bytes 589832 | tf_op jit(solution)/shard_map/ppermute | solution.py:504
  63.3 4.5 %collective-permute-start.5 = (bf16[384,256]{1,0:T(8,128)(2,1)S(1)}, bf16[384,256]{1,0:T(8,128)(2,1)S(1)}, u32[]{:S(2)}, u32[]{:S(2)}) collective-permute-start(bf16[384,256]{1,0:T(8,128)(2,1)S(1)} %get-tuple-element.28), channel_id=1, source_target_pairs={{1,0},{2,1},{3,2},{4,3},{5,4},{6,5},{7,6},{8,7},{9,8},{10,9},{11,1... | collective-permute-start | bytes 589832 | tf_op jit(solution)/shard_map/ppermute | solution.py:505
  67.9 3.5 %collective-permute-start.6 = (bf16[384,256]{1,0:T(8,128)(2,1)S(1)}, bf16[384,256]{1,0:T(8,128)(2,1)S(1)}, u32[]{:S(2)}, u32[]{:S(2)}) collective-permute-start(bf16[384,256]{1,0:T(8,128)(2,1)S(1)} %get-tuple-element.29), channel_id=1, source_target_pairs={{0,32},{32,64},{64,96},{96,112},{112,80},{80,48},{48,16},{1,33},{3... | collective-permute-start | bytes 589832 | tf_op jit(solution)/shard_map/ppermute | solution.py:506
  71.4 1.5 %collective-permute-start.7 = (bf16[384,256]{1,0:T(8,128)(2,1)S(1)}, bf16[384,256]{1,0:T(8,128)(2,1)S(1)}, u32[]{:S(2)}, u32[]{:S(2)}) collective-permute-start(bf16[384,256]{1,0:T(8,128)(2,1)S(1)} %get-tuple-element.30), channel_id=1, source_target_pairs={{32,0},{64,32},{96,64},{112,96},{80,112},{48,80},{16,48},{33,1},{6... | collective-permute-start | bytes 589832 | tf_op jit(solution)/shard_map/ppermute | solution.py:507
  72.9 5.1 %shard_map.95.partial_ref = f32[16,16,8,256]{3,2,1,0:T(8,128)S(1)} custom-call(f32[17,2,8,128]{3,2,1,0:T(8,128)S(1)} %get-tuple-element.26.weight_ref, f32[22,176,256]{2,1,0:T(8,128)S(1)} %get-tuple-element.31.state.in_ref), custom_call_target="tpu_custom_call" | custom-call | flops 60000000 | bytes 8000000 | tf_op jit(solution)/shard_map/pallas_call | solution.py:480
  78.0 1.0 collective-permute-done.7.col_hi
  79.0 4.6 %shard_map.96 = (f32[22,176,256]{2,1,0:T(8,128)S(1)}, f32[16,16,8,256]{3,2,1,0:T(8,128)S(1)}, f32[8,48,8,128]{3,2,1,0:T(8,128)S(1)}) custom-call(f32[17,2,8,128]{3,2,1,0:T(8,128)S(1)} %get-tuple-element.26.weight_ref, bf16[384,256]{1,0:T(8,128)(2,1)S(1)} %collective-permute-done.4.row_lo, ...), custom_call_target="tpu_custom_call", output_to_operand_aliasing={{0}: (8, {}), {1}: (9, {})} | custom-call | tf_op jit(solution)/shard_map/pallas_call | solution.py:480
  83.6 28.2 %all_to_all.10.in_ref = f32[8,48,8,128]{3,2,1,0:T(8,128)S(1)} all-to-all(f32[8,48,8,128]{3,2,1,0:T(8,128)S(1)} %get-tuple-element.32), channel_id=1, replica_groups=mesh['tracer'=8,'tile'=16] {'tracer'}, dimensions={0} | all-to-all | bytes 3145728 | tf_op jit(solution)/shard_map/all_to_all | solution.py:493
  111.8 2.7 %shard_map.97 = f32[3072,128]{1,0:T(8,128)} custom-call(f32[8,48,8,128]{3,2,1,0:T(8,128)S(1)} %all_to_all.10.in_ref), custom_call_target="tpu_custom_call" | custom-call | tf_op jit(solution)/shard_map/pallas_call | solution.py:480
  (17 shorter events, 0.1 us)
Async XLA Ops:
  4.1 7.8 %copy-start.2 = (s32[512,192]{0,1:T(8,128)S(1)}, s32[512,192]{0,1:T(8,128)}, u32[]{:S(2)}) copy-start(s32[512,192]{0,1:T(8,128)} %param.15) | copy-start | bytes 1179652
  4.1 8.1 %copy-start.3 = (s32[512,2]{0,1:T(2,128)S(1)}, s32[512,2]{0,1:T(2,128)}, u32[]{:S(2)}) copy-start(s32[512,2]{0,1:T(2,128)} %param.14) | copy-start | bytes 12292
  4.1 35.2 %copy-start.1 = (s32[2]{0:T(128)S(1)}, s32[2]{0:T(128)}, u32[]{:S(2)}) copy-start(s32[2]{0:T(128)} %rec_ref.1) | copy-start | bytes 28
  4.1 35.2 %all-to-all-start = ((f32[8,56,8,128]{3,2,1,0:T(8,128)}), f32[8,56,8,128]{3,2,1,0:T(8,128)S(1)}, u32[]{:S(2)}, u32[]{:S(2)}) async-start(f32[8,56,8,128]{3,2,1,0:T(8,128)} %shard_map.91), calls=%async_computation | async-start | bytes 3670016 | tf_op jit(solution)/shard_map/all_to_all | solution.py:493
  41.1 14.6 %collective-permute-start = (bf16[400,256]{1,0:T(8,128)(2,1)S(1)}, bf16[400,256]{1,0:T(8,128)(2,1)S(1)}, u32[]{:S(2)}, u32[]{:S(2)}) collective-permute-start(bf16[400,256]{1,0:T(8,128)(2,1)S(1)} %get-tuple-element.20), channel_id=1, source_target_pairs={{0,1},{1,2},{2,3},{3,4},{4,5},{5,6},{6,7},{7,8},{8,9},{9,10},{10,1... | collective-permute-start | bytes 614408 | tf_op jit(solution)/shard_map/ppermute | solution.py:504
  43.0 12.7 %collective-permute-start.1 = (bf16[400,256]{1,0:T(8,128)(2,1)S(1)}, bf16[400,256]{1,0:T(8,128)(2,1)S(1)}, u32[]{:S(2)}, u32[]{:S(2)}) collective-permute-start(bf16[400,256]{1,0:T(8,128)(2,1)S(1)} %get-tuple-element.21), channel_id=1, source_target_pairs={{1,0},{2,1},{3,2},{4,3},{5,4},{6,5},{7,6},{8,7},{9,8},{10,9},{11,1... | collective-permute-start | bytes 614408 | tf_op jit(solution)/shard_map/ppermute | solution.py:505
  47.6 8.2 %collective-permute-start.2 = (bf16[400,256]{1,0:T(8,128)(2,1)S(1)}, bf16[400,256]{1,0:T(8,128)(2,1)S(1)}, u32[]{:S(2)}, u32[]{:S(2)}) collective-permute-start(bf16[400,256]{1,0:T(8,128)(2,1)S(1)} %get-tuple-element.22), channel_id=1, source_target_pairs={{0,32},{32,64},{64,96},{96,112},{112,80},{80,48},{48,16},{1,33},{3... | collective-permute-start | bytes 614408 | tf_op jit(solution)/shard_map/ppermute | solution.py:506
  49.1 7.7 %collective-permute-start.3 = (bf16[416,256]{1,0:T(8,128)(2,1)S(1)}, bf16[416,256]{1,0:T(8,128)(2,1)S(1)}, u32[]{:S(2)}, u32[]{:S(2)}) collective-permute-start(bf16[416,256]{1,0:T(8,128)(2,1)S(1)} %get-tuple-element.23), channel_id=1, source_target_pairs={{32,0},{64,32},{96,64},{112,96},{80,112},{48,80},{16,48},{33,1},{6... | collective-permute-start | bytes 638984 | tf_op jit(solution)/shard_map/ppermute | solution.py:507
  50.6 6.2 %copy-start = (f32[512]{0:T(512)S(1)}, f32[512]{0:T(512)}, u32[]{:S(2)}) copy-start(f32[512]{0:T(512)} %param.16) | copy-start | bytes 6148
  61.4 16.6 %collective-permute-start.4 = (bf16[384,256]{1,0:T(8,128)(2,1)S(1)}, bf16[384,256]{1,0:T(8,128)(2,1)S(1)}, u32[]{:S(2)}, u32[]{:S(2)}) collective-permute-start(bf16[384,256]{1,0:T(8,128)(2,1)S(1)} %get-tuple-element.27), channel_id=1, source_target_pairs={{0,1},{1,2},{2,3},{3,4},{4,5},{5,6},{6,7},{7,8},{8,9},{9,10},{10,1... | collective-permute-start | bytes 589832 | tf_op jit(solution)/shard_map/ppermute | solution.py:504
  63.3 14.7 %collective-permute-start.5 = (bf16[384,256]{1,0:T(8,128)(2,1)S(1)}, bf16[384,256]{1,0:T(8,128)(2,1)S(1)}, u32[]{:S(2)}, u32[]{:S(2)}) collective-permute-start(bf16[384,256]{1,0:T(8,128)(2,1)S(1)} %get-tuple-element.28), channel_id=1, source_target_pairs={{1,0},{2,1},{3,2},{4,3},{5,4},{6,5},{7,6},{8,7},{9,8},{10,9},{11,1... | collective-permute-start | bytes 589832 | tf_op jit(solution)/shard_map/ppermute | solution.py:505
  67.9 10.1 %collective-permute-start.6 = (bf16[384,256]{1,0:T(8,128)(2,1)S(1)}, bf16[384,256]{1,0:T(8,128)(2,1)S(1)}, u32[]{:S(2)}, u32[]{:S(2)}) collective-permute-start(bf16[384,256]{1,0:T(8,128)(2,1)S(1)} %get-tuple-element.29), channel_id=1, source_target_pairs={{0,32},{32,64},{64,96},{96,112},{112,80},{80,48},{48,16},{1,33},{3... | collective-permute-start | bytes 589832 | tf_op jit(solution)/shard_map/ppermute | solution.py:506
  71.4 7.6 %collective-permute-start.7 = (bf16[384,256]{1,0:T(8,128)(2,1)S(1)}, bf16[384,256]{1,0:T(8,128)(2,1)S(1)}, u32[]{:S(2)}, u32[]{:S(2)}) collective-permute-start(bf16[384,256]{1,0:T(8,128)(2,1)S(1)} %get-tuple-element.30), channel_id=1, source_target_pairs={{32,0},{64,32},{96,64},{112,96},{80,112},{48,80},{16,48},{33,1},{6... | collective-permute-start | bytes 589832 | tf_op jit(solution)/shard_map/ppermute | solution.py:507

commit v9 on v8

--- a/solution.py
+++ b/solution.py
@@ -169,7 +169,7 @@
             state_ref[r + 3, pl.ds(24, 128), 128 * half : 128 * half + 128] = whole
         return carry
 
-    lax.fori_loop(0, ROWS, row, 0, unroll=8)
+    lax.fori_loop(0, ROWS, row, 0, unroll=16)
     write_edges(state_ref, row_up, row_down, col_right, col_left)
 
     def lanes(*blocks):
@@ -468,7 +468,7 @@
             out_ref[g // 3, 16 * (g % 3) + r] = turned[8 * g : 8 * g + 8]
         return carry
 
-    lax.fori_loop(0, ROWS, row, 0, unroll=8)
+    lax.fori_loop(0, ROWS, row, 0, unroll=16)
 
 
 def blocks(*lead):

time: 115 us -> 114 us (level)
  no operation moved by 1% of the time
where the time goes in v9:
time: 114 us
  waiting for transfers between devices  28.9 us (25%)
  starting transfers between devices  28.4 us (25%)
  blocking collectives  28.2 us (25%)
  Pallas kernels  26.9 us (24%)
    all_to_all x1, blocking collectives, swap(): return lax.all_to_all(x, 'tracer', split_axis=0, concat_axis=0, tiled=True)  28.2 us
    pallas_call x7, Pallas kernels, call(): pl.pallas_call(kernel, out_shape=outs, in_specs=specs, out_specs=out_spec...  26.9 us
    all_to_all x1, waiting for transfers between devices, swap(): return lax.all_to_all(x, 'tracer', split_axis=0, concat_axis=0, tiled=True)  26.9 us
    ppermute x2, starting transfers between devices, halo(): lax.ppermute(row_down, 'tile', back(tiles))  9.08 us
    all_to_all x1, starting transfers between devices, swap(): return lax.all_to_all(x, 'tracer', split_axis=0, concat_axis=0, tiled=True)  7.76 us
    ppermute x2, starting transfers between devices, halo(): lax.ppermute(col_right, 'tracer', columns)  5 us
    ppermute x2, starting transfers between devices, halo(): lax.ppermute(row_up, 'tile', tiles)  3.84 us
    ppermute x2, starting transfers between devices, halo(): lax.ppermute(col_left, 'tracer', back(columns))  2.76 us
  transfers between devices with their start and end apart: 9, of which 3 were waited for; matrix products, arithmetic and copies ran while one was open for 1% of the time, Pallas kernels for 9%

profile of v9, /device:TPU:16, one launch (start us, length us, event | category | flops | bytes accessed | tf_op | source)
XLA Modules:
  0.0 113.6 jit_solution(2007071423806745986)
XLA Ops:
  0.0 4.1 %shard_map.91 = f32[8,56,8,128]{3,2,1,0:T(8,128)} custom-call(f32[3072,128]{1,0:T(8,128)} %bitcast.16, f32[128,128]{1,0:T(8,128)} %bitcast.17, f32[128,128]{1,0:T(8,128)} %bitcast.18, f32[128,128]{1,0:T(8,128)} %bitcast.19, f32[128,128]{1,0:T(8,128)} %bitcast.20), custom_call_target="tpu_custom_call" | custom-call | tf_op jit(solution)/shard_map/pallas_call | solution.py:480
  4.1 7.8 %all-to-all-start = ((f32[8,56,8,128]{3,2,1,0:T(8,128)}), f32[8,56,8,128]{3,2,1,0:T(8,128)S(1)}, u32[]{:S(2)}, u32[]{:S(2)}) async-start(f32[8,56,8,128]{3,2,1,0:T(8,128)} %shard_map.91), calls=%async_computation | async-start | bytes 3670016 | tf_op jit(solution)/shard_map/all_to_all | solution.py:493
  11.9 0.2 copy.14
  12.1 0.1 pad_add_fusion.place_ref
  12.2 0.1 iota_compare_fusion.2
  12.4 26.9 %all-to-all-done.in_ref = f32[8,56,8,128]{3,2,1,0:T(8,128)S(1)} async-done(((f32[8,56,8,128]{3,2,1,0:T(8,128)}), f32[8,56,8,128]{3,2,1,0:T(8,128)S(1)}, u32[]{:S(2)}, u32[]{:S(2)}) %all-to-all-start) | async-done | bytes 1835040 | tf_op jit(solution)/shard_map/all_to_all | solution.py:493
  39.3 1.5 %shard_map.92 = (f32[22,176,256]{2,1,0:T(8,128)S(1)}, f32[2,8,8,128]{3,2,1,0:T(8,128)S(1)}, f32[17,2,8,128]{3,2,1,0:T(8,128)S(1)}, bf16[400,256]{1,0:T(8,128)(2,...) custom-call(s32[2]{0:T(128)S(1)} %copy-done.1, ...), custom_call_target="tpu_custom_call" | custom-call | tf_op jit(solution)/shard_map/pallas_call | solution.py:480
  40.8 1.9 %collective-permute-start = (bf16[400,256]{1,0:T(8,128)(2,1)S(1)}, bf16[400,256]{1,0:T(8,128)(2,1)S(1)}, u32[]{:S(2)}, u32[]{:S(2)}) collective-permute-start(bf16[400,256]{1,0:T(8,128)(2,1)S(1)} %get-tuple-element.20), channel_id=1, source_target_pairs={{0,1},{1,2},{2,3},{3,4},{4,5},{5,6},{6,7},{7,8},{8,9},{9,10},{10,1... | collective-permute-start | bytes 614408 | tf_op jit(solution)/shard_map/ppermute | solution.py:504
  42.7 4.5 %collective-permute-start.1 = (bf16[400,256]{1,0:T(8,128)(2,1)S(1)}, bf16[400,256]{1,0:T(8,128)(2,1)S(1)}, u32[]{:S(2)}, u32[]{:S(2)}) collective-permute-start(bf16[400,256]{1,0:T(8,128)(2,1)S(1)} %get-tuple-element.21), channel_id=1, source_target_pairs={{1,0},{2,1},{3,2},{4,3},{5,4},{6,5},{7,6},{8,7},{9,8},{10,9},{11,1... | collective-permute-start | bytes 614408 | tf_op jit(solution)/shard_map/ppermute | solution.py:505
  47.3 1.5 %collective-permute-start.2 = (bf16[400,256]{1,0:T(8,128)(2,1)S(1)}, bf16[400,256]{1,0:T(8,128)(2,1)S(1)}, u32[]{:S(2)}, u32[]{:S(2)}) collective-permute-start(bf16[400,256]{1,0:T(8,128)(2,1)S(1)} %get-tuple-element.22), channel_id=1, source_target_pairs={{0,32},{32,64},{64,96},{96,112},{112,80},{80,48},{48,16},{1,33},{3... | collective-permute-start | bytes 614408 | tf_op jit(solution)/shard_map/ppermute | solution.py:506
  48.8 1.3 %collective-permute-start.3 = (bf16[416,256]{1,0:T(8,128)(2,1)S(1)}, bf16[416,256]{1,0:T(8,128)(2,1)S(1)}, u32[]{:S(2)}, u32[]{:S(2)}) collective-permute-start(bf16[416,256]{1,0:T(8,128)(2,1)S(1)} %get-tuple-element.23), channel_id=1, source_target_pairs={{32,0},{64,32},{96,64},{112,96},{80,112},{48,80},{16,48},{33,1},{6... | collective-permute-start | bytes 638984 | tf_op jit(solution)/shard_map/ppermute | solution.py:507
  50.1 0.2 subtract_convert_fusion.net_ref
  50.3 5.1 %shard_map.93.partial_ref = f32[16,16,8,256]{3,2,1,0:T(8,128)S(1)} custom-call(f32[17,2,8,128]{3,2,1,0:T(8,128)S(1)} %get-tuple-element.25.weight_ref, f32[22,176,256]{2,1,0:T(8,128)S(1)} %get-tuple-element.24.state.in_ref), custom_call_target="tpu_custom_call" | custom-call | flops 60000000 | bytes 8000000 | tf_op jit(solution)/shard_map/pallas_call | solution.py:480
  55.4 1.1 collective-permute-done.3.col_hi
  56.5 4.6 %shard_map.94 = (f32[22,176,256]{2,1,0:T(8,128)S(1)}, f32[16,16,8,256]{3,2,1,0:T(8,128)S(1)}, f32[17,2,8,128]{3,2,1,0:T(8,128)S(1)}, bf16[384,256]{1,0:T(8,128)(...) custom-call(s32[2]{0:T(128)S(1)} %pad_add_fusion.place_ref, ...), custom_call_target="tpu_custom_call", output_to_operand_aliasing={{0}: (9, {}), {1}: (10, {})} | custom-call | tf_op jit(solution)/shard_map/pallas_call | solution.py:480
  61.1 1.9 %collective-permute-start.4 = (bf16[384,256]{1,0:T(8,128)(2,1)S(1)}, bf16[384,256]{1,0:T(8,128)(2,1)S(1)}, u32[]{:S(2)}, u32[]{:S(2)}) collective-permute-start(bf16[384,256]{1,0:T(8,128)(2,1)S(1)} %get-tuple-element.27), channel_id=1, source_target_pairs={{0,1},{1,2},{2,3},{3,4},{4,5},{5,6},{6,7},{7,8},{8,9},{9,10},{10,1... | collective-permute-start | bytes 589832 | tf_op jit(solution)/shard_map/ppermute | solution.py:504
  63.0 4.5 %collective-permute-start.5 = (bf16[384,256]{1,0:T(8,128)(2,1)S(1)}, bf16[384,256]{1,0:T(8,128)(2,1)S(1)}, u32[]{:S(2)}, u32[]{:S(2)}) collective-permute-start(bf16[384,256]{1,0:T(8,128)(2,1)S(1)} %get-tuple-element.28), channel_id=1, source_target_pairs={{1,0},{2,1},{3,2},{4,3},{5,4},{6,5},{7,6},{8,7},{9,8},{10,9},{11,1... | collective-permute-start | bytes 589832 | tf_op jit(solution)/shard_map/ppermute | solution.py:505
  67.6 3.5 %collective-permute-start.6 = (bf16[384,256]{1,0:T(8,128)(2,1)S(1)}, bf16[384,256]{1,0:T(8,128)(2,1)S(1)}, u32[]{:S(2)}, u32[]{:S(2)}) collective-permute-start(bf16[384,256]{1,0:T(8,128)(2,1)S(1)} %get-tuple-element.29), channel_id=1, source_target_pairs={{0,32},{32,64},{64,96},{96,112},{112,80},{80,48},{48,16},{1,33},{3... | collective-permute-start | bytes 589832 | tf_op jit(solution)/shard_map/ppermute | solution.py:506
  71.1 1.5 %collective-permute-start.7 = (bf16[384,256]{1,0:T(8,128)(2,1)S(1)}, bf16[384,256]{1,0:T(8,128)(2,1)S(1)}, u32[]{:S(2)}, u32[]{:S(2)}) collective-permute-start(bf16[384,256]{1,0:T(8,128)(2,1)S(1)} %get-tuple-element.30), channel_id=1, source_target_pairs={{32,0},{64,32},{96,64},{112,96},{80,112},{48,80},{16,48},{33,1},{6... | collective-permute-start | bytes 589832 | tf_op jit(solution)/shard_map/ppermute | solution.py:507
  72.6 5.1 %shard_map.95.partial_ref = f32[16,16,8,256]{3,2,1,0:T(8,128)S(1)} custom-call(f32[17,2,8,128]{3,2,1,0:T(8,128)S(1)} %get-tuple-element.26.weight_ref, f32[22,176,256]{2,1,0:T(8,128)S(1)} %get-tuple-element.31.state.in_ref), custom_call_target="tpu_custom_call" | custom-call | flops 60000000 | bytes 8000000 | tf_op jit(solution)/shard_map/pallas_call | solution.py:480
  77.7 1.0 collective-permute-done.7.col_hi
  78.7 3.9 %shard_map.96 = (f32[22,176,256]{2,1,0:T(8,128)S(1)}, f32[16,16,8,256]{3,2,1,0:T(8,128)S(1)}, f32[8,48,8,128]{3,2,1,0:T(8,128)S(1)}) custom-call(f32[17,2,8,128]{3,2,1,0:T(8,128)S(1)} %get-tuple-element.26.weight_ref, bf16[384,256]{1,0:T(8,128)(2,1)S(1)} %collective-permute-done.4.row_lo, ...), custom_call_target="tpu_custom_call", output_to_operand_aliasing={{0}: (8, {}), {1}: (9, {})} | custom-call | tf_op jit(solution)/shard_map/pallas_call | solution.py:480
  82.5 28.2 %all_to_all.10.in_ref = f32[8,48,8,128]{3,2,1,0:T(8,128)S(1)} all-to-all(f32[8,48,8,128]{3,2,1,0:T(8,128)S(1)} %get-tuple-element.32), channel_id=1, replica_groups=mesh['tracer'=8,'tile'=16] {'tracer'}, dimensions={0} | all-to-all | bytes 3145728 | tf_op jit(solution)/shard_map/all_to_all | solution.py:493
  110.7 2.7 %shard_map.97 = f32[3072,128]{1,0:T(8,128)} custom-call(f32[8,48,8,128]{3,2,1,0:T(8,128)S(1)} %all_to_all.10.in_ref), custom_call_target="tpu_custom_call" | custom-call | tf_op jit(solution)/shard_map/pallas_call | solution.py:480
  (17 shorter events, 0.1 us)
Async XLA Ops:
  4.1 7.8 %copy-start.2 = (s32[512,192]{0,1:T(8,128)S(1)}, s32[512,192]{0,1:T(8,128)}, u32[]{:S(2)}) copy-start(s32[512,192]{0,1:T(8,128)} %param.15) | copy-start | bytes 1179652
  4.1 8.1 %copy-start.3 = (s32[512,2]{0,1:T(2,128)S(1)}, s32[512,2]{0,1:T(2,128)}, u32[]{:S(2)}) copy-start(s32[512,2]{0,1:T(2,128)} %param.14) | copy-start | bytes 12292
  4.1 35.2 %copy-start.1 = (s32[2]{0:T(128)S(1)}, s32[2]{0:T(128)}, u32[]{:S(2)}) copy-start(s32[2]{0:T(128)} %rec_ref.1) | copy-start | bytes 28
  4.1 35.2 %all-to-all-start = ((f32[8,56,8,128]{3,2,1,0:T(8,128)}), f32[8,56,8,128]{3,2,1,0:T(8,128)S(1)}, u32[]{:S(2)}, u32[]{:S(2)}) async-start(f32[8,56,8,128]{3,2,1,0:T(8,128)} %shard_map.91), calls=%async_computation | async-start | bytes 3670016 | tf_op jit(solution)/shard_map/all_to_all | solution.py:493
  40.8 14.6 %collective-permute-start = (bf16[400,256]{1,0:T(8,128)(2,1)S(1)}, bf16[400,256]{1,0:T(8,128)(2,1)S(1)}, u32[]{:S(2)}, u32[]{:S(2)}) collective-permute-start(bf16[400,256]{1,0:T(8,128)(2,1)S(1)} %get-tuple-element.20), channel_id=1, source_target_pairs={{0,1},{1,2},{2,3},{3,4},{4,5},{5,6},{6,7},{7,8},{8,9},{9,10},{10,1... | collective-permute-start | bytes 614408 | tf_op jit(solution)/shard_map/ppermute | solution.py:504
  42.7 12.7 %collective-permute-start.1 = (bf16[400,256]{1,0:T(8,128)(2,1)S(1)}, bf16[400,256]{1,0:T(8,128)(2,1)S(1)}, u32[]{:S(2)}, u32[]{:S(2)}) collective-permute-start(bf16[400,256]{1,0:T(8,128)(2,1)S(1)} %get-tuple-element.21), channel_id=1, source_target_pairs={{1,0},{2,1},{3,2},{4,3},{5,4},{6,5},{7,6},{8,7},{9,8},{10,9},{11,1... | collective-permute-start | bytes 614408 | tf_op jit(solution)/shard_map/ppermute | solution.py:505
  47.3 8.2 %collective-permute-start.2 = (bf16[400,256]{1,0:T(8,128)(2,1)S(1)}, bf16[400,256]{1,0:T(8,128)(2,1)S(1)}, u32[]{:S(2)}, u32[]{:S(2)}) collective-permute-start(bf16[400,256]{1,0:T(8,128)(2,1)S(1)} %get-tuple-element.22), channel_id=1, source_target_pairs={{0,32},{32,64},{64,96},{96,112},{112,80},{80,48},{48,16},{1,33},{3... | collective-permute-start | bytes 614408 | tf_op jit(solution)/shard_map/ppermute | solution.py:506
  48.8 7.7 %collective-permute-start.3 = (bf16[416,256]{1,0:T(8,128)(2,1)S(1)}, bf16[416,256]{1,0:T(8,128)(2,1)S(1)}, u32[]{:S(2)}, u32[]{:S(2)}) collective-permute-start(bf16[416,256]{1,0:T(8,128)(2,1)S(1)} %get-tuple-element.23), channel_id=1, source_target_pairs={{32,0},{64,32},{96,64},{112,96},{80,112},{48,80},{16,48},{33,1},{6... | collective-permute-start | bytes 638984 | tf_op jit(solution)/shard_map/ppermute | solution.py:507
  50.3 6.2 %copy-start = (f32[512]{0:T(512)S(1)}, f32[512]{0:T(512)}, u32[]{:S(2)}) copy-start(f32[512]{0:T(512)} %param.16) | copy-start | bytes 6148
  61.1 16.6 %collective-permute-start.4 = (bf16[384,256]{1,0:T(8,128)(2,1)S(1)}, bf16[384,256]{1,0:T(8,128)(2,1)S(1)}, u32[]{:S(2)}, u32[]{:S(2)}) collective-permute-start(bf16[384,256]{1,0:T(8,128)(2,1)S(1)} %get-tuple-element.27), channel_id=1, source_target_pairs={{0,1},{1,2},{2,3},{3,4},{4,5},{5,6},{6,7},{7,8},{8,9},{9,10},{10,1... | collective-permute-start | bytes 589832 | tf_op jit(solution)/shard_map/ppermute | solution.py:504
  63.0 14.7 %collective-permute-start.5 = (bf16[384,256]{1,0:T(8,128)(2,1)S(1)}, bf16[384,256]{1,0:T(8,128)(2,1)S(1)}, u32[]{:S(2)}, u32[]{:S(2)}) collective-permute-start(bf16[384,256]{1,0:T(8,128)(2,1)S(1)} %get-tuple-element.28), channel_id=1, source_target_pairs={{1,0},{2,1},{3,2},{4,3},{5,4},{6,5},{7,6},{8,7},{9,8},{10,9},{11,1... | collective-permute-start | bytes 589832 | tf_op jit(solution)/shard_map/ppermute | solution.py:505
  67.6 10.1 %collective-permute-start.6 = (bf16[384,256]{1,0:T(8,128)(2,1)S(1)}, bf16[384,256]{1,0:T(8,128)(2,1)S(1)}, u32[]{:S(2)}, u32[]{:S(2)}) collective-permute-start(bf16[384,256]{1,0:T(8,128)(2,1)S(1)} %get-tuple-element.29), channel_id=1, source_target_pairs={{0,32},{32,64},{64,96},{96,112},{112,80},{80,48},{48,16},{1,33},{3... | collective-permute-start | bytes 589832 | tf_op jit(solution)/shard_map/ppermute | solution.py:506
  71.1 7.6 %collective-permute-start.7 = (bf16[384,256]{1,0:T(8,128)(2,1)S(1)}, bf16[384,256]{1,0:T(8,128)(2,1)S(1)}, u32[]{:S(2)}, u32[]{:S(2)}) collective-permute-start(bf16[384,256]{1,0:T(8,128)(2,1)S(1)} %get-tuple-element.30), channel_id=1, source_target_pairs={{32,0},{64,32},{96,64},{112,96},{80,112},{48,80},{16,48},{33,1},{6... | collective-permute-start | bytes 589832 | tf_op jit(solution)/shard_map/ppermute | solution.py:507

commit v10 on v9

--- a/solution.py
+++ b/solution.py
@@ -356,8 +356,8 @@
             x_edges[3 + k, c] = edges[k]
         weights = [pick(third, XA + i, c) for i in range(3)]
         x_flux[c] = face_flux(weights, edges[1], edges[0], edges[2], q[2], q[3])
-    lax.fori_loop(3, 13, functools.partial(row, True), 0, unroll=2)
-    lax.fori_loop(0, 6, lambda k, carry: row(False, jnp.where(k < 3, k, k + 10), carry), 0, unroll=2)
+    lax.fori_loop(3, 13, functools.partial(row, True), 0, unroll=5)
+    lax.fori_loop(0, 6, lambda k, carry: row(False, jnp.where(k < 3, k, k + 10), carry), 0, unroll=3)
 
 
 def four_faces(q, weights):

time: 114 us -> 114 us (level)
  no operation moved by 1% of the time
where the time goes in v10:
time: 114 us; the launch traced here: 113 us
  waiting for transfers between devices  29 us (25%)
  starting transfers between devices  28.4 us (25%)
  blocking collectives  28.2 us (25%)
  Pallas kernels  26.8 us (24%)
    all_to_all x1, blocking collectives, swap(): return lax.all_to_all(x, 'tracer', split_axis=0, concat_axis=0, tiled=True)  28.2 us
    all_to_all x1, waiting for transfers between devices, swap(): return lax.all_to_all(x, 'tracer', split_axis=0, concat_axis=0, tiled=True)  26.9 us
    pallas_call x7, Pallas kernels, call(): pl.pallas_call(kernel, out_shape=outs, in_specs=specs, out_specs=out_spec...  26.8 us
    ppermute x2, starting transfers between devices, halo(): lax.ppermute(row_down, 'tile', back(tiles))  9.08 us
    all_to_all x1, starting transfers between devices, swap(): return lax.all_to_all(x, 'tracer', split_axis=0, concat_axis=0, tiled=True)  7.76 us
    ppermute x2, starting transfers between devices, halo(): lax.ppermute(col_right, 'tracer', columns)  4.97 us
    ppermute x2, starting transfers between devices, halo(): lax.ppermute(row_up, 'tile', tiles)  3.84 us
    ppermute x2, starting transfers between devices, halo(): lax.ppermute(col_left, 'tracer', back(columns))  2.76 us
  transfers between devices with their start and end apart: 9, of which 3 were waited for; matrix products, arithmetic and copies ran while one was open for 1% of the time, Pallas kernels for 9%

profile of v10, /device:TPU:16, one launch (start us, length us, event | category | flops | bytes accessed | tf_op | source)
XLA Modules:
  0.0 113.5 jit_solution(8313349339877150664)
XLA Ops:
  0.0 4.1 %shard_map.91 = f32[8,56,8,128]{3,2,1,0:T(8,128)} custom-call(f32[3072,128]{1,0:T(8,128)} %bitcast.16, f32[128,128]{1,0:T(8,128)} %bitcast.17, f32[128,128]{1,0:T(8,128)} %bitcast.18, f32[128,128]{1,0:T(8,128)} %bitcast.19, f32[128,128]{1,0:T(8,128)} %bitcast.20), custom_call_target="tpu_custom_call" | custom-call | tf_op jit(solution)/shard_map/pallas_call | solution.py:480
  4.1 7.8 %all-to-all-start = ((f32[8,56,8,128]{3,2,1,0:T(8,128)}), f32[8,56,8,128]{3,2,1,0:T(8,128)S(1)}, u32[]{:S(2)}, u32[]{:S(2)}) async-start(f32[8,56,8,128]{3,2,1,0:T(8,128)} %shard_map.91), calls=%async_computation | async-start | bytes 3670016 | tf_op jit(solution)/shard_map/all_to_all | solution.py:493
  11.9 0.2 copy.14
  12.1 0.1 pad_add_fusion.place_ref
  12.2 0.1 iota_compare_fusion.2
  12.4 26.9 %all-to-all-done.in_ref = f32[8,56,8,128]{3,2,1,0:T(8,128)S(1)} async-done(((f32[8,56,8,128]{3,2,1,0:T(8,128)}), f32[8,56,8,128]{3,2,1,0:T(8,128)S(1)}, u32[]{:S(2)}, u32[]{:S(2)}) %all-to-all-start) | async-done | bytes 1835040 | tf_op jit(solution)/shard_map/all_to_all | solution.py:493
  39.3 1.5 %shard_map.92 = (f32[22,176,256]{2,1,0:T(8,128)S(1)}, f32[2,8,8,128]{3,2,1,0:T(8,128)S(1)}, f32[17,2,8,128]{3,2,1,0:T(8,128)S(1)}, bf16[400,256]{1,0:T(8,128)(2,...) custom-call(s32[2]{0:T(128)S(1)} %copy-done.1, ...), custom_call_target="tpu_custom_call" | custom-call | tf_op jit(solution)/shard_map/pallas_call | solution.py:480
  40.8 1.9 %collective-permute-start = (bf16[400,256]{1,0:T(8,128)(2,1)S(1)}, bf16[400,256]{1,0:T(8,128)(2,1)S(1)}, u32[]{:S(2)}, u32[]{:S(2)}) collective-permute-start(bf16[400,256]{1,0:T(8,128)(2,1)S(1)} %get-tuple-element.20), channel_id=1, source_target_pairs={{0,1},{1,2},{2,3},{3,4},{4,5},{5,6},{6,7},{7,8},{8,9},{9,10},{10,1... | collective-permute-start | bytes 614408 | tf_op jit(solution)/shard_map/ppermute | solution.py:504
  42.7 4.5 %collective-permute-start.1 = (bf16[400,256]{1,0:T(8,128)(2,1)S(1)}, bf16[400,256]{1,0:T(8,128)(2,1)S(1)}, u32[]{:S(2)}, u32[]{:S(2)}) collective-permute-start(bf16[400,256]{1,0:T(8,128)(2,1)S(1)} %get-tuple-element.21), channel_id=1, source_target_pairs={{1,0},{2,1},{3,2},{4,3},{5,4},{6,5},{7,6},{8,7},{9,8},{10,9},{11,1... | collective-permute-start | bytes 614408 | tf_op jit(solution)/shard_map/ppermute | solution.py:505
  47.3 1.5 %collective-permute-start.2 = (bf16[400,256]{1,0:T(8,128)(2,1)S(1)}, bf16[400,256]{1,0:T(8,128)(2,1)S(1)}, u32[]{:S(2)}, u32[]{:S(2)}) collective-permute-start(bf16[400,256]{1,0:T(8,128)(2,1)S(1)} %get-tuple-element.22), channel_id=1, source_target_pairs={{0,32},{32,64},{64,96},{96,112},{112,80},{80,48},{48,16},{1,33},{3... | collective-permute-start | bytes 614408 | tf_op jit(solution)/shard_map/ppermute | solution.py:506
  48.8 1.3 %collective-permute-start.3 = (bf16[416,256]{1,0:T(8,128)(2,1)S(1)}, bf16[416,256]{1,0:T(8,128)(2,1)S(1)}, u32[]{:S(2)}, u32[]{:S(2)}) collective-permute-start(bf16[416,256]{1,0:T(8,128)(2,1)S(1)} %get-tuple-element.23), channel_id=1, source_target_pairs={{32,0},{64,32},{96,64},{112,96},{80,112},{48,80},{16,48},{33,1},{6... | collective-permute-start | bytes 638984 | tf_op jit(solution)/shard_map/ppermute | solution.py:507
  50.1 0.2 subtract_convert_fusion.net_ref
  50.3 5.1 %shard_map.93.partial_ref = f32[16,16,8,256]{3,2,1,0:T(8,128)S(1)} custom-call(f32[17,2,8,128]{3,2,1,0:T(8,128)S(1)} %get-tuple-element.25.weight_ref, f32[22,176,256]{2,1,0:T(8,128)S(1)} %get-tuple-element.24.state.in_ref), custom_call_target="tpu_custom_call" | custom-call | flops 60000000 | bytes 8000000 | tf_op jit(solution)/shard_map/pallas_call | solution.py:480
  55.4 1.1 collective-permute-done.3.col_hi
  56.5 4.6 %shard_map.94 = (f32[22,176,256]{2,1,0:T(8,128)S(1)}, f32[16,16,8,256]{3,2,1,0:T(8,128)S(1)}, f32[17,2,8,128]{3,2,1,0:T(8,128)S(1)}, bf16[384,256]{1,0:T(8,128)(...) custom-call(s32[2]{0:T(128)S(1)} %pad_add_fusion.place_ref, ...), custom_call_target="tpu_custom_call", output_to_operand_aliasing={{0}: (9, {}), {1}: (10, {})} | custom-call | tf_op jit(solution)/shard_map/pallas_call | solution.py:480
  61.1 1.9 %collective-permute-start.4 = (bf16[384,256]{1,0:T(8,128)(2,1)S(1)}, bf16[384,256]{1,0:T(8,128)(2,1)S(1)}, u32[]{:S(2)}, u32[]{:S(2)}) collective-permute-start(bf16[384,256]{1,0:T(8,128)(2,1)S(1)} %get-tuple-element.27), channel_id=1, source_target_pairs={{0,1},{1,2},{2,3},{3,4},{4,5},{5,6},{6,7},{7,8},{8,9},{9,10},{10,1... | collective-permute-start | bytes 589832 | tf_op jit(solution)/shard_map/ppermute | solution.py:504
  63.0 4.5 %collective-permute-start.5 = (bf16[384,256]{1,0:T(8,128)(2,1)S(1)}, bf16[384,256]{1,0:T(8,128)(2,1)S(1)}, u32[]{:S(2)}, u32[]{:S(2)}) collective-permute-start(bf16[384,256]{1,0:T(8,128)(2,1)S(1)} %get-tuple-element.28), channel_id=1, source_target_pairs={{1,0},{2,1},{3,2},{4,3},{5,4},{6,5},{7,6},{8,7},{9,8},{10,9},{11,1... | collective-permute-start | bytes 589832 | tf_op jit(solution)/shard_map/ppermute | solution.py:505
  67.6 3.5 %collective-permute-start.6 = (bf16[384,256]{1,0:T(8,128)(2,1)S(1)}, bf16[384,256]{1,0:T(8,128)(2,1)S(1)}, u32[]{:S(2)}, u32[]{:S(2)}) collective-permute-start(bf16[384,256]{1,0:T(8,128)(2,1)S(1)} %get-tuple-element.29), channel_id=1, source_target_pairs={{0,32},{32,64},{64,96},{96,112},{112,80},{80,48},{48,16},{1,33},{3... | collective-permute-start | bytes 589832 | tf_op jit(solution)/shard_map/ppermute | solution.py:506
  71.1 1.5 %collective-permute-start.7 = (bf16[384,256]{1,0:T(8,128)(2,1)S(1)}, bf16[384,256]{1,0:T(8,128)(2,1)S(1)}, u32[]{:S(2)}, u32[]{:S(2)}) collective-permute-start(bf16[384,256]{1,0:T(8,128)(2,1)S(1)} %get-tuple-element.30), channel_id=1, source_target_pairs={{32,0},{64,32},{96,64},{112,96},{80,112},{48,80},{16,48},{33,1},{6... | collective-permute-start | bytes 589832 | tf_op jit(solution)/shard_map/ppermute | solution.py:507
  72.5 5.1 %shard_map.95.partial_ref = f32[16,16,8,256]{3,2,1,0:T(8,128)S(1)} custom-call(f32[17,2,8,128]{3,2,1,0:T(8,128)S(1)} %get-tuple-element.26.weight_ref, f32[22,176,256]{2,1,0:T(8,128)S(1)} %get-tuple-element.31.state.in_ref), custom_call_target="tpu_custom_call" | custom-call | flops 60000000 | bytes 8000000 | tf_op jit(solution)/shard_map/pallas_call | solution.py:480
  77.6 1.0 collective-permute-done.7.col_hi
  78.6 3.9 %shard_map.96 = (f32[22,176,256]{2,1,0:T(8,128)S(1)}, f32[16,16,8,256]{3,2,1,0:T(8,128)S(1)}, f32[8,48,8,128]{3,2,1,0:T(8,128)S(1)}) custom-call(f32[17,2,8,128]{3,2,1,0:T(8,128)S(1)} %get-tuple-element.26.weight_ref, bf16[384,256]{1,0:T(8,128)(2,1)S(1)} %collective-permute-done.4.row_lo, ...), custom_call_target="tpu_custom_call", output_to_operand_aliasing={{0}: (8, {}), {1}: (9, {})} | custom-call | tf_op jit(solution)/shard_map/pallas_call | solution.py:480
  82.5 28.2 %all_to_all.10.in_ref = f32[8,48,8,128]{3,2,1,0:T(8,128)S(1)} all-to-all(f32[8,48,8,128]{3,2,1,0:T(8,128)S(1)} %get-tuple-element.32), channel_id=1, replica_groups=mesh['tracer'=8,'tile'=16] {'tracer'}, dimensions={0} | all-to-all | bytes 3145728 | tf_op jit(solution)/shard_map/all_to_all | solution.py:493
  110.7 2.7 %shard_map.97 = f32[3072,128]{1,0:T(8,128)} custom-call(f32[8,48,8,128]{3,2,1,0:T(8,128)S(1)} %all_to_all.10.in_ref), custom_call_target="tpu_custom_call" | custom-call | tf_op jit(solution)/shard_map/pallas_call | solution.py:480
  (17 shorter events, 0.1 us)
Async XLA Ops:
  4.1 7.8 %copy-start.2 = (s32[512,192]{0,1:T(8,128)S(1)}, s32[512,192]{0,1:T(8,128)}, u32[]{:S(2)}) copy-start(s32[512,192]{0,1:T(8,128)} %param.15) | copy-start | bytes 1179652
  4.1 8.1 %copy-start.3 = (s32[512,2]{0,1:T(2,128)S(1)}, s32[512,2]{0,1:T(2,128)}, u32[]{:S(2)}) copy-start(s32[512,2]{0,1:T(2,128)} %param.14) | copy-start | bytes 12292
  4.1 35.2 %copy-start.1 = (s32[2]{0:T(128)S(1)}, s32[2]{0:T(128)}, u32[]{:S(2)}) copy-start(s32[2]{0:T(128)} %rec_ref.1) | copy-start | bytes 28
  4.1 35.2 %all-to-all-start = ((f32[8,56,8,128]{3,2,1,0:T(8,128)}), f32[8,56,8,128]{3,2,1,0:T(8,128)S(1)}, u32[]{:S(2)}, u32[]{:S(2)}) async-start(f32[8,56,8,128]{3,2,1,0:T(8,128)} %shard_map.91), calls=%async_computation | async-start | bytes 3670016 | tf_op jit(solution)/shard_map/all_to_all | solution.py:493
  40.8 14.6 %collective-permute-start = (bf16[400,256]{1,0:T(8,128)(2,1)S(1)}, bf16[400,256]{1,0:T(8,128)(2,1)S(1)}, u32[]{:S(2)}, u32[]{:S(2)}) collective-permute-start(bf16[400,256]{1,0:T(8,128)(2,1)S(1)} %get-tuple-element.20), channel_id=1, source_target_pairs={{0,1},{1,2},{2,3},{3,4},{4,5},{5,6},{6,7},{7,8},{8,9},{9,10},{10,1... | collective-permute-start | bytes 614408 | tf_op jit(solution)/shard_map/ppermute | solution.py:504
  42.7 12.7 %collective-permute-start.1 = (bf16[400,256]{1,0:T(8,128)(2,1)S(1)}, bf16[400,256]{1,0:T(8,128)(2,1)S(1)}, u32[]{:S(2)}, u32[]{:S(2)}) collective-permute-start(bf16[400,256]{1,0:T(8,128)(2,1)S(1)} %get-tuple-element.21), channel_id=1, source_target_pairs={{1,0},{2,1},{3,2},{4,3},{5,4},{6,5},{7,6},{8,7},{9,8},{10,9},{11,1... | collective-permute-start | bytes 614408 | tf_op jit(solution)/shard_map/ppermute | solution.py:505
  47.3 8.1 %collective-permute-start.2 = (bf16[400,256]{1,0:T(8,128)(2,1)S(1)}, bf16[400,256]{1,0:T(8,128)(2,1)S(1)}, u32[]{:S(2)}, u32[]{:S(2)}) collective-permute-start(bf16[400,256]{1,0:T(8,128)(2,1)S(1)} %get-tuple-element.22), channel_id=1, source_target_pairs={{0,32},{32,64},{64,96},{96,112},{112,80},{80,48},{48,16},{1,33},{3... | collective-permute-start | bytes 614408 | tf_op jit(solution)/shard_map/ppermute | solution.py:506
  48.8 7.7 %collective-permute-start.3 = (bf16[416,256]{1,0:T(8,128)(2,1)S(1)}, bf16[416,256]{1,0:T(8,128)(2,1)S(1)}, u32[]{:S(2)}, u32[]{:S(2)}) collective-permute-start(bf16[416,256]{1,0:T(8,128)(2,1)S(1)} %get-tuple-element.23), channel_id=1, source_target_pairs={{32,0},{64,32},{96,64},{112,96},{80,112},{48,80},{16,48},{33,1},{6... | collective-permute-start | bytes 638984 | tf_op jit(solution)/shard_map/ppermute | solution.py:507
  50.3 6.2 %copy-start = (f32[512]{0:T(512)S(1)}, f32[512]{0:T(512)}, u32[]{:S(2)}) copy-start(f32[512]{0:T(512)} %param.16) | copy-start | bytes 6148
  61.1 16.5 %collective-permute-start.4 = (bf16[384,256]{1,0:T(8,128)(2,1)S(1)}, bf16[384,256]{1,0:T(8,128)(2,1)S(1)}, u32[]{:S(2)}, u32[]{:S(2)}) collective-permute-start(bf16[384,256]{1,0:T(8,128)(2,1)S(1)} %get-tuple-element.27), channel_id=1, source_target_pairs={{0,1},{1,2},{2,3},{3,4},{4,5},{5,6},{6,7},{7,8},{8,9},{9,10},{10,1... | collective-permute-start | bytes 589832 | tf_op jit(solution)/shard_map/ppermute | solution.py:504
  63.0 14.6 %collective-permute-start.5 = (bf16[384,256]{1,0:T(8,128)(2,1)S(1)}, bf16[384,256]{1,0:T(8,128)(2,1)S(1)}, u32[]{:S(2)}, u32[]{:S(2)}) collective-permute-start(bf16[384,256]{1,0:T(8,128)(2,1)S(1)} %get-tuple-element.28), channel_id=1, source_target_pairs={{1,0},{2,1},{3,2},{4,3},{5,4},{6,5},{7,6},{8,7},{9,8},{10,9},{11,1... | collective-permute-start | bytes 589832 | tf_op jit(solution)/shard_map/ppermute | solution.py:505
  67.6 10.1 %collective-permute-start.6 = (bf16[384,256]{1,0:T(8,128)(2,1)S(1)}, bf16[384,256]{1,0:T(8,128)(2,1)S(1)}, u32[]{:S(2)}, u32[]{:S(2)}) collective-permute-start(bf16[384,256]{1,0:T(8,128)(2,1)S(1)} %get-tuple-element.29), channel_id=1, source_target_pairs={{0,32},{32,64},{64,96},{96,112},{112,80},{80,48},{48,16},{1,33},{3... | collective-permute-start | bytes 589832 | tf_op jit(solution)/shard_map/ppermute | solution.py:506
  71.1 7.6 %collective-permute-start.7 = (bf16[384,256]{1,0:T(8,128)(2,1)S(1)}, bf16[384,256]{1,0:T(8,128)(2,1)S(1)}, u32[]{:S(2)}, u32[]{:S(2)}) collective-permute-start(bf16[384,256]{1,0:T(8,128)(2,1)S(1)} %get-tuple-element.30), channel_id=1, source_target_pairs={{32,0},{64,32},{96,64},{112,96},{80,112},{48,80},{16,48},{33,1},{6... | collective-permute-start | bytes 589832 | tf_op jit(solution)/shard_map/ppermute | solution.py:507
